TPU v7x, 32 devices: a whole 2x2x4 slice. The times are simulated.
32 devices in a mesh: dp: 8 (over z, y), mp: 4 (over x, core).
Axes of the slice: x: 2, y: 2, z: 4, core: 2. Of those that a mesh axis runs over, the one named last changes fastest.
Arguments:
- tokens: bfloat16 [8192, 768], P('dp'), may hold values from -6 to 6
- noise_field: bfloat16 [8192, 768], P('dp'), may hold values from -6 to 6
- codec_tokens: bfloat16 [16, 256, 768], P('dp'), may hold values from -6 to 6
- timesteps: int32 [16], P('dp'), may hold values from 0 to 999
- segments: int32 [16, 512], P('dp'), may hold values from 0 to 3, never falling along the last dimension, each value on 1 to 256 neighbouring positions
- cotangent: bfloat16 [8192, 768], P('dp'), may hold values from -6 to 6
- w_in: float32 [16, 768, 768], P(None, 'dp', 'mp'), may hold values from -0.14433757 to 0.14433757
- w_back: float32 [11, 768, 768], P(None, 'mp', 'dp'), may hold values from -0.4082483 to 0.4082483
- w_up: float32 [768, 3072], P('dp', 'mp'), may hold values from -0.21875 to 0.21875
- w_down: float32 [3072, 768], P('mp', 'dp'), may hold values from -0.109375 to 0.109375
- m_in: float32 [16, 768, 768], P(None, 'dp', 'mp'), may hold values from -256 to 256
- m_back: float32 [11, 768, 768], P(None, 'mp', 'dp'), may hold values from -256 to 256
- m_up: float32 [768, 3072], P('dp', 'mp'), may hold values from -256 to 256
- m_down: float32 [3072, 768], P('mp', 'dp'), may hold values from -256 to 256
- v_in: float32 [16, 768, 768], P(None, 'dp', 'mp'), may hold values from 2048 to 8192
- v_back: float32 [11, 768, 768], P(None, 'mp', 'dp'), may hold values from 2048 to 8192
- v_up: float32 [768, 3072], P('dp', 'mp'), may hold values from 2048 to 8192
- v_down: float32 [3072, 768], P('mp', 'dp'), may hold values from 2048 to 8192
- norm_params: float32 [10, 768], replicated, may hold values from -1.2 to 1.4
- norm_m: float32 [10, 768], replicated, may hold values from -256 to 256
- norm_v: float32 [10, 768], replicated, may hold values from 2048 to 8192
Outputs:
- out: bfloat16 [8192, 768], P('dp')
- grad_x: float32 [8192, 768], P('dp')
- new_w_in: float32 [16, 768, 768], P(None, 'dp', 'mp')
- new_w_back: float32 [11, 768, 768], P(None, 'mp', 'dp')
- new_w_up: float32 [768, 3072], P('dp', 'mp')
- new_w_down: float32 [3072, 768], P('mp', 'dp')
- new_m_in: float32 [16, 768, 768], P(None, 'dp', 'mp')
- new_m_back: float32 [11, 768, 768], P(None, 'mp', 'dp')
- new_m_up: float32 [768, 3072], P('dp', 'mp')
- new_m_down: float32 [3072, 768], P('mp', 'dp')
- new_v_in: float32 [16, 768, 768], P(None, 'dp', 'mp')
- new_v_back: float32 [11, 768, 768], P(None, 'mp', 'dp')
- new_v_up: float32 [768, 3072], P('dp', 'mp')
- new_v_down: float32 [3072, 768], P('mp', 'dp')
- new_norm_params: float32 [10, 768], replicated
- new_norm_m: float32 [10, 768], replicated
- new_norm_v: float32 [10, 768], replicated
- matrix_norms: float32 [2, 29], replicated
Inputs may be any that keep to these rules, and one draw needn't show every extreme that they name: `segments`: along a sequence segment ids never fall; patches attend only within their segment; a segment holds at most 256 patches.
All inputs are finite; a program needn't handle non-finite values.
Results may differ from a plain program's by a relative error of at most 0.015.
Values may be sent and summed in bfloat16 or wider, within the bound.
A program may use at most 256 MiB of HBM per device.

v0:
```python
from functools import partial
import math

import jax
import jax.numpy as jnp
from jax import lax
from jax.sharding import PartitionSpec as P

HD = 64
GROUPS = 32
FREQ = 8
TIME = 64
TSTEPS = 1000
STEP = 5


NORM_EPS = 1e-05
MOMENT_DECAY = 0.5
LEARN_RATE = 0.5
WEIGHT_DECAY = 0.01
ADAM_EPS = 1e-06
MASK_VALUE = -1e30
HIGHEST_PRECISION = lax.Precision.HIGHEST


def layer_norm(value_tensor, gain_row, shift_row):
    centre = value_tensor - jnp.mean(value_tensor, axis=-1, keepdims=True)
    spread = jnp.mean(centre * centre, axis=-1, keepdims=True)
    return centre * lax.rsqrt(spread + NORM_EPS) * gain_row + shift_row


def group_norm(value_tensor, gain_row, shift_row, group_width):
    seqs_here, length, channels = value_tensor.shape
    grouped = value_tensor.reshape(seqs_here, length, channels // group_width, group_width)
    centre = grouped - jnp.mean(grouped, axis=(1, 3), keepdims=True)
    spread = jnp.mean(centre * centre, axis=(1, 3), keepdims=True)
    normed = (centre * lax.rsqrt(spread + NORM_EPS)).reshape(seqs_here, length, channels)
    return normed * gain_row + shift_row


def norm_silu(value_tensor, gain_row, shift_row, group_width):
    return jax.nn.silu(group_norm(value_tensor, gain_row, shift_row, group_width))


def time_embedding(timesteps, features):
    half_width = features // 2
    freq_rates = jnp.exp(
        -math.log(10000.0) * jnp.arange(half_width, dtype=jnp.float32) / half_width
    )
    angles = timesteps.astype(jnp.float32)[:, None] * freq_rates[None, :]
    return jnp.concatenate([jnp.sin(angles), jnp.cos(angles)], axis=1)


def flatten_rows(value_tensor):
    return value_tensor.reshape(-1, value_tensor.shape[-1])


def project(values_low, weight_matrix):
    summed = jnp.dot(flatten_rows(values_low), weight_matrix, preferred_element_type=jnp.float32)
    return summed.reshape(values_low.shape[0], values_low.shape[1], weight_matrix.shape[1])


def back_project(grad_low, weight_matrix):
    summed = jnp.einsum(
        "ne,ce->nc", flatten_rows(grad_low), weight_matrix, preferred_element_type=jnp.float32
    )
    return summed.reshape(grad_low.shape[0], grad_low.shape[1], weight_matrix.shape[0])


def weight_grad(left_low, right_low):
    return jnp.einsum(
        "nc,ne->ce",
        flatten_rows(left_low),
        flatten_rows(right_low),
        preferred_element_type=jnp.float32,
    )


def padded_grid(grid_rows):
    seqs_here = grid_rows.shape[0]
    return jnp.pad(grid_rows.reshape(seqs_here, FREQ, TIME, -1), ((0, 0), (1, 1), (1, 1), (0, 0)))


def grid_window(padded, tap_index):
    row_off = tap_index // 3
    col_off = tap_index % 3
    return padded[:, row_off : row_off + FREQ, col_off : col_off + TIME, :].reshape(
        -1, padded.shape[3]
    )


def conv_grid(grid_rows, tap_weights, backward):
    seqs_here = grid_rows.shape[0]
    padded = padded_grid(grid_rows)
    out_width = tap_weights.shape[1] if backward else tap_weights.shape[2]
    summed = jnp.zeros((seqs_here * FREQ * TIME, out_width), jnp.float32)
    for tap_index in range(9):
        window = grid_window(padded, tap_index)
        if backward:
            summed = summed + jnp.einsum(
                "nc,dc->nd", window, tap_weights[8 - tap_index], preferred_element_type=jnp.float32
            )
        else:
            summed = summed + jnp.dot(
                window, tap_weights[tap_index], preferred_element_type=jnp.float32
            )
    return summed.reshape(seqs_here, FREQ * TIME, out_width)


def conv_weight_grad(grid_low, grad_low):
    padded = padded_grid(grid_low)
    grad_flat = flatten_rows(grad_low)
    tap_grads = []
    for tap_index in range(9):
        window = grid_window(padded, tap_index)
        tap_grads.append(
            jnp.einsum("nc,ne->ce", window, grad_flat, preferred_element_type=jnp.float32)
        )
    return jnp.stack(tap_grads)


def split_heads(rows_low):
    return rows_low.reshape(rows_low.shape[0], rows_low.shape[1], rows_low.shape[2] // HD, HD)


def head_scores(queries, key_rows, allowed, score_scale):
    scores = (
        jnp.einsum(
            "sqhd,skhd->shqk",
            split_heads(queries),
            split_heads(key_rows),
            preferred_element_type=jnp.float32,
        )
        * score_scale
    )
    if allowed is not None:
        scores = jnp.where(allowed[:, None], scores, MASK_VALUE)
    return scores


def attend(queries, key_rows, value_rows, allowed, score_scale):
    scores = head_scores(queries, key_rows, allowed, score_scale)
    highest = jnp.max(scores, axis=-1, keepdims=True)
    raised = jnp.exp(scores - highest)
    totals = jnp.sum(raised, axis=-1, keepdims=True)
    soft_low = (raised / totals).astype(jnp.bfloat16)
    mixed_rows = jnp.einsum(
        "shqk,skhd->sqhd", soft_low, split_heads(value_rows), preferred_element_type=jnp.float32
    )
    return (mixed_rows.reshape(queries.shape), highest + jnp.log(totals))


def attend_back(queries, key_rows, value_rows, allowed, score_scale, log_total, grad_mixed):
    scores = head_scores(queries, key_rows, allowed, score_scale)
    soft = jnp.exp(scores - log_total)
    grad_heads = split_heads(grad_mixed)
    grad_soft = jnp.einsum(
        "sqhd,skhd->shqk", grad_heads, split_heads(value_rows), preferred_element_type=jnp.float32
    )
    grad_values = jnp.einsum(
        "shqk,sqhd->skhd", soft.astype(jnp.bfloat16), grad_heads, preferred_element_type=jnp.float32
    )
    row_dot = jnp.sum(soft * grad_soft, axis=-1, keepdims=True)
    grad_scores = (soft * (grad_soft - row_dot)).astype(jnp.bfloat16)
    grad_queries = (
        jnp.einsum(
            "shqk,skhd->sqhd",
            grad_scores,
            split_heads(key_rows),
            preferred_element_type=jnp.float32,
        )
        * score_scale
    )
    grad_keys = (
        jnp.einsum(
            "shqk,sqhd->skhd", grad_scores, split_heads(queries), preferred_element_type=jnp.float32
        )
        * score_scale
    )
    return (
        grad_queries.reshape(queries.shape).astype(jnp.bfloat16),
        grad_keys.reshape(key_rows.shape).astype(jnp.bfloat16),
        grad_values.reshape(value_rows.shape).astype(jnp.bfloat16),
    )


def tensor_parallel_sum(term_rows):
    return lax.psum(term_rows, "mp")


def matrix_squares(first_stack, second_stack, up_rows, down_rows):
    return jnp.concatenate(
        [
            jnp.sum(first_stack * first_stack, axis=(1, 2)),
            jnp.sum(second_stack * second_stack, axis=(1, 2)),
            jnp.sum(up_rows * up_rows)[None],
            jnp.sum(down_rows * down_rows)[None],
        ]
    )


def adam_update(master, grad_rows, first_moment, second_moment, decay_rate):
    first_new = MOMENT_DECAY * first_moment + (1.0 - MOMENT_DECAY) * grad_rows
    second_new = MOMENT_DECAY * second_moment + (1.0 - MOMENT_DECAY) * grad_rows * grad_rows
    correct = 1.0 - MOMENT_DECAY**STEP
    update = first_new / correct / (jnp.sqrt(second_new / correct) + ADAM_EPS) + decay_rate * master
    return (first_new, second_new, update)


def per_device(
    tokens,
    noise_field,
    codec_tokens,
    timesteps,
    segments,
    cotangent,
    w_in,
    w_back,
    w_up,
    w_down,
    m_in,
    m_back,
    m_up,
    m_down,
    v_in,
    v_back,
    v_up,
    v_down,
    norm_params,
    norm_m,
    norm_v,
):
    seqs_here, length = segments.shape
    features = tokens.shape[1]
    chans_here = w_in.shape[2]
    group_width = features // GROUPS
    score_scale = HD ** (-0.5)
    channel_start = lax.axis_index("mp") * chans_here
    lead_device = (lax.axis_index("mp") == 0).astype(jnp.float32)
    weight_sq = matrix_squares(w_in, w_back, w_up, w_down)
    full_in, full_back, complete_up_weight, full_down = (
        lax.all_gather(w_in.astype(jnp.bfloat16), "dp", axis=1, tiled=True),
        lax.all_gather(w_back.astype(jnp.bfloat16), "dp", axis=2, tiled=True),
        lax.all_gather(w_up.astype(jnp.bfloat16), "dp", axis=0, tiled=True),
        lax.all_gather(w_down.astype(jnp.bfloat16), "dp", axis=1, tiled=True),
    )
    resid_in = tokens.astype(jnp.float32).reshape(seqs_here, length, features)
    allowed = segments[:, :, None] == segments[:, None, :]
    normed_one_low = layer_norm(resid_in, norm_params[0], norm_params[1]).astype(jnp.bfloat16)
    queries = project(normed_one_low, full_in[0]).astype(jnp.bfloat16)
    key_rows = project(normed_one_low, full_in[1]).astype(jnp.bfloat16)
    value_rows = project(normed_one_low, full_in[2]).astype(jnp.bfloat16)
    mixed_rows, log_self = attend(queries, key_rows, value_rows, allowed, score_scale)
    mixed_low = mixed_rows.astype(jnp.bfloat16)
    resid_one = resid_in + tensor_parallel_sum(project(mixed_low, full_back[0]))
    normed_two_low = layer_norm(resid_one, norm_params[2], norm_params[3]).astype(jnp.bfloat16)
    hidden_pre = project(normed_two_low, complete_up_weight)
    hidden_low = jax.nn.gelu(hidden_pre).astype(jnp.bfloat16)
    resid_two = resid_one + tensor_parallel_sum(project(hidden_low, full_down))
    noise_level = jnp.sqrt((timesteps.astype(jnp.float32) + 1.0) / TSTEPS)
    noisy = resid_two + noise_level[:, None, None] * noise_field.astype(jnp.float32).reshape(
        seqs_here, length, features
    )
    first_low = norm_silu(noisy, norm_params[4], norm_params[5], group_width).astype(jnp.bfloat16)
    embed_low = jax.nn.silu(time_embedding(timesteps, features)).astype(jnp.bfloat16)
    time_shift = jnp.dot(embed_low, full_in[3], preferred_element_type=jnp.float32)
    conv_one = conv_grid(first_low, full_in[7:16], False) + time_shift[:, None, :]
    gain_six = lax.dynamic_slice_in_dim(norm_params[6], channel_start, chans_here)
    shift_six = lax.dynamic_slice_in_dim(norm_params[7], channel_start, chans_here)
    second_low = norm_silu(conv_one, gain_six, shift_six, group_width).astype(jnp.bfloat16)
    resid_three = noisy + tensor_parallel_sum(conv_grid(second_low, full_back[2:11], False))
    normed_three_low = layer_norm(resid_three, norm_params[8], norm_params[9]).astype(jnp.bfloat16)
    cross_queries = project(normed_three_low, full_in[4]).astype(jnp.bfloat16)
    cross_keys = project(codec_tokens, full_in[5]).astype(jnp.bfloat16)
    cross_values = project(codec_tokens, full_in[6]).astype(jnp.bfloat16)
    cross_mixed, log_cross = attend(cross_queries, cross_keys, cross_values, None, score_scale)
    cross_low = cross_mixed.astype(jnp.bfloat16)
    result = resid_three + tensor_parallel_sum(project(cross_low, full_back[1]))
    out_low = result.astype(jnp.bfloat16)
    grad_out = cotangent.astype(jnp.float32).reshape(seqs_here, length, features)
    grad_cross_low = grad_out.astype(jnp.bfloat16)
    grad_w_co = weight_grad(cross_low, grad_cross_low)
    grad_cross_mixed = back_project(grad_cross_low, full_back[1]).astype(jnp.bfloat16)
    grad_cq, grad_ck, grad_cv = attend_back(
        cross_queries, cross_keys, cross_values, None, score_scale, log_cross, grad_cross_mixed
    )
    grad_w_cq = weight_grad(normed_three_low, grad_cq)
    grad_w_ck = weight_grad(codec_tokens, grad_ck)
    grad_w_cv = weight_grad(codec_tokens, grad_cv)
    grad_normed_three = tensor_parallel_sum(back_project(grad_cq, full_in[4]))
    pull_three = jax.vjp(layer_norm, resid_three, norm_params[8], norm_params[9])[1]
    grad_part, grad_gain_eight, grad_shift_eight = pull_three(grad_normed_three)
    grad_three = grad_out + grad_part
    grad_conv_low = grad_three.astype(jnp.bfloat16)
    grad_w_conv_two = conv_weight_grad(second_low, grad_conv_low)
    grad_second = conv_grid(grad_conv_low, full_back[2:11], True)
    gather_second_moment = jax.vjp(
        partial(norm_silu, group_width=group_width), conv_one, gain_six, shift_six
    )[1]
    grad_conv_one, grad_gain_six, grad_shift_six = gather_second_moment(grad_second)
    grad_conv_one_low = grad_conv_one.astype(jnp.bfloat16)
    grad_w_time = jnp.einsum(
        "sd,sc->dc",
        embed_low.astype(jnp.float32),
        jnp.sum(grad_conv_one_low.astype(jnp.float32), axis=1),
        precision=HIGHEST_PRECISION,
    )
    grad_w_conv_one = conv_weight_grad(first_low, grad_conv_one_low)
    grad_first = tensor_parallel_sum(conv_grid(grad_conv_one_low, full_in[7:16], True))
    gather_first_moment = jax.vjp(
        partial(norm_silu, group_width=group_width), noisy, norm_params[4], norm_params[5]
    )[1]
    grad_part, grad_gain_four, grad_shift_four = gather_first_moment(grad_first)
    grad_two = grad_three + grad_part
    grad_mlp_low = grad_two.astype(jnp.bfloat16)
    grad_w_down = weight_grad(hidden_low, grad_mlp_low)
    grad_hidden = back_project(grad_mlp_low, full_down)
    grad_pre_low = jax.vjp(jax.nn.gelu, hidden_pre)[1](grad_hidden)[0].astype(jnp.bfloat16)
    up_weight_gradient = weight_grad(normed_two_low, grad_pre_low)
    grad_normed_two = tensor_parallel_sum(back_project(grad_pre_low, complete_up_weight))
    pull_two = jax.vjp(layer_norm, resid_one, norm_params[2], norm_params[3])[1]
    grad_part, grad_gain_two, grad_shift_two = pull_two(grad_normed_two)
    grad_one = grad_two + grad_part
    grad_attn_low = grad_one.astype(jnp.bfloat16)
    grad_w_out = weight_grad(mixed_low, grad_attn_low)
    grad_mixed = back_project(grad_attn_low, full_back[0]).astype(jnp.bfloat16)
    grad_q, grad_k, grad_v = attend_back(
        queries, key_rows, value_rows, allowed, score_scale, log_self, grad_mixed
    )
    grad_w_q = weight_grad(normed_one_low, grad_q)
    grad_w_k = weight_grad(normed_one_low, grad_k)
    grad_w_v = weight_grad(normed_one_low, grad_v)
    grad_normed_one = tensor_parallel_sum(
        back_project(grad_q, full_in[0])
        + back_project(grad_k, full_in[1])
        + back_project(grad_v, full_in[2])
    )
    pull_one = jax.vjp(layer_norm, resid_in, norm_params[0], norm_params[1])[1]
    grad_part, grad_gain_zero, grad_shift_zero = pull_one(grad_normed_one)
    grad_input = grad_one + grad_part
    grad_in_stack = jnp.concatenate(
        [
            jnp.stack([grad_w_q, grad_w_k, grad_w_v, grad_w_time, grad_w_cq, grad_w_ck, grad_w_cv]),
            grad_w_conv_one,
        ]
    )
    grad_back_stack = jnp.concatenate([jnp.stack([grad_w_out, grad_w_co]), grad_w_conv_two])
    summed_in, summed_back, summed_up, summed_down = (
        lax.psum_scatter(grad_in_stack, "dp", scatter_dimension=1, tiled=True),
        lax.psum_scatter(grad_back_stack, "dp", scatter_dimension=2, tiled=True),
        lax.psum_scatter(up_weight_gradient, "dp", scatter_dimension=0, tiled=True),
        lax.psum_scatter(grad_w_down, "dp", scatter_dimension=1, tiled=True),
    )
    shared_rows = (
        jnp.stack(
            [
                grad_gain_zero,
                grad_shift_zero,
                grad_gain_two,
                grad_shift_two,
                grad_gain_four,
                grad_shift_four,
            ]
        )
        * lead_device
    )
    group_rows = lax.dynamic_update_slice(
        jnp.zeros((2, features), jnp.float32),
        jnp.stack([grad_gain_six, grad_shift_six]),
        (0, channel_start),
    )
    last_rows = jnp.stack([grad_gain_eight, grad_shift_eight]) * lead_device
    norm_grad = lax.psum(jnp.concatenate([shared_rows, group_rows, last_rows]), ("dp", "mp"))
    m_in_new, v_in_new, upd_in = adam_update(w_in, summed_in, m_in, v_in, WEIGHT_DECAY)
    m_back_new, v_back_new, upd_back = adam_update(
        w_back, summed_back, m_back, v_back, WEIGHT_DECAY
    )
    m_up_new, v_up_new, upd_up = adam_update(w_up, summed_up, m_up, v_up, WEIGHT_DECAY)
    m_down_new, v_down_new, upd_down = adam_update(
        w_down, summed_down, m_down, v_down, WEIGHT_DECAY
    )
    update_sq = matrix_squares(upd_in, upd_back, upd_up, upd_down)
    weight_total, update_total = lax.psum((weight_sq, update_sq), ("dp", "mp"))
    weight_len = jnp.sqrt(weight_total)
    update_len = jnp.sqrt(update_total)
    trust = weight_len / update_len
    new_in = w_in - LEARN_RATE * trust[0:16, None, None] * upd_in
    new_back = w_back - LEARN_RATE * trust[16:27, None, None] * upd_back
    new_up = w_up - LEARN_RATE * trust[27] * upd_up
    new_down = w_down - LEARN_RATE * trust[28] * upd_down
    norm_m_new, norm_v_new, upd_norm = adam_update(norm_params, norm_grad, norm_m, norm_v, 0.0)
    row_trust = jnp.sqrt(jnp.sum(norm_params * norm_params, axis=1)) / jnp.sqrt(
        jnp.sum(upd_norm * upd_norm, axis=1)
    )
    new_norm = norm_params - LEARN_RATE * row_trust[:, None] * upd_norm
    matrix_norms = jnp.stack([weight_len, update_len])
    out_rows = out_low.reshape(seqs_here * length, features)
    grad_rows = grad_input.reshape(seqs_here * length, features)
    return (
        out_rows,
        grad_rows,
        new_in,
        new_back,
        new_up,
        new_down,
        m_in_new,
        m_back_new,
        m_up_new,
        m_down_new,
        v_in_new,
        v_back_new,
        v_up_new,
        v_down_new,
        new_norm,
        norm_m_new,
        norm_v_new,
        matrix_norms,
    )


def solution(mesh):
    placed = (
        P("dp", None),
        P("dp", None),
        P("dp", None, None),
        P("dp"),
        P("dp", None),
        P("dp", None),
        P(None, "dp", "mp"),
        P(None, "mp", "dp"),
        P("dp", "mp"),
        P("mp", "dp"),
        P(None, "dp", "mp"),
        P(None, "mp", "dp"),
        P("dp", "mp"),
        P("mp", "dp"),
        P(None, "dp", "mp"),
        P(None, "mp", "dp"),
        P("dp", "mp"),
        P("mp", "dp"),
        P(),
        P(),
        P(),
    )
    return jax.shard_map(
        per_device,
        mesh=mesh,
        in_specs=placed,
        out_specs=(
            P("dp", None),
            P("dp", None),
            P(None, "dp", "mp"),
            P(None, "mp", "dp"),
            P("dp", "mp"),
            P("mp", "dp"),
            P(None, "dp", "mp"),
            P(None, "mp", "dp"),
            P("dp", "mp"),
            P("mp", "dp"),
            P(None, "dp", "mp"),
            P(None, "mp", "dp"),
            P("dp", "mp"),
            P("mp", "dp"),
            P(),
            P(),
            P(),
            P(),
        ),
        check_vma=False,
    )
```

profile of v0, /device:TPU:0, one launch (start us, length us, event | category | flops | bytes accessed | tf_op | source)
XLA Modules:
  0.0 1573.5 jit_solution(16508479176457147613)
XLA Ops:
  10.9 3.1 copy.334
  19.7 92.9 %all-gather.7.cloned.1.call-done = bf16[11,192,768]{1,0,2:T(8,128)(2,1)} async-done(((bf16[11,192,96]{1,0,2:T(8,128)(2,1)}), bf16[11,192,768]{1,0,2:T(8,128)(2,1)}) %all-gather.7.cloned.1.call-update) | async-done | bytes 3244048 | tf_op jit(solution)/shard_map/all_gather | solution.py:243
  112.7 18.8 %fusion.216 = (bf16[1,192,768]{1,0,2:T(2,128)(2,1)}, bf16[1,192,768]{1,0,2:T(2,128)(2,1)S(1)}, bf16[1,192,768]{1,0,2:T(2,128)(2,1)}, bf16[1,192,768]{1,0,2:T(2,1...) fusion(bf16[11,192,768]{1,0,2:T(8,128)(2,1)} %all-gather.7.clon, ...), kind=kLoop, calls=%fused_computation.447 | loop fusion | bytes 6488064 | tf_op jit(solution)/shard_map/slice | solution.py:278
  134.3 78.4 %all-gather.5.cloned.1.call-done = bf16[16,768,192]{2,0,1:T(8,128)(2,1)} async-done(((bf16[16,96,192]{2,0,1:T(8,128)(2,1)}), bf16[16,768,192]{2,0,1:T(8,128)(2,1)}) %all-gather.5.cloned.1.call-update) | async-done | bytes 4718608 | tf_op jit(solution)/shard_map/all_gather | solution.py:242
  212.7 24.1 %fusion.217 = (bf16[1,768,192]{2,0,1:T(2,128)(2,1)}, bf16[1,768,192]{2,0,1:T(2,128)(2,1)}, bf16[1,768,192]{2,0,1:T(2,128)(2,1)}, bf16[1,768,192]{2,0,1:T(2,128)(...) fusion(bf16[16,768,192]{2,0,1:T(8,128)(2,1)} %all-gather.5.clon, ...), kind=kLoop, calls=%fused_computation.448 | loop fusion | bytes 9437184 | tf_op jit(solution)/shard_map/slice | solution.py:274
  244.6 3.0 convolution_convert_fusion.4
  265.2 63.7 %all-reduce.14.cloned.1.call-done = f32[2,512,768]{2,1,0:T(8,128)} async-done(((f32[2,512,768]{2,1,0:T(8,128)}), f32[2,512,768]{2,1,0:T(8,128)}) %all-reduce.14.cloned.1.call-update) | async-done | bytes 3145744 | tf_op jit(solution)/shard_map/psum | solution.py:188
  328.9 3.9 bitcast_add_fusion.1
  337.3 35.4 %all-gather.9.cloned.1.call-done = bf16[768,768]{1,0:T(8,128)(2,1)} async-done(((bf16[96,768]{1,0:T(8,128)(2,1)}), bf16[768,768]{1,0:T(8,128)(2,1)}) %all-gather.9.cloned.1.call-update) | async-done | bytes 1179664 | tf_op jit(solution)/shard_map/all_gather | solution.py:244
  372.7 5.6 fusion.66
  378.3 36.9 %all-gather.11.cloned.1.call-done = bf16[768,768]{0,1:T(8,128)(2,1)} async-done(((bf16[768,96]{0,1:T(8,128)(2,1)}), bf16[768,768]{0,1:T(8,128)(2,1)}) %all-gather.11.cloned.1.call-update) | async-done | bytes 1179664 | tf_op jit(solution)/shard_map/all_gather | solution.py:245
  415.2 5.8 fusion.62
  424.9 2.9 copy.305
  430.7 2.9 copy.303
  439.2 2.9 copy.306
  454.5 2.9 copy.293
  457.4 2.9 copy.294
  460.3 2.9 copy.295
  478.8 9.6 all-reduce.16.cloned.1.call-done
  488.4 5.7 fusion.214
  497.1 2.9 multiply_convert_fusion.2
  500.0 5.8 pad_slice_fusion.8
  529.6 5.0 add_add_fusion.10
  534.7 2.9 copy.313
  547.5 55.9 %all-reduce.18.cloned.1.call-done = f32[2,512,768]{2,1,0:T(8,128)} async-done(((f32[2,512,768]{2,1,0:T(8,128)}), f32[2,512,768]{2,1,0:T(8,128)}) %all-reduce.18.cloned.1.call-update) | async-done | bytes 3145744 | tf_op jit(solution)/shard_map/psum | solution.py:188
  603.4 3.2 fusion.213
  617.2 68.5 %all-reduce.20.cloned.1.call-done = f32[2,512,768]{2,1,0:T(8,128)} async-done(((f32[2,512,768]{2,1,0:T(8,128)}), f32[2,512,768]{2,1,0:T(8,128)}) %all-reduce.20.cloned.1.call-update) | async-done | bytes 3145744 | tf_op jit(solution)/shard_map/psum | solution.py:188
  685.6 4.6 multiply_reduce_fusion.1
  694.0 5.5 pad_slice_fusion
  712.8 4.8 multiply_reduce_fusion.20
  734.1 4.9 add_add_fusion.8
  739.0 68.6 %all-reduce.22.cloned.1.call-done = f32[2,512,768]{2,1,0:T(8,128)} async-done(((f32[2,512,768]{2,1,0:T(8,128)}), f32[2,512,768]{2,1,0:T(8,128)}) %all-reduce.22.cloned.1.call-update) | async-done | bytes 3145744 | tf_op jit(solution)/shard_map/psum | solution.py:188
  807.6 5.8 fusion.198
  819.1 4.5 multiply_reduce_fusion.2
  829.2 5.6 add_add_fusion.7
  834.8 2.9 fusion.8
  838.9 3.1 fusion.64
  849.1 61.6 %all-reduce.24.cloned.1.call-done = f32[2,512,768]{2,1,0:T(8,128)} async-done(((f32[2,512,768]{2,1,0:T(8,128)}), f32[2,512,768]{2,1,0:T(8,128)}) %all-reduce.24.cloned.1.call-update) | async-done | bytes 3145744 | tf_op jit(solution)/shard_map/psum | solution.py:188
  910.7 4.5 multiply_reduce_fusion.3
  932.4 5.5 convolution_bitcast_fusion.1
  938.5 6.2 convolution_bitcast_fusion
  944.7 2.9 fusion.48
  947.7 2.9 fusion.47
  962.9 11.1 copy.285
  974.0 11.8 reshape.808
  1014.7 13.1 copy.283
  1027.8 13.2 reshape.806
  1044.2 3.1 copy.258
  1047.4 3.3 copy.264
  1056.0 2.9 fusion.199
  1067.7 57.6 %reduce-scatter.9.cloned.1.call-done = f32[96,768]{1,0:T(8,128)} async-done(((f32[768,768]{1,0:T(8,128)}), f32[96,768]{1,0:T(8,128)}) %reduce-scatter.9.cloned.1.call-update) | async-done | bytes 294928 | tf_op jit(solution)/shard_map/reduce_scatter | solution.py:351
  1127.9 69.6 %reduce-scatter.11.cloned.1.call-done = f32[768,96]{0,1:T(8,128)} async-done(((f32[768,768]{0,1:T(8,128)}), f32[768,96]{0,1:T(8,128)}) %reduce-scatter.11.cloned.1.call-update) | async-done | bytes 294928 | tf_op jit(solution)/shard_map/reduce_scatter | solution.py:352
  1200.3 5.6 add_add_fusion.4
  1205.9 117.7 %reduce-scatter.15.cloned.1.call-done = f32[96,2112]{1,0:T(8,128)} async-done(((f32[768,2112]{1,0:T(8,128)}), f32[96,2112]{1,0:T(8,128)}) %reduce-scatter.15.cloned.1.call-update) | async-done | bytes 811024
  1327.2 4.2 multiply_reduce_fusion.18
  1332.8 156.8 %reduce-scatter.13.cloned.1.call-done = f32[96,3072]{1,0:T(8,128)} async-done(((f32[768,3072]{1,0:T(8,128)}), f32[96,3072]{1,0:T(8,128)}) %reduce-scatter.13.cloned.1.call-update) | async-done | bytes 1179664
  1489.7 3.2 reshape.807
  1492.8 3.4 copy.284
  1496.2 5.3 multiply_reduce_fusion.15
  1504.4 39.8 %all-reduce.4 = (f32[29]{0:T(128)S(1)}, f32[29]{0:T(128)S(1)}, f32[10,768]{1,0:T(8,128)S(1)}) all-reduce(f32[29]{0:T(128)S(1)} %pad_maximum_fusion.5, f32[29]{0:T(128)S(1)} %pad_maximum_fusion.4, f32[10,768]{1,0:T(8,128)S(1)} %copy-done.148), channel_id=1, replica_groups=mesh['dp'=8,'mp'=4] {'dp','mp'}, use_global_device_ids=true, to_apply=%region_52.53 | all-reduce | flops 7738 | bytes 61904 | tf_op jit(solution)/shard_map/psum | solution.py:383
  1546.2 3.1 copy.270
  1549.4 3.1 copy.271
  1552.5 3.9 multiply_subtract_fusion
  1556.4 3.3 copy.269
  (745 shorter events, 277.6 us)
Async XLA Ops:
  7.2 539.4 %copy-start = (bf16[2,256,768]{2,1,0:T(8,128)(2,1)S(1)}, bf16[2,256,768]{2,1,0:T(8,128)(2,1)}, u32[]{:S(2)}) copy-start(bf16[2,256,768]{2,1,0:T(8,128)(2,1)} %param.23) | copy-start | bytes 2359300
  7.2 6.9 copy-start.2
  7.2 105.5 %all-gather.7.cloned.1.call-start = ((), (), s32[]{:S(2)}) async-start(), calls=%async_computation.5 | async-start | bytes 7077888 | tf_op jit(solution)/shard_map/all_gather | solution.py:243
  10.8 6.0 copy-start.207
  10.8 201.9 %all-gather.5.cloned.1.call-start = ((), (), s32[]{:S(2)}) async-start(), calls=%async_computation.4 | async-start | bytes 7077888 | tf_op jit(solution)/shard_map/all_gather | solution.py:242
  14.0 314.9 %all-reduce.14.cloned.1.call-start = ((), (), s32[]{:S(2)}) async-start(), calls=%async_computation.6 | async-start | bytes 6291456 | tf_op jit(solution)/shard_map/psum | solution.py:188
  16.8 355.9 %copy-start.174 = (f32[768]{0:T(1024)}, f32[768]{0:T(1024)S(1)}, u32[]{:S(2)}) copy-start(f32[768]{0:T(1024)S(1)} %get-tuple-element.137) | copy-start | bytes 9220
  16.8 355.9 %copy-start.218 = (f32[768]{0:T(1024)}, f32[768]{0:T(1024)S(1)}, u32[]{:S(2)}) copy-start(f32[768]{0:T(1024)S(1)} %get-tuple-element.136) | copy-start | bytes 9220
  16.8 480.3 %copy-start.152 = (f32[768]{0:T(1024)}, f32[768]{0:T(1024)S(1)}, u32[]{:S(2)}) copy-start(f32[768]{0:T(1024)S(1)} %get-tuple-element.135) | copy-start | bytes 9220
  16.8 480.3 %copy-start.184 = (f32[768]{0:T(1024)}, f32[768]{0:T(1024)S(1)}, u32[]{:S(2)}) copy-start(f32[768]{0:T(1024)S(1)} %get-tuple-element.134) | copy-start | bytes 9220
  244.6 10.6 copy-start.121
  262.1 110.6 %all-gather.9.cloned.1.call-start = ((), (), s32[]{:S(2)}) async-start(), calls=%async_computation.7 | async-start | bytes 1327104 | tf_op jit(solution)/shard_map/all_gather | solution.py:244
  263.8 151.4 %all-gather.11.cloned.1.call-start = ((), (), s32[]{:S(2)}) async-start(), calls=%async_computation.8 | async-start | bytes 1327104 | tf_op jit(solution)/shard_map/all_gather | solution.py:245
  264.6 223.8 %all-reduce.16.cloned.1.call-start = ((), (), s32[]{:S(2)}) async-start(), calls=%async_computation.9 | async-start | bytes 6291456 | tf_op jit(solution)/shard_map/psum | solution.py:188
  334.9 43.4 %copy-start.155 = (f32[2,512]{1,0:T(2,128)}, f32[2,512]{1,0:T(2,128)S(1)}, u32[]{:S(2)}) copy-start(f32[2,512]{1,0:T(2,128)S(1)} %broadcast_multiply_fusion.3) | copy-start | bytes 12292
  337.3 41.0 %copy-start.180 = (f32[2,512]{1,0:T(2,128)}, f32[2,512]{1,0:T(2,128)S(1)}, u32[]{:S(2)}) copy-start(f32[2,512]{1,0:T(2,128)S(1)} %multiply_reduce_fusion.12) | copy-start | bytes 12292
  337.3 41.0 %copy-start.176 = (f32[2,512]{1,0:T(2,128)}, f32[2,512]{1,0:T(2,128)S(1)}, u32[]{:S(2)}) copy-start(f32[2,512]{1,0:T(2,128)S(1)} %fusion.187) | copy-start | bytes 12292
  421.0 182.4 %all-reduce.18.cloned.1.call-start = ((), (), s32[]{:S(2)}) async-start(), calls=%async_computation.10 | async-start | bytes 6291456 | tf_op jit(solution)/shard_map/psum | solution.py:188
  424.8 97.3 %copy-start.197 = (f32[1,192]{1,0:T(1,128)}, f32[1,192]{1,0:T(1,128)S(1)}, u32[]{:S(2)}) copy-start(f32[1,192]{1,0:T(1,128)S(1)} %get-tuple-element.166) | copy-start | bytes 2308
  424.9 51.3 %copy-start.193 = (f32[2,384]{1,0:T(2,128)}, f32[2,384]{1,0:T(2,128)S(1)}, u32[]{:S(2)}) copy-start(f32[2,384]{1,0:T(2,128)S(1)} %get-tuple-element.240) | copy-start | bytes 9220
  424.9 51.3 %copy-start.195 = (f32[2,384]{1,0:T(2,128)}, f32[2,384]{1,0:T(2,128)S(1)}, u32[]{:S(2)}) copy-start(f32[2,384]{1,0:T(2,128)S(1)} %get-tuple-element.241) | copy-start | bytes 9220
  454.5 52.2 %copy-start.83 = (bf16[1,768,192]{1,2,0:T(8,128)(2,1)}, bf16[1,768,192]{1,2,0:T(8,128)(2,1)S(1)}, u32[]{:S(2)}) copy-start(bf16[1,768,192]{1,2,0:T(8,128)(2,1)S(1)} %copy.292) | copy-start | bytes 884740
  457.4 17.2 %copy-start.77 = (bf16[1,768,192]{2,0,1:T(2,128)(2,1)S(1)}, bf16[1,768,192]{2,0,1:T(2,128)(2,1)}, u32[]{:S(2)}) copy-start(bf16[1,768,192]{2,0,1:T(2,128)(2,1)} %get-tuple-element.189) | copy-start | bytes 884740
  477.3 42.8 %copy-start.163 = (f32[2,192]{1,0:T(2,128)}, f32[2,192]{1,0:T(2,128)S(1)}, u32[]{:S(2)}) copy-start(f32[2,192]{1,0:T(2,128)S(1)} %fusion.144) | copy-start | bytes 4612
  496.9 8.9 copy-start.215
  500.0 8.7 copy-start.16
  500.0 5.9 copy-start.111
  514.6 6.0 copy-start.44
  521.3 5.9 copy-start.67
  521.3 6.5 copy-start.59
  521.4 7.1 copy-start.57
  521.4 7.7 copy-start.55
  521.4 8.2 copy-start.53
  534.7 151.0 %all-reduce.20.cloned.1.call-start = ((), (), s32[]{:S(2)}) async-start(), calls=%async_computation.11 | async-start | bytes 6291456 | tf_op jit(solution)/shard_map/psum | solution.py:188
  547.5 63.8 %copy-start.136 = (bf16[2,256,192]{1,2,0:T(8,128)(2,1)}, bf16[2,256,192]{1,2,0:T(8,128)(2,1)S(1)}, u32[]{:S(2)}) copy-start(bf16[2,256,192]{1,2,0:T(8,128)(2,1)S(1)} %convolution_convert_fusion.7) | copy-start | bytes 589828
  606.7 83.6 %copy-start.157 = (f32[2,512]{1,0:T(2,128)}, f32[2,512]{1,0:T(2,128)S(1)}, u32[]{:S(2)}) copy-start(f32[2,512]{1,0:T(2,128)S(1)} %broadcast_multiply_fusion.2) | copy-start | bytes 12292
  607.2 83.1 %copy-start.178 = (f32[2,512]{1,0:T(2,128)}, f32[2,512]{1,0:T(2,128)S(1)}, u32[]{:S(2)}) copy-start(f32[2,512]{1,0:T(2,128)S(1)} %fusion.188) | copy-start | bytes 12292
  616.9 190.7 %all-reduce.22.cloned.1.call-start = ((), (), s32[]{:S(2)}) async-start(), calls=%async_computation.12 | async-start | bytes 6291456 | tf_op jit(solution)/shard_map/psum | solution.py:188
  694.0 6.2 copy-start.110
  707.6 9.9 copy-start.183
  738.9 171.7 %all-reduce.24.cloned.1.call-start = ((), (), s32[]{:S(2)}) async-start(), calls=%async_computation.13 | async-start | bytes 6291456 | tf_op jit(solution)/shard_map/psum | solution.py:188
  842.0 214.0 %all-reduce.26.cloned.1.call-start = ((), (), s32[]{:S(2)}) async-start(), calls=%async_computation.18 | async-start | bytes 12582912 | tf_op jit(solution)/shard_map/psum | solution.py:188
  932.4 192.9 %reduce-scatter.9.cloned.1.call-start = ((), (), s32[]{:S(2)}) async-start(), calls=%async_computation.14 | async-start | bytes 2654208 | tf_op jit(solution)/shard_map/reduce_scatter | solution.py:351
  938.0 259.6 %reduce-scatter.11.cloned.1.call-start = ((), (), s32[]{:S(2)}) async-start(), calls=%async_computation.15 | async-start | bytes 2654208 | tf_op jit(solution)/shard_map/reduce_scatter | solution.py:352
  944.7 378.9 %reduce-scatter.15.cloned.1.call-start = ((), (), s32[]{:S(2)}) async-start(), calls=%async_computation.17 | async-start | bytes 7520256
  985.9 503.8 %reduce-scatter.13.cloned.1.call-start = ((), (), s32[]{:S(2)}) async-start(), calls=%async_computation.16 | async-start | bytes 10616832
  1047.3 6.4 copy-start.211
  1047.3 6.9 copy-start.210
  1047.3 7.5 copy-start.213
  1047.3 8.1 copy-start.212
  1047.4 8.6 copy-start.3
  1047.4 8.6 copy-start.154
  1059.5 65.7 %copy-start.82 = (f32[96,768]{1,0:T(8,128)S(1)}, f32[96,768]{1,0:T(8,128)}, u32[]{:S(2)}) copy-start(f32[96,768]{1,0:T(8,128)} %param.29) | copy-start | bytes 884740
  1059.5 65.7 %copy-start.142 = (f32[96,768]{1,0:T(8,128)S(1)}, f32[96,768]{1,0:T(8,128)}, u32[]{:S(2)}) copy-start(f32[96,768]{1,0:T(8,128)} %param.33) | copy-start | bytes 884740
  1059.5 65.7 %copy-start.143 = (f32[96,768]{1,0:T(8,128)S(1)}, f32[96,768]{1,0:T(8,128)}, u32[]{:S(2)}) copy-start(f32[96,768]{1,0:T(8,128)} %param.37) | copy-start | bytes 884740
  1059.5 138.0 %copy-start.80 = (f32[768,96]{0,1:T(8,128)S(1)}, f32[768,96]{0,1:T(8,128)}, u32[]{:S(2)}) copy-start(f32[768,96]{0,1:T(8,128)} %param.30) | copy-start | bytes 884740
  1061.8 138.6 %copy-start.187 = (f32[2,512]{1,0:T(2,128)S(1)}, f32[2,512]{1,0:T(2,128)}, u32[]{:S(2)}) copy-start(f32[2,512]{1,0:T(2,128)} %copy-done.186) | copy-start | bytes 12292
  1205.9 121.3 %copy-start.43 = (f32[11,192,96]{2,1,0:T(8,128)S(1)}, f32[11,192,96]{2,1,0:T(8,128)}, u32[]{:S(2)}) copy-start(f32[11,192,96]{2,1,0:T(8,128)} %param.28) | copy-start | bytes 2433028
  1331.3 164.9 %copy-start.38 = (f32[16,96,192]{1,2,0:T(8,128)S(1)}, f32[16,96,192]{1,2,0:T(8,128)}, u32[]{:S(2)}) copy-start(f32[16,96,192]{1,2,0:T(8,128)} %copy.268) | copy-start | bytes 3538948
  1496.2 6.8 copy-start.7
  1496.2 6.8 copy-start.78
  1556.4 8.7 copy-start.69
  1560.4 6.3 copy-start.146
  1560.4 6.3 copy-start.147
  (182 other events, 512.9 us)
Sparse Core Ops, SparseCore 0:
  10.9 101.7 all-gather.6
  115.4 97.1 all-gather.4
  262.2 66.6 all-reduce.13
  331.5 41.1 all-gather.8
  375.3 39.8 all-gather.10
  421.2 67.1 all-reduce.15
  534.8 68.5 all-reduce.17
  617.1 68.5 all-reduce.19
  739.1 68.5 all-reduce.21
  842.1 68.5 all-reduce.23
  932.5 119.8 all-reduce.25
  1055.8 69.4 reduce-scatter.8
  1129.3 68.1 reduce-scatter.10
  1201.0 122.5 reduce-scatter.14
  1327.1 162.5 reduce-scatter.12
where the time goes:
time: 1580 us; the launch traced here: 1570 us
  waiting for transfers between devices  974 us (62%)
  local copies, waits for them, and re-layouts  262 us (17%)
  matrix products  148 us (9%)
  other arithmetic  130 us (8%)
  blocking collectives  39.8 us (3%)
  between operations  18.4 us (1%)
    psum x7, waiting for transfers between devices, tensor_parallel_sum(): return lax.psum(term_rows, 'mp')  328 us
    unnamed x17, waiting for transfers between devices  275 us
    unnamed x513, local copies, waits for them, and re-layouts  176 us
    all_gather x1, waiting for transfers between devices, per_device(): lax.all_gather(w_back.astype(jnp.bfloat16), 'dp', axis=2, tiled=True)  92.9 us
    all_gather x1, waiting for transfers between devices, per_device(): lax.all_gather(w_in.astype(jnp.bfloat16), 'dp', axis=1, tiled=True)  78.4 us
    reduce_scatter x1, waiting for transfers between devices, per_device(): lax.psum_scatter(grad_w_down, 'dp', scatter_dimension=1, tiled=True)  69.6 us
    reduce_scatter x1, waiting for transfers between devices, per_device(): lax.psum_scatter(up_weight_gradient, 'dp', scatter_dimension=0, tiled=True)  57.6 us
    psum x1, blocking collectives, per_device(): weight_total, update_total = lax.psum((weight_sq, update_sq), ('dp', 'mp'))  39.8 us
  transfers between devices with their start and end apart: 15, of which 14 were waited for; matrix products, arithmetic and copies ran while one was open for 17% of the time, Pallas kernels for 0%

commit v1 on v0

--- a/solution.py
+++ b/solution.py
@@ -207,7 +207,7 @@
     return (first_new, second_new, update)
 
 
-def per_device(
+def generic_device(
     tokens,
     noise_field,
     codec_tokens,
@@ -418,7 +418,421 @@
     )
 
 
+CORE_SWAP = [(i, i ^ 1) for i in range(4)]
+X_SWAP = [(i, i ^ 2) for i in range(4)]
+Y_SWAP = [(i, i ^ 1) for i in range(8)]
+Z_TURN = [[(i, (i + 2 * k) % 8) for i in range(8)] for k in range(4)]
+LOW = jnp.bfloat16
+F32 = jnp.float32
+
+
+def swap_core(v):
+    return lax.ppermute(v, "mp", CORE_SWAP)
+
+
+def swap_x(v):
+    return lax.ppermute(v, "mp", X_SWAP)
+
+
+def swap_y(v):
+    return lax.ppermute(v, "dp", Y_SWAP)
+
+
+def turn_z(v, k):
+    return lax.ppermute(v, "dp", Z_TURN[k])
+
+
+def by_parity(flag, own, other, axis):
+    first = jnp.where(flag == 0, own, other)
+    second = jnp.where(flag == 0, other, own)
+    return jnp.stack([first, second], axis=axis)
+
+
+def gather_line(piece, z):
+    rows, cols = piece.shape
+    buf = jnp.zeros((4, rows, cols), piece.dtype)
+    for k in range(4):
+        got = piece if k == 0 else turn_z(piece, k)
+        buf = lax.dynamic_update_slice(buf, got[None], ((z - k) % 4, 0, 0))
+    return buf
+
+
+def gather_zyx(piece, z, y):
+    line = gather_line(piece, z)
+    plane = by_parity(y, line, swap_y(line), 1).reshape(-1, piece.shape[1])
+    return plane, swap_x(plane)
+
+
+def gather_zxy(piece, z, y):
+    line = gather_line(piece, z)
+    line_x = swap_x(line)
+    own = by_parity(y, line, swap_y(line), 1).reshape(-1, piece.shape[1])
+    other = by_parity(y, line_x, swap_y(line_x), 1).reshape(-1, piece.shape[1])
+    return own, other
+
+
+def pick(v, index, axis):
+    return lax.dynamic_index_in_dim(v, index, axis, keepdims=False)
+
+
+def scatter_line(rows4, z):
+    sums = pick(rows4, z, 0)
+    for k in range(1, 4):
+        sent = pick(rows4, (z + k) % 4, 0).astype(LOW)
+        sums = sums + turn_z(sent, k).astype(F32)
+    return sums
+
+
+def scatter_xyz(own, other, z, y):
+    cols = own.shape[1]
+    got = swap_x(other)
+    plane = (own.astype(F32) + got.astype(F32)).reshape(4, 2, -1, cols)
+    got_y = swap_y(pick(plane, 1 - y, 1).astype(LOW))
+    return scatter_line(pick(plane, y, 1) + got_y.astype(F32), z)
+
+
+def scatter_yxz(own, other, z, y):
+    cols = own.shape[1]
+    lines = []
+    for part in (other, own):
+        part = part.reshape(4, 2, -1, cols)
+        got = swap_y(pick(part, 1 - y, 1))
+        lines.append(pick(part, y, 1).astype(F32) + got.astype(F32))
+    got_x = swap_x(lines[0].astype(LOW))
+    return scatter_line(lines[1] + got_x.astype(F32), z)
+
+
+def core_sum(partial_rows):
+    low = partial_rows.astype(LOW)
+    return low.astype(F32) + swap_core(low).astype(F32)
+
+
+def ln_stats(v):
+    centre = v - jnp.mean(v, axis=-1, keepdims=True)
+    scale = lax.rsqrt(jnp.mean(centre * centre, axis=-1, keepdims=True) + NORM_EPS)
+    return centre * scale, scale
+
+
+def ln_back(v, gain, grad):
+    hat, scale = ln_stats(v)
+    pulled = grad * gain
+    back = scale * (
+        pulled
+        - jnp.mean(pulled, axis=-1, keepdims=True)
+        - hat * jnp.mean(pulled * hat, axis=-1, keepdims=True)
+    )
+    return back, jnp.sum(grad * hat, axis=0), jnp.sum(grad, axis=0)
+
+
+def group_mean(row, width, count):
+    means = jnp.mean(row.reshape(-1, width), axis=1, keepdims=True) / count
+    return jnp.broadcast_to(means, (means.shape[0], width)).reshape(-1)
+
+
+def gn_stats(v, width):
+    rows = v.shape[0]
+    centre = v - group_mean(jnp.sum(v, axis=0), width, rows)
+    scale = lax.rsqrt(group_mean(jnp.sum(centre * centre, axis=0), width, rows) + NORM_EPS)
+    return centre * scale, scale
+
+
+def gn_silu(v, gain, shift, width):
+    hat, _ = gn_stats(v, width)
+    return jax.nn.silu(hat * gain + shift)
+
+
+def gn_silu_back(v, gain, shift, width, grad):
+    rows = v.shape[0]
+    hat, scale = gn_stats(v, width)
+    pre = hat * gain + shift
+    gate = jax.nn.sigmoid(pre)
+    grad_pre = grad * gate * (1.0 + pre * (1.0 - gate))
+    grad_gain = jnp.sum(grad_pre * hat, axis=0)
+    grad_shift = jnp.sum(grad_pre, axis=0)
+    back = scale * (
+        grad_pre * gain
+        - group_mean(grad_shift * gain, width, rows)
+        - hat * group_mean(grad_gain * gain, width, rows)
+    )
+    return back, grad_gain, grad_shift
+
+
+def tap_shift(rows, tap, back):
+    row_off, col_off = tap // 3 - 1, tap % 3 - 1
+    if back:
+        row_off, col_off = -row_off, -col_off
+    grid = jnp.pad(rows.reshape(FREQ, TIME, -1), ((1, 1), (1, 1), (0, 0)))
+    return grid[
+        1 + row_off : 1 + row_off + FREQ, 1 + col_off : 1 + col_off + TIME
+    ].reshape(rows.shape)
+
+
+def tap_columns(rows, back):
+    return jnp.concatenate([tap_shift(rows, tap, back) for tap in range(9)], axis=1)
+
+
+def tap_sum(products, back):
+    width = products.shape[1] // 9
+    return sum(
+        tap_shift(products[:, width * tap : width * (tap + 1)], tap, back) for tap in range(9)
+    )
+
+
+def mm(a, b):
+    return lax.dot_general(a, b, (((1,), (0,)), ((), ())), preferred_element_type=F32)
+
+
+def mm_nt(a, b):
+    return lax.dot_general(a, b, (((1,), (1,)), ((), ())), preferred_element_type=F32)
+
+
+def mm_tn(a, b):
+    return lax.dot_general(a, b, (((0,), (0,)), ((), ())), preferred_element_type=F32)
+
+
+def fast_device(
+    tokens,
+    noise_field,
+    codec_tokens,
+    timesteps,
+    segments,
+    cotangent,
+    w_in,
+    w_back,
+    w_up,
+    w_down,
+    m_in,
+    m_back,
+    m_up,
+    m_down,
+    v_in,
+    v_back,
+    v_up,
+    v_down,
+    norm_params,
+    norm_m,
+    norm_v,
+):
+    length = segments.shape[1]
+    features = tokens.shape[1]
+    chans = w_in.shape[2]
+    width = features // GROUPS
+    score_scale = HD ** (-0.5)
+    mp = lax.axis_index("mp")
+    dp = lax.axis_index("dp")
+    x, core, z, y = mp // 2, mp % 2, dp // 2, dp % 2
+    lead = (core == 0).astype(F32)
+    slices = [2 * x + core, 2 * (1 - x) + core]
+
+    low_in = w_in.astype(LOW).transpose(1, 0, 2).reshape(w_in.shape[1], -1)
+    low_back = w_back.astype(LOW).transpose(2, 0, 1).reshape(w_back.shape[2], -1)
+    low_up = w_up.astype(LOW)
+    low_down = w_down.astype(LOW).T
+    n = chans
+    piece_attn = jnp.concatenate([low_in[:, : 3 * n], low_back[:, :n]], axis=1)
+    piece_mlp = jnp.concatenate([low_up, low_down], axis=1)
+    piece_one = low_in[:, 7 * n :]
+    piece_two = jnp.concatenate([low_back[:, 2 * n :], low_in[:, 3 * n : 4 * n]], axis=1)
+    piece_cross = jnp.concatenate([low_in[:, 4 * n : 7 * n], low_back[:, n : 2 * n]], axis=1)
+    w_attn = gather_zyx(piece_attn, z, y)
+    w_mlp = gather_zxy(piece_mlp, z, y)
+    w_one = gather_zyx(piece_one, z, y)
+    w_two = gather_zxy(piece_two, z, y)
+    w_cross = gather_zyx(piece_cross, z, y)
+    weight_sq = matrix_squares(w_in, w_back, w_up, w_down)
+
+    def own_rows(v):
+        return lax.dynamic_slice_in_dim(v, x * length, length, 0)
+
+    tok = own_rows(tokens).astype(F32)
+    noise = own_rows(noise_field).astype(F32)
+    cot = own_rows(cotangent)
+    codec = pick(codec_tokens, x, 0)
+    step = pick(timesteps, x, 0)
+    seg = pick(segments, x, 0)
+    allowed = (seg[:, None] == seg[None, :])[None]
+    hid = w_up.shape[1]
+
+    normed_one = ln_stats(tok)[0] * norm_params[0] + norm_params[1]
+    normed_one = normed_one.astype(LOW)
+    qkv = [mm(normed_one, w[:, : 3 * n]).astype(LOW) for w in w_attn]
+
+    def join(parts, first):
+        return jnp.concatenate([p[:, first * n : (first + 1) * n] for p in parts], axis=1)[None]
+
+    queries, keys, values = join(qkv, 0), join(qkv, 1), join(qkv, 2)
+    mixed, log_self = attend(queries, keys, values, allowed, score_scale)
+    mixed = mixed.astype(LOW)[0]
+    mixed = [mixed[:, :n], mixed[:, n:]]
+    resid_one = tok + core_sum(sum(mm_nt(a, w[:, 3 * n :]) for a, w in zip(mixed, w_attn)))
+    normed_two = (ln_stats(resid_one)[0] * norm_params[2] + norm_params[3]).astype(LOW)
+    pre = [mm(normed_two, w[:, :hid]) for w in w_mlp]
+    hidden = [jax.nn.gelu(p).astype(LOW) for p in pre]
+    resid_two = resid_one + core_sum(sum(mm_nt(a, w[:, hid:]) for a, w in zip(hidden, w_mlp)))
+    noise_level = jnp.sqrt((step.astype(F32) + 1.0) / TSTEPS)
+    noisy = resid_two + noise_level * noise
+    first = gn_silu(noisy, norm_params[4], norm_params[5], width).astype(LOW)
+    embed = jax.nn.silu(time_embedding(step[None], features)).astype(LOW)
+    gains = [lax.dynamic_slice_in_dim(norm_params[6], s * n, n) for s in slices]
+    shifts = [lax.dynamic_slice_in_dim(norm_params[7], s * n, n) for s in slices]
+    conv_one = [
+        tap_sum(mm(first, w), False) + mm(embed, t[:, 9 * n :]) for w, t in zip(w_one, w_two)
+    ]
+    second = [gn_silu(v, g, b, width).astype(LOW) for v, g, b in zip(conv_one, gains, shifts)]
+    second_taps = [tap_columns(v, False) for v in second]
+    resid_three = noisy + core_sum(
+        sum(mm_nt(a, w[:, : 9 * n]) for a, w in zip(second_taps, w_two))
+    )
+    normed_three = (ln_stats(resid_three)[0] * norm_params[8] + norm_params[9]).astype(LOW)
+    cross_q = [mm(normed_three, w[:, :n]).astype(LOW) for w in w_cross]
+    cross_kv = [mm(codec, w[:, n : 3 * n]).astype(LOW) for w in w_cross]
+    cq, ck, cv = join(cross_q, 0), join(cross_kv, 0), join(cross_kv, 1)
+    cross_mixed, log_cross = attend(cq, ck, cv, None, score_scale)
+    cross_mixed = cross_mixed.astype(LOW)[0]
+    cross_mixed = [cross_mixed[:, :n], cross_mixed[:, n:]]
+    result = resid_three + core_sum(
+        sum(mm_nt(a, w[:, 3 * n :]) for a, w in zip(cross_mixed, w_cross))
+    )
+    out_low = result.astype(LOW)
+    out_rows = by_parity(x, out_low, swap_x(out_low), 0).reshape(-1, features)
+
+    grad_out = cot.astype(F32)
+    grad_co = [mm_tn(cot, a) for a in cross_mixed]
+    grad_cm = jnp.concatenate([mm(cot, w[:, 3 * n :]).astype(LOW) for w in w_cross], axis=1)
+    grad_cq, grad_ck, grad_cv = attend_back(
+        cq, ck, cv, None, score_scale, log_cross, grad_cm[None]
+    )
+
+    def parts(v):
+        return [v[0][:, :n], v[0][:, n:]]
+
+    grad_cq = parts(grad_cq)
+    grad_ckv = [
+        jnp.concatenate([a, b], axis=1) for a, b in zip(parts(grad_ck), parts(grad_cv))
+    ]
+    d_cross = [
+        jnp.concatenate([mm_tn(normed_three, q), mm_tn(codec, kv), o], axis=1).astype(LOW)
+        for q, kv, o in zip(grad_cq, grad_ckv, grad_co)
+    ]
+    sum_cross = scatter_xyz(d_cross[0], d_cross[1], z, y)
+    grad_n3 = core_sum(sum(mm_nt(g, w[:, :n]) for g, w in zip(grad_cq, w_cross)))
+    part, gain_eight, shift_eight = ln_back(resid_three, norm_params[8], grad_n3)
+    grad_three = grad_out + part
+    grad_conv = grad_three.astype(LOW)
+    d_two = [mm_tn(grad_conv, a) for a in second_taps]
+    grad_second = [tap_sum(mm(grad_conv, w[:, : 9 * n]), True) for w in w_two]
+    backs = [
+        gn_silu_back(v, g, b, width, d)
+        for v, g, b, d in zip(conv_one, gains, shifts, grad_second)
+    ]
+    grad_c1 = [b[0].astype(LOW) for b in backs]
+    d_time = [
+        embed[0].astype(F32)[:, None] * jnp.sum(g.astype(F32), axis=0)[None, :] for g in grad_c1
+    ]
+    d_two = [jnp.concatenate([a, b], axis=1).astype(LOW) for a, b in zip(d_two, d_time)]
+    sum_two = scatter_yxz(d_two[0], d_two[1], z, y)
+    c1_taps = [tap_columns(g, True) for g in grad_c1]
+    d_one = [mm_tn(first, g).astype(LOW) for g in c1_taps]
+    sum_one = scatter_xyz(d_one[0], d_one[1], z, y)
+    grad_first = core_sum(sum(mm_nt(g, w) for g, w in zip(c1_taps, w_one)))
+    part, gain_four, shift_four = gn_silu_back(
+        noisy, norm_params[4], norm_params[5], width, grad_first
+    )
+    grad_two = grad_three + part
+    grad_mlp = grad_two.astype(LOW)
+    grad_hidden = [mm(grad_mlp, w[:, hid:]) for w in w_mlp]
+    grad_pre = [
+        jax.vjp(jax.nn.gelu, p)[1](g)[0].astype(LOW) for p, g in zip(pre, grad_hidden)
+    ]
+    d_mlp = [
+        jnp.concatenate([mm_tn(normed_two, g), mm_tn(grad_mlp, a)], axis=1).astype(LOW)
+        for g, a in zip(grad_pre, hidden)
+    ]
+    sum_mlp = scatter_yxz(d_mlp[0], d_mlp[1], z, y)
+    grad_n2 = core_sum(sum(mm_nt(g, w[:, :hid]) for g, w in zip(grad_pre, w_mlp)))
+    part, gain_two, shift_two = ln_back(resid_one, norm_params[2], grad_n2)
+    grad_one = grad_two + part
+    grad_attn = grad_one.astype(LOW)
+    grad_o = [mm_tn(grad_attn, a) for a in mixed]
+    grad_mixed = jnp.concatenate([mm(grad_attn, w[:, 3 * n :]).astype(LOW) for w in w_attn], axis=1)
+    grad_q, grad_k, grad_v = attend_back(
+        queries, keys, values, allowed, score_scale, log_self, grad_mixed[None]
+    )
+    grad_qkv = [
+        jnp.concatenate(g, axis=1) for g in zip(parts(grad_q), parts(grad_k), parts(grad_v))
+    ]
+    d_attn = [
+        jnp.concatenate([mm_tn(normed_one, g), o], axis=1).astype(LOW)
+        for g, o in zip(grad_qkv, grad_o)
+    ]
+    sum_attn = scatter_xyz(d_attn[0], d_attn[1], z, y)
+    grad_n1 = core_sum(sum(mm_nt(g, w[:, : 3 * n]) for g, w in zip(grad_qkv, w_attn)))
+    part, gain_zero, shift_zero = ln_back(tok, norm_params[0], grad_n1)
+    grad_x = (grad_one + part).astype(LOW)
+    half = length // 2
+    mine = lax.dynamic_slice_in_dim(grad_x, core * half, half, 0)
+    got = swap_x(mine)
+    other_x = by_parity(core, got, swap_core(got), 0).reshape(length, features)
+    grad_rows = by_parity(x, grad_x, other_x, 0).reshape(-1, features).astype(F32)
+
+    def unpack_in(v):
+        return v.reshape(v.shape[0], -1, n).transpose(1, 0, 2)
+
+    def unpack_back(v):
+        return v.reshape(v.shape[0], -1, n).transpose(1, 2, 0)
+
+    summed_in = unpack_in(
+        jnp.concatenate(
+            [sum_attn[:, : 3 * n], sum_two[:, 9 * n :], sum_cross[:, : 3 * n], sum_one], axis=1
+        )
+    )
+    summed_back = unpack_back(
+        jnp.concatenate([sum_attn[:, 3 * n :], sum_cross[:, 3 * n :], sum_two[:, : 9 * n]], axis=1)
+    )
+    summed_up = sum_mlp[:, :hid]
+    summed_down = sum_mlp[:, hid:].T
+
+    shared = jnp.stack([gain_zero, shift_zero, gain_two, shift_two, gain_four, shift_four]) * lead
+    group_rows = jnp.zeros((2, features), F32)
+    for s, b in zip(slices, backs):
+        group_rows = lax.dynamic_update_slice(group_rows, jnp.stack([b[1], b[2]]), (0, s * n))
+    last = jnp.stack([gain_eight, shift_eight]) * lead
+    norm_grad = lax.psum(jnp.concatenate([shared, group_rows, last]), ("dp", "mp"))
+    return finish(
+        out_rows, grad_rows, weight_sq, (summed_in, summed_back, summed_up, summed_down),
+        (w_in, w_back, w_up, w_down), (m_in, m_back, m_up, m_down), (v_in, v_back, v_up, v_down),
+        norm_grad, norm_params, norm_m, norm_v,
+    )
+
+
+def finish(out_rows, grad_rows, weight_sq, grads, masters, moments, squares, norm_grad, norm_params, norm_m, norm_v):
+    stepped = [
+        adam_update(w, g, m, v, WEIGHT_DECAY)
+        for w, g, m, v in zip(masters, grads, moments, squares)
+    ]
+    new_m = [s[0] for s in stepped]
+    new_v = [s[1] for s in stepped]
+    updates = [s[2] for s in stepped]
+    update_sq = matrix_squares(*updates)
+    weight_total, update_total = lax.psum((weight_sq, update_sq), ("dp", "mp"))
+    weight_len = jnp.sqrt(weight_total)
+    update_len = jnp.sqrt(update_total)
+    trust = LEARN_RATE * (weight_len / update_len)
+    scales = (trust[0:16, None, None], trust[16:27, None, None], trust[27], trust[28])
+    new_w = [w - s * u for w, s, u in zip(masters, scales, updates)]
+    norm_m_new, norm_v_new, upd_norm = adam_update(norm_params, norm_grad, norm_m, norm_v, 0.0)
+    row_trust = jnp.sqrt(jnp.sum(norm_params * norm_params, axis=1)) / jnp.sqrt(
+        jnp.sum(upd_norm * upd_norm, axis=1)
+    )
+    new_norm = norm_params - LEARN_RATE * row_trust[:, None] * upd_norm
+    return (
+        out_rows, grad_rows, *new_w, *new_m, *new_v, new_norm, norm_m_new, norm_v_new,
+        jnp.stack([weight_len, update_len]),
+    )
+
+
 def solution(mesh):
+    per_device = fast_device if dict(mesh.shape) == {"dp": 8, "mp": 4} else generic_device
     placed = (
         P("dp", None),
         P("dp", None),

time: 1580 us -> 1000 us (0.63)
  waiting for transfers between devices: 974 us -> 257 us
  starting transfers between devices: 1.79 us -> 130 us
  matrix products: 148 us -> 109 us
  local copies, waits for them, and re-layouts: 262 us -> 301 us
  other arithmetic: 130 us -> 149 us
    psum x7 -> x0, waiting for transfers between devices: 328 us -> none  [tensor_parallel_sum(): return lax.psum(term_rows, 'mp')]
    unnamed x17 -> x0, waiting for transfers between devices: 275 us -> none
    ppermute x0 -> x65, waiting for transfers between devices: none -> 257 us  [the longest x14 105 us: swap_y(): return lax.ppermute(v, 'dp', Y_SWAP)]
    all_gather x4 -> x0, waiting for transfers between devices: 244 us -> none  [the longest x1 92.9 us: per_device(): lax.all_gather(w_back.astype(jnp.bfloat16), 'dp', axis=2, tiled=True)]
    unnamed x513 -> x543, local copies, waits for them, and re-layouts: 176 us -> 42.3 us
    ppermute x0 -> x65, starting transfers between devices: none -> 130 us  [the longest x30 98.8 us: turn_z(): return lax.ppermute(v, 'dp', Z_TURN[k])]
    reduce_scatter x2 -> x0, waiting for transfers between devices: 127 us -> none  [the longest x1 69.6 us: per_device(): lax.psum_scatter(grad_w_down, 'dp', scatter_dimension=1, tiled=True)]
    reshape x2 -> x57, local copies, waits for them, and re-layouts: 3.35 us -> 82.2 us  [the longest x48 74.6 us: tap_shift(): return grid[1 + row_off:1 + row_off + FREQ, 1 + col_off:1 + col_off + TIM...]
  transfers between devices with their start and end apart: 15 -> 65, of which waited for: 14 -> 25; matrix products, arithmetic and copies ran while one was open for 17% -> 43% of each run, Pallas kernels for 0% -> 0%
where the time goes in v1:
time: 1000 us; the launch traced here: 990 us
  local copies, waits for them, and re-layouts  301 us (30%)
  waiting for transfers between devices  257 us (26%)
  other arithmetic  149 us (15%)
  starting transfers between devices  130 us (13%)
  matrix products  109 us (11%)
  blocking collectives  37.6 us (4%)
    ppermute x14, waiting for transfers between devices, swap_y(): return lax.ppermute(v, 'dp', Y_SWAP)  105 us
    ppermute x30, starting transfers between devices, turn_z(): return lax.ppermute(v, 'dp', Z_TURN[k])  98.8 us
    ppermute x30, waiting for transfers between devices, turn_z(): return lax.ppermute(v, 'dp', Z_TURN[k])  97.6 us
    reshape x48, local copies, waits for them, and re-layouts, tap_shift(): return grid[1 + row_off:1 + row_off + FREQ, 1 + col_off:1 + col_off + TIM...  74.6 us
    slice x40, local copies, waits for them, and re-layouts, tap_sum(): products[:, width * tap:width * (tap + 1)]  73.9 us
    ppermute x12, waiting for transfers between devices, swap_x(): return lax.ppermute(v, 'mp', X_SWAP)  54.4 us
    unnamed x543, local copies, waits for them, and re-layouts  42.3 us
    dot_general x20, matrix products, mm(): lax.dot_general(a, b, (((1,), (0,)), ((), ())), preferred_element_type=F32)  39.1 us
  transfers between devices with their start and end apart: 65, of which 25 were waited for; matrix products, arithmetic and copies ran while one was open for 43% of the time, Pallas kernels for 0%

profile of v1, /device:TPU:0, one launch (start us, length us, event | category | flops | bytes accessed | tf_op | source)
XLA Modules:
  0.0 989.7 jit_solution(12190733360331916885)
XLA Ops:
  3.7 4.0 collective-permute-start.7
  48.9 2.9 collective-permute-start.25
  60.6 6.0 collective-permute-done.26
  70.1 2.9 collective-permute-done.27
  73.7 4.3 collective-permute-start.15
  83.7 4.6 collective-permute-done.13
  88.4 13.2 %collective-permute-start.19 = (bf16[96,1920]{0,1:T(8,128)(2,1)}, bf16[96,1920]{0,1:T(8,128)(2,1)}, u32[]{:S(2)}, u32[]{:S(2)}) collective-permute-start(bf16[96,1920]{0,1:T(8,128)(2,1)} %get-tuple-element.284), channel_id=1, source_target_pairs={{0,24},{4,28},{8,0},{12,4},{16,8},{20,12},{24,16},{28,20},{1,25},{... | collective-permute-start | bytes 1105928 | tf_op jit(solution)/shard_map/ppermute | solution.py:442
  102.3 13.6 %collective-permute-done.14 = bf16[96,1728]{1,0:T(8,128)(2,1)S(1)} collective-permute-done((bf16[96,1728]{1,0:T(8,128)(2,1)S(1)}, bf16[96,1728]{1,0:T(8,128)(2,1)S(1)}, u32[]{:S(2)}, u32[]{:S(2)}) %collective-permute-start.14) | collective-permute-done | bytes 331808 | tf_op jit(solution)/shard_map/ppermute | solution.py:442
  119.4 14.5 %collective-permute-done.18 = bf16[96,1920]{0,1:T(8,128)(2,1)} collective-permute-done((bf16[96,1920]{0,1:T(8,128)(2,1)}, bf16[96,1920]{0,1:T(8,128)(2,1)}, u32[]{:S(2)}, u32[]{:S(2)}) %collective-permute-start.18) | collective-permute-done | bytes 368672 | tf_op jit(solution)/shard_map/ppermute | solution.py:442
  162.9 3.4 collective-permute-done.9
  171.4 24.4 %collective-permute-done.16 = bf16[4,96,1728]{2,1,0:T(8,128)(2,1)} collective-permute-done((bf16[4,96,1728]{2,1,0:T(8,128)(2,1)}, bf16[4,96,1728]{2,1,0:T(8,128)(2,1)}, u32[]{:S(2)}, u32[]{:S(2)}) %collective-permute-start.16) | collective-permute-done | bytes 1327136 | tf_op jit(solution)/shard_map/ppermute | solution.py:438
  199.6 3.3 copy.494
  203.5 23.9 %collective-permute-done.20 = bf16[4,96,1920]{2,1,0:T(8,128)(2,1)} collective-permute-done((bf16[4,96,1920]{2,1,0:T(8,128)(2,1)}, bf16[4,96,1920]{2,1,0:T(8,128)(2,1)}, u32[]{:S(2)}, u32[]{:S(2)}) %collective-permute-start.20) | collective-permute-done | bytes 1474592 | tf_op jit(solution)/shard_map/ppermute | solution.py:438
  247.4 5.4 collective-permute-done.11
  262.9 18.6 %collective-permute-done.23 = bf16[4,96,1920]{2,1,0:T(8,128)(2,1)S(1)} collective-permute-done((bf16[4,96,1920]{2,1,0:T(8,128)(2,1)}, bf16[4,96,1920]{2,1,0:T(8,128)(2,1)S(1)}, u32[]{:S(2)}, u32[]{:S(2)}) %collective-permute-start.23) | collective-permute-done | bytes 1474592 | tf_op jit(solution)/shard_map/ppermute | solution.py:438
  289.8 4.0 fusion.244
  311.2 4.6 fusion.263
  348.4 3.5 fusion.243
  371.8 4.5 fusion.261
  409.1 4.6 add_convert_fusion.7
  449.4 3.4 fusion.9
  452.8 3.4 fusion.13
  456.1 3.1 convolution_convert_fusion.3
  459.2 3.3 convolution_convert_fusion.2
  465.2 4.5 copy.575
  469.6 4.6 copy.573
  474.2 3.6 fusion.268
  493.9 4.8 fusion.247
  520.9 3.4 fusion.267
  539.4 4.9 fusion.246
  554.2 2.8 fusion.56
  584.8 3.9 fusion.284
  591.8 5.2 convolution_convert_fusion
  597.0 3.0 convert_add_fusion.6
  600.0 3.1 copy.579
  606.8 3.7 fusion.245
  611.1 3.0 fusion.254
  629.1 6.5 collective-permute-done.50
  636.9 8.8 collective-permute-start.51
  645.9 3.9 collective-permute-start.52
  652.9 5.8 collective-permute-done.52
  661.6 3.1 fusion.6
  687.9 22.4 %collective-permute-done.60 = bf16[4,96,1536]{2,1,0:T(8,128)(2,1)} collective-permute-done((bf16[4,96,1536]{2,1,0:T(8,128)(2,1)}, bf16[4,96,1536]{2,1,0:T(8,128)(2,1)}, u32[]{:S(2)}, u32[]{:S(2)}) %collective-permute-start.60) | collective-permute-done | bytes 1179680 | tf_op jit(solution)/shard_map/ppermute | solution.py:438
  722.4 5.8 convert_add_fusion
  728.2 6.1 copy.581
  734.4 3.1 fusion.71
  737.4 33.6 %collective-permute-done.38 = bf16[768,768]{0,1:T(8,128)(2,1)S(1)} collective-permute-done((bf16[768,768]{0,1:T(8,128)(2,1)}, bf16[768,768]{0,1:T(8,128)(2,1)S(1)}, u32[]{:S(2)}, u32[]{:S(2)}) %collective-permute-start.38) | collective-permute-done | bytes 1179680 | tf_op jit(solution)/shard_map/ppermute | solution.py:434
  774.2 3.3 copy.572
  780.5 20.6 %collective-permute-done.36 = bf16[256,768]{1,0:T(8,128)(2,1)} collective-permute-done((bf16[256,768]{1,0:T(8,128)(2,1)}, bf16[256,768]{1,0:T(8,128)(2,1)}, u32[]{:S(2)}, u32[]{:S(2)}) %collective-permute-start.36) | collective-permute-done | bytes 393248 | tf_op jit(solution)/shard_map/ppermute | solution.py:434
  805.3 5.1 collective-permute-start.46
  813.4 3.6 collective-permute-start.47
  820.7 17.4 %collective-permute-start.62 = (bf16[96,1536]{1,0:T(8,128)(2,1)S(1)}, bf16[96,1536]{1,0:T(8,128)(2,1)S(1)}, u32[]{:S(2)}, u32[]{:S(2)}) collective-permute-start(bf16[96,1536]{1,0:T(8,128)(2,1)S(1)} %get-tuple-element.232), channel_id=1, source_target_pairs={{0,8},{4,12},{8,16},{12,20},{16,24},{20,28},{24,0},{28,4},{1,9},{5... | collective-permute-start | bytes 884744 | tf_op jit(solution)/shard_map/ppermute | solution.py:442
  838.1 12.5 %collective-permute-done.47 = bf16[96,1920]{1,0:T(8,128)(2,1)S(1)} collective-permute-done((bf16[96,1920]{1,0:T(8,128)(2,1)S(1)}, bf16[96,1920]{1,0:T(8,128)(2,1)S(1)}, u32[]{:S(2)}, u32[]{:S(2)}) %collective-permute-start.47) | collective-permute-done | bytes 368672 | tf_op jit(solution)/shard_map/ppermute | solution.py:442
  852.7 4.1 collective-permute-start.40
  856.8 4.3 collective-permute-start.42
  861.1 9.0 collective-permute-start.41
  876.2 5.9 collective-permute-done.41
  887.7 3.1 collective-permute-start.58
  895.1 4.4 collective-permute-done.56
  899.5 5.2 collective-permute-done.58
  904.7 15.9 %collective-permute-done.57 = bf16[96,1728]{1,0:T(8,128)(2,1)S(1)} collective-permute-done((bf16[96,1728]{1,0:T(8,128)(2,1)S(1)}, bf16[96,1728]{1,0:T(8,128)(2,1)S(1)}, u32[]{:S(2)}, u32[]{:S(2)}) %collective-permute-start.57) | collective-permute-done | bytes 331808 | tf_op jit(solution)/shard_map/ppermute | solution.py:442
  922.0 3.1 reshape.1721
  925.1 7.6 multiply_reduce_fusion.5
  936.1 37.6 %all-reduce.36 = (f32[29]{0:T(128)S(1)}, f32[29]{0:T(128)S(1)}, f32[10,768]{1,0:T(8,128)S(1)}) all-reduce(f32[29]{0:T(128)S(1)} %pad_maximum_fusion.37, f32[29]{0:T(128)S(1)} %pad_maximum_fusion.36, f32[10,768]{1,0:T(8,128)S(1)} %copy-done.145), channel_id=1, replica_groups=mesh['dp'=8,'mp'=4] {'dp','mp'}, use_global_device_ids=true, to_apply=%region_53.54 | all-reduce | flops 7738 | bytes 61904 | tf_op jit(solution)/shard_map/psum | solution.py:817
  (1064 shorter events, 492.1 us)
Async XLA Ops:
  3.7 75.3 %collective-permute-start.7 = (bf16[96,1536]{1,0:T(8,128)(2,1)}, bf16[96,1536]{1,0:T(8,128)(2,1)}, u32[]{:S(2)}, u32[]{:S(2)}) collective-permute-start(bf16[96,1536]{1,0:T(8,128)(2,1)} %pad_maximum_fusion.21), channel_id=1, source_target_pairs={{0,16},{4,20},{8,24},{12,28},{16,0},{20,4},{24,8},{28,12},{1,17},{... | collective-permute-start | bytes 884744 | tf_op jit(solution)/shard_map/ppermute | solution.py:442
  7.7 66.0 %collective-permute-start.6 = (bf16[96,1536]{1,0:T(8,128)(2,1)}, bf16[96,1536]{1,0:T(8,128)(2,1)}, u32[]{:S(2)}, u32[]{:S(2)}) collective-permute-start(bf16[96,1536]{1,0:T(8,128)(2,1)} %pad_maximum_fusion.21), channel_id=1, source_target_pairs={{0,8},{4,12},{8,16},{12,20},{16,24},{20,28},{24,0},{28,4},{1,9},{5... | collective-permute-start | bytes 884744 | tf_op jit(solution)/shard_map/ppermute | solution.py:442
  9.3 71.4 %collective-permute-start.8 = (bf16[96,1536]{1,0:T(8,128)(2,1)}, bf16[96,1536]{1,0:T(8,128)(2,1)}, u32[]{:S(2)}, u32[]{:S(2)}) collective-permute-start(bf16[96,1536]{1,0:T(8,128)(2,1)} %pad_maximum_fusion.21), channel_id=1, source_target_pairs={{0,24},{4,28},{8,0},{12,4},{16,8},{20,12},{24,16},{28,20},{1,25},{... | collective-permute-start | bytes 884744 | tf_op jit(solution)/shard_map/ppermute | solution.py:442
  19.2 38.7 %collective-permute-start.1 = (bf16[96,768]{1,0:T(8,128)(2,1)}, bf16[96,768]{1,0:T(8,128)(2,1)}, u32[]{:S(2)}, u32[]{:S(2)}) collective-permute-start(bf16[96,768]{1,0:T(8,128)(2,1)} %get-tuple-element.183), channel_id=1, source_target_pairs={{0,16},{4,20},{8,24},{12,28},{16,0},{20,4},{24,8},{28,12},{1,17},{... | collective-permute-start | bytes 442376 | tf_op jit(solution)/shard_map/ppermute | solution.py:442
  19.2 29.6 %collective-permute-start = (bf16[96,768]{1,0:T(8,128)(2,1)}, bf16[96,768]{1,0:T(8,128)(2,1)}, u32[]{:S(2)}, u32[]{:S(2)}) collective-permute-start(bf16[96,768]{1,0:T(8,128)(2,1)} %get-tuple-element.183), channel_id=1, source_target_pairs={{0,8},{4,12},{8,16},{12,20},{16,24},{20,28},{24,0},{28,4},{1,9},{5... | collective-permute-start | bytes 442376 | tf_op jit(solution)/shard_map/ppermute | solution.py:442
  48.9 6.9 collective-permute-start.25
  55.8 13.6 %collective-permute-start.2 = (bf16[96,768]{1,0:T(8,128)(2,1)}, bf16[96,768]{1,0:T(8,128)(2,1)S(1)}, u32[]{:S(2)}, u32[]{:S(2)}) collective-permute-start(bf16[96,768]{1,0:T(8,128)(2,1)} %get-tuple-element.183), channel_id=1, source_target_pairs={{0,24},{4,28},{8,0},{12,4},{16,8},{20,12},{24,16},{28,20},{1,25},{... | collective-permute-start | bytes 442376 | tf_op jit(solution)/shard_map/ppermute | solution.py:442
  57.9 8.7 collective-permute-start.26
  66.6 6.4 collective-permute-start.27
  69.4 46.5 %collective-permute-start.14 = (bf16[96,1728]{1,0:T(8,128)(2,1)S(1)}, bf16[96,1728]{1,0:T(8,128)(2,1)S(1)}, u32[]{:S(2)}, u32[]{:S(2)}) collective-permute-start(bf16[96,1728]{1,0:T(8,128)(2,1)S(1)} %copy-done.136), channel_id=1, source_target_pairs={{0,16},{4,20},{8,24},{12,28},{16,0},{20,4},{24,8},{28,12},{1,17},{... | collective-permute-start | bytes 995336 | tf_op jit(solution)/shard_map/ppermute | solution.py:442
  73.0 15.3 %collective-permute-start.13 = (bf16[96,1728]{1,0:T(8,128)(2,1)S(1)}, bf16[96,1728]{1,0:T(8,128)(2,1)S(1)}, u32[]{:S(2)}, u32[]{:S(2)}) collective-permute-start(bf16[96,1728]{1,0:T(8,128)(2,1)S(1)} %copy-done.136), channel_id=1, source_target_pairs={{0,8},{4,12},{8,16},{12,20},{16,24},{20,28},{24,0},{28,4},{1,9},{5... | collective-permute-start | bytes 995336 | tf_op jit(solution)/shard_map/ppermute | solution.py:442
  73.7 44.5 %collective-permute-start.15 = (bf16[96,1728]{1,0:T(8,128)(2,1)S(1)}, bf16[96,1728]{1,0:T(8,128)(2,1)S(1)}, u32[]{:S(2)}, u32[]{:S(2)}) collective-permute-start(bf16[96,1728]{1,0:T(8,128)(2,1)S(1)} %copy-done.136), channel_id=1, source_target_pairs={{0,24},{4,28},{8,0},{12,4},{16,8},{20,12},{24,16},{28,20},{1,25},{... | collective-permute-start | bytes 995336 | tf_op jit(solution)/shard_map/ppermute | solution.py:442
  79.1 54.9 %collective-permute-start.18 = (bf16[96,1920]{0,1:T(8,128)(2,1)}, bf16[96,1920]{0,1:T(8,128)(2,1)}, u32[]{:S(2)}, u32[]{:S(2)}) collective-permute-start(bf16[96,1920]{0,1:T(8,128)(2,1)} %get-tuple-element.284), channel_id=1, source_target_pairs={{0,16},{4,20},{8,24},{12,28},{16,0},{20,4},{24,8},{28,12},{1,17},{... | collective-permute-start | bytes 1105928 | tf_op jit(solution)/shard_map/ppermute | solution.py:442
  80.7 56.7 %collective-permute-start.17 = (bf16[96,1920]{0,1:T(8,128)(2,1)}, bf16[96,1920]{0,1:T(8,128)(2,1)}, u32[]{:S(2)}, u32[]{:S(2)}) collective-permute-start(bf16[96,1920]{0,1:T(8,128)(2,1)} %get-tuple-element.284), channel_id=1, source_target_pairs={{0,8},{4,12},{8,16},{12,20},{16,24},{20,28},{24,0},{28,4},{1,9},{5... | collective-permute-start | bytes 1105928 | tf_op jit(solution)/shard_map/ppermute | solution.py:442
  88.4 52.5 %collective-permute-start.19 = (bf16[96,1920]{0,1:T(8,128)(2,1)}, bf16[96,1920]{0,1:T(8,128)(2,1)}, u32[]{:S(2)}, u32[]{:S(2)}) collective-permute-start(bf16[96,1920]{0,1:T(8,128)(2,1)} %get-tuple-element.284), channel_id=1, source_target_pairs={{0,24},{4,28},{8,0},{12,4},{16,8},{20,12},{24,16},{28,20},{1,25},{... | collective-permute-start | bytes 1105928 | tf_op jit(solution)/shard_map/ppermute | solution.py:442
  115.9 31.7 %collective-permute-start.28 = (bf16[4,96,768]{2,1,0:T(8,128)(2,1)}, bf16[4,96,768]{2,1,0:T(8,128)(2,1)}, u32[]{:S(2)}, u32[]{:S(2)}) collective-permute-start(bf16[4,96,768]{2,1,0:T(8,128)(2,1)} %bitcast_dynamic-update-slice_fusion.8), channel_id=1, source_target_pairs={{0,4},{4,0},{8,12},{12,8},{16,20},{20,16},{24,28},{28,24},{1,5},{5... | collective-permute-start | bytes 1769480 | tf_op jit(solution)/shard_map/ppermute | solution.py:438
  118.2 32.5 %collective-permute-start.3 = (bf16[4,96,768]{2,1,0:T(8,128)(2,1)}, bf16[4,96,768]{2,1,0:T(8,128)(2,1)}, u32[]{:S(2)}, u32[]{:S(2)}) collective-permute-start(bf16[4,96,768]{2,1,0:T(8,128)(2,1)} %bitcast_dynamic-update-slice_fusion.12), channel_id=1, source_target_pairs={{0,4},{4,0},{8,12},{12,8},{16,20},{20,16},{24,28},{28,24},{1,5},{5... | collective-permute-start | bytes 1769480 | tf_op jit(solution)/shard_map/ppermute | solution.py:438
  133.9 36.0 %collective-permute-start.10 = (bf16[4,96,1536]{2,1,0:T(8,128)(2,1)S(1)}, bf16[4,96,1536]{2,1,0:T(8,128)(2,1)}, u32[]{:S(2)}, u32[]{:S(2)}) collective-permute-start(bf16[4,96,1536]{2,1,0:T(8,128)(2,1)S(1)} %bitcast_dynamic-update-slice_fusion.4), channel_id=1, source_target_pairs={{0,2},{1,3},{2,0},{3,1},{4,6},{5,7},{6,4},{7,5},{8,10},{9,11},{10,... | collective-permute-start | bytes 3538952 | tf_op jit(solution)/shard_map/ppermute | solution.py:434
  137.4 29.0 %collective-permute-start.9 = (bf16[4,96,1536]{2,1,0:T(8,128)(2,1)S(1)}, bf16[4,96,1536]{2,1,0:T(8,128)(2,1)}, u32[]{:S(2)}, u32[]{:S(2)}) collective-permute-start(bf16[4,96,1536]{2,1,0:T(8,128)(2,1)S(1)} %bitcast_dynamic-update-slice_fusion.4), channel_id=1, source_target_pairs={{0,4},{4,0},{8,12},{12,8},{16,20},{20,16},{24,28},{28,24},{1,5},{5... | collective-permute-start | bytes 3538952 | tf_op jit(solution)/shard_map/ppermute | solution.py:438
  140.9 55.0 %collective-permute-start.16 = (bf16[4,96,1728]{2,1,0:T(8,128)(2,1)}, bf16[4,96,1728]{2,1,0:T(8,128)(2,1)}, u32[]{:S(2)}, u32[]{:S(2)}) collective-permute-start(bf16[4,96,1728]{2,1,0:T(8,128)(2,1)} %bitcast_dynamic-update-slice_fusion), channel_id=1, source_target_pairs={{0,4},{4,0},{8,12},{12,8},{16,20},{20,16},{24,28},{28,24},{1,5},{5... | collective-permute-start | bytes 3981320 | tf_op jit(solution)/shard_map/ppermute | solution.py:438
  147.7 55.3 %collective-permute-start.22 = (bf16[4,96,1920]{2,1,0:T(8,128)(2,1)}, bf16[4,96,1920]{2,1,0:T(8,128)(2,1)}, u32[]{:S(2)}, u32[]{:S(2)}) collective-permute-start(bf16[4,96,1920]{2,1,0:T(8,128)(2,1)} %constant_dynamic-update-slice_fusion.32), channel_id=1, source_target_pairs={{0,2},{1,3},{2,0},{3,1},{4,6},{5,7},{6,4},{7,5},{8,10},{9,11},{10,... | collective-permute-start | bytes 4423688 | tf_op jit(solution)/shard_map/ppermute | solution.py:434
  150.7 76.7 %collective-permute-start.20 = (bf16[4,96,1920]{2,1,0:T(8,128)(2,1)}, bf16[4,96,1920]{2,1,0:T(8,128)(2,1)}, u32[]{:S(2)}, u32[]{:S(2)}) collective-permute-start(bf16[4,96,1920]{2,1,0:T(8,128)(2,1)} %constant_dynamic-update-slice_fusion.32), channel_id=1, source_target_pairs={{0,4},{4,0},{8,12},{12,8},{16,20},{20,16},{24,28},{28,24},{1,5},{5... | collective-permute-start | bytes 4423688 | tf_op jit(solution)/shard_map/ppermute | solution.py:438
  166.4 66.6 %collective-permute-start.4 = (bf16[768,768]{1,0:T(8,128)(2,1)}, bf16[768,768]{1,0:T(8,128)(2,1)}, u32[]{:S(2)}, u32[]{:S(2)}) collective-permute-start(bf16[768,768]{1,0:T(8,128)(2,1)} %bitcast.10), channel_id=1, source_target_pairs={{0,2},{1,3},{2,0},{3,1},{4,6},{5,7},{6,4},{7,5},{8,10},{9,11},{10,... | collective-permute-start | bytes 3538952 | tf_op jit(solution)/shard_map/ppermute | solution.py:434
  169.9 75.1 %collective-permute-start.29 = (bf16[768,768]{1,0:T(8,128)(2,1)}, bf16[768,768]{1,0:T(8,128)(2,1)}, u32[]{:S(2)}, u32[]{:S(2)}) collective-permute-start(bf16[768,768]{1,0:T(8,128)(2,1)} %bitcast.111), channel_id=1, source_target_pairs={{0,2},{1,3},{2,0},{3,1},{4,6},{5,7},{6,4},{7,5},{8,10},{9,11},{10,... | collective-permute-start | bytes 3538952 | tf_op jit(solution)/shard_map/ppermute | solution.py:434
  195.9 56.9 %collective-permute-start.11 = (bf16[4,96,1536]{2,1,0:T(8,128)(2,1)}, bf16[4,96,1536]{2,1,0:T(8,128)(2,1)}, u32[]{:S(2)}, u32[]{:S(2)}) collective-permute-start(bf16[4,96,1536]{2,1,0:T(8,128)(2,1)} %collective-permute-done.10), channel_id=1, source_target_pairs={{0,4},{4,0},{8,12},{12,8},{16,20},{20,16},{24,28},{28,24},{1,5},{5... | collective-permute-start | bytes 3538952 | tf_op jit(solution)/shard_map/ppermute | solution.py:438
  202.9 145.4 %collective-permute-start.21 = (bf16[768,1728]{0,1:T(8,128)(2,1)}, bf16[768,1728]{0,1:T(8,128)(2,1)}, u32[]{:S(2)}, u32[]{:S(2)}) collective-permute-start(bf16[768,1728]{0,1:T(8,128)(2,1)} %copy.494), channel_id=1, source_target_pairs={{0,2},{1,3},{2,0},{3,1},{4,6},{5,7},{6,4},{7,5},{8,10},{9,11},{10,... | collective-permute-start | bytes 7962632 | tf_op jit(solution)/shard_map/ppermute | solution.py:434
  227.5 54.1 %collective-permute-start.23 = (bf16[4,96,1920]{2,1,0:T(8,128)(2,1)}, bf16[4,96,1920]{2,1,0:T(8,128)(2,1)S(1)}, u32[]{:S(2)}, u32[]{:S(2)}) collective-permute-start(bf16[4,96,1920]{2,1,0:T(8,128)(2,1)} %collective-permute-done.22), channel_id=1, source_target_pairs={{0,4},{4,0},{8,12},{12,8},{16,20},{20,16},{24,28},{28,24},{1,5},{5... | collective-permute-start | bytes 4423688 | tf_op jit(solution)/shard_map/ppermute | solution.py:438
  244.8 10.1 %collective-permute-start.5 = (bf16[512,768]{1,0:T(8,128)(2,1)S(1)}, bf16[512,768]{1,0:T(8,128)(2,1)S(1)}, u32[]{:S(2)}, u32[]{:S(2)}) collective-permute-start(bf16[512,768]{1,0:T(8,128)(2,1)S(1)} %add_convert_fusion.10), channel_id=1, source_target_pairs={{0,1},{1,0},{2,3},{3,2},{4,5},{5,4},{6,7},{7,6},{8,9},{9,8},{10,11... | collective-permute-start | bytes 2359304 | tf_op jit(solution)/shard_map/ppermute | solution.py:430
  262.8 22.4 %collective-permute-start.12 = (bf16[512,768]{1,0:T(8,128)(2,1)S(1)}, bf16[512,768]{1,0:T(8,128)(2,1)S(1)}, u32[]{:S(2)}, u32[]{:S(2)}) collective-permute-start(bf16[512,768]{1,0:T(8,128)(2,1)S(1)} %add_convert_fusion.8), channel_id=1, source_target_pairs={{0,1},{1,0},{2,3},{3,2},{4,5},{5,4},{6,7},{7,6},{8,9},{9,8},{10,11... | collective-permute-start | bytes 2359304 | tf_op jit(solution)/shard_map/ppermute | solution.py:430
  413.8 7.5 collective-permute-start.24
  439.0 8.2 collective-permute-start.30
  442.5 154.5 %collective-permute-start.49 = (bf16[768,768]{0,1:T(8,128)(2,1)}, bf16[768,768]{0,1:T(8,128)(2,1)}, u32[]{:S(2)}, u32[]{:S(2)}) collective-permute-start(bf16[768,768]{0,1:T(8,128)(2,1)} %pad_maximum_fusion.10), channel_id=1, source_target_pairs={{0,2},{1,3},{2,0},{3,1},{4,6},{5,7},{6,4},{7,5},{8,10},{9,11},{10,... | collective-permute-start | bytes 3538952 | tf_op jit(solution)/shard_map/ppermute | solution.py:434
  463.7 159.3 %collective-permute-start.31 = (bf16[512,768]{1,0:T(8,128)(2,1)}, bf16[512,768]{1,0:T(8,128)(2,1)}, u32[]{:S(2)}, u32[]{:S(2)}) collective-permute-start(bf16[512,768]{1,0:T(8,128)(2,1)} %get-tuple-element.243), channel_id=1, source_target_pairs={{0,2},{1,3},{2,0},{3,1},{4,6},{5,7},{6,4},{7,5},{8,10},{9,11},{10,... | collective-permute-start | bytes 2359304 | tf_op jit(solution)/shard_map/ppermute | solution.py:434
  557.0 104.1 %collective-permute-start.44 = (bf16[4,96,1920]{2,1,0:T(8,128)(2,1)}, bf16[4,96,1920]{2,1,0:T(8,128)(2,1)}, u32[]{:S(2)}, u32[]{:S(2)}) collective-permute-start(bf16[4,96,1920]{2,1,0:T(8,128)(2,1)} %fusion.56), channel_id=1, source_target_pairs={{0,4},{4,0},{8,12},{12,8},{16,20},{20,16},{24,28},{28,24},{1,5},{5... | collective-permute-start | bytes 4423688 | tf_op jit(solution)/shard_map/ppermute | solution.py:438
  559.8 219.1 %collective-permute-start.43 = (bf16[4,96,1920]{2,1,0:T(8,128)(2,1)}, bf16[4,96,1920]{2,1,0:T(8,128)(2,1)}, u32[]{:S(2)}, u32[]{:S(2)}) collective-permute-start(bf16[4,96,1920]{2,1,0:T(8,128)(2,1)} %fusion.60), channel_id=1, source_target_pairs={{0,4},{4,0},{8,12},{12,8},{16,20},{20,16},{24,28},{28,24},{1,5},{5... | collective-permute-start | bytes 4423688 | tf_op jit(solution)/shard_map/ppermute | solution.py:438
  590.6 16.2 %collective-permute-start.33 = (bf16[512,768]{1,0:T(8,128)(2,1)S(1)}, bf16[512,768]{1,0:T(8,128)(2,1)}, u32[]{:S(2)}, u32[]{:S(2)}) collective-permute-start(bf16[512,768]{1,0:T(8,128)(2,1)S(1)} %add_convert_fusion.2), channel_id=1, source_target_pairs={{0,1},{1,0},{2,3},{3,2},{4,5},{5,4},{6,7},{7,6},{8,9},{9,8},{10,11... | collective-permute-start | bytes 2359304 | tf_op jit(solution)/shard_map/ppermute | solution.py:430
  605.2 30.4 %collective-permute-start.50 = (bf16[4,96,768]{2,1,0:T(8,128)(2,1)}, bf16[4,96,768]{2,1,0:T(8,128)(2,1)}, u32[]{:S(2)}, u32[]{:S(2)}) collective-permute-start(bf16[4,96,768]{2,1,0:T(8,128)(2,1)} %fusion.124), channel_id=1, source_target_pairs={{0,4},{4,0},{8,12},{12,8},{16,20},{20,16},{24,28},{28,24},{1,5},{5... | collective-permute-start | bytes 1769480 | tf_op jit(solution)/shard_map/ppermute | solution.py:438
  636.9 14.2 %collective-permute-start.51 = (bf16[96,768]{1,0:T(8,128)(2,1)S(1)}, bf16[96,768]{1,0:T(8,128)(2,1)S(1)}, u32[]{:S(2)}, u32[]{:S(2)}) collective-permute-start(bf16[96,768]{1,0:T(8,128)(2,1)S(1)} %get-tuple-element.246), channel_id=1, source_target_pairs={{0,8},{4,12},{8,16},{12,20},{16,24},{20,28},{24,0},{28,4},{1,9},{5... | collective-permute-start | bytes 442376 | tf_op jit(solution)/shard_map/ppermute | solution.py:442
  645.8 7.1 collective-permute-start.53
  645.9 12.8 %collective-permute-start.52 = (bf16[96,768]{1,0:T(8,128)(2,1)S(1)}, bf16[96,768]{1,0:T(8,128)(2,1)S(1)}, u32[]{:S(2)}, u32[]{:S(2)}) collective-permute-start(bf16[96,768]{1,0:T(8,128)(2,1)S(1)} %get-tuple-element.248), channel_id=1, source_target_pairs={{0,16},{4,20},{8,24},{12,28},{16,0},{20,4},{24,8},{28,12},{1,17},{... | collective-permute-start | bytes 442376 | tf_op jit(solution)/shard_map/ppermute | solution.py:442
  651.1 69.8 %collective-permute-start.54 = (bf16[768,1728]{0,1:T(8,128)(2,1)}, bf16[768,1728]{0,1:T(8,128)(2,1)}, u32[]{:S(2)}, u32[]{:S(2)}) collective-permute-start(bf16[768,1728]{0,1:T(8,128)(2,1)} %convolution_convert_fusion), channel_id=1, source_target_pairs={{0,2},{1,3},{2,0},{3,1},{4,6},{5,7},{6,4},{7,5},{8,10},{9,11},{10,... | collective-permute-start | bytes 7962632 | tf_op jit(solution)/shard_map/ppermute | solution.py:434
  652.8 11.8 %collective-permute-start.34 = (bf16[512,768]{1,0:T(8,128)(2,1)S(1)}, bf16[512,768]{1,0:T(8,128)(2,1)S(1)}, u32[]{:S(2)}, u32[]{:S(2)}) collective-permute-start(bf16[512,768]{1,0:T(8,128)(2,1)S(1)} %add_convert_fusion.1), channel_id=1, source_target_pairs={{0,1},{1,0},{2,3},{3,2},{4,5},{5,4},{6,7},{7,6},{8,9},{9,8},{10,11... | collective-permute-start | bytes 2359304 | tf_op jit(solution)/shard_map/ppermute | solution.py:430
  658.7 146.6 %collective-permute-start.59 = (bf16[4,96,1536]{2,1,0:T(8,128)(2,1)}, bf16[4,96,1536]{2,1,0:T(8,128)(2,1)}, u32[]{:S(2)}, u32[]{:S(2)}) collective-permute-start(bf16[4,96,1536]{2,1,0:T(8,128)(2,1)} %fusion.88), channel_id=1, source_target_pairs={{0,4},{4,0},{8,12},{12,8},{16,20},{20,16},{24,28},{28,24},{1,5},{5... | collective-permute-start | bytes 3538952 | tf_op jit(solution)/shard_map/ppermute | solution.py:438
  661.0 49.3 %collective-permute-start.60 = (bf16[4,96,1536]{2,1,0:T(8,128)(2,1)}, bf16[4,96,1536]{2,1,0:T(8,128)(2,1)}, u32[]{:S(2)}, u32[]{:S(2)}) collective-permute-start(bf16[4,96,1536]{2,1,0:T(8,128)(2,1)} %fusion.84), channel_id=1, source_target_pairs={{0,4},{4,0},{8,12},{12,8},{16,20},{20,16},{24,28},{28,24},{1,5},{5... | collective-permute-start | bytes 3538952 | tf_op jit(solution)/shard_map/ppermute | solution.py:438
  681.6 32.9 %collective-permute-start.35 = (bf16[512,768]{1,0:T(8,128)(2,1)S(1)}, bf16[512,768]{1,0:T(8,128)(2,1)S(1)}, u32[]{:S(2)}, u32[]{:S(2)}) collective-permute-start(bf16[512,768]{1,0:T(8,128)(2,1)S(1)} %add_convert_fusion), channel_id=1, source_target_pairs={{0,1},{1,0},{2,3},{3,2},{4,5},{5,4},{6,7},{7,6},{8,9},{9,8},{10,11... | collective-permute-start | bytes 2359304 | tf_op jit(solution)/shard_map/ppermute | solution.py:430
  710.3 92.3 %collective-permute-start.45 = (bf16[4,96,1920]{2,1,0:T(8,128)(2,1)}, bf16[4,96,1920]{2,1,0:T(8,128)(2,1)}, u32[]{:S(2)}, u32[]{:S(2)}) collective-permute-start(bf16[4,96,1920]{2,1,0:T(8,128)(2,1)} %fusion.6), channel_id=1, source_target_pairs={{0,2},{1,3},{2,0},{3,1},{4,6},{5,7},{6,4},{7,5},{8,10},{9,11},{10,... | collective-permute-start | bytes 4423688 | tf_op jit(solution)/shard_map/ppermute | solution.py:434
  714.5 56.6 %collective-permute-start.38 = (bf16[768,768]{0,1:T(8,128)(2,1)}, bf16[768,768]{0,1:T(8,128)(2,1)S(1)}, u32[]{:S(2)}, u32[]{:S(2)}) collective-permute-start(bf16[768,768]{0,1:T(8,128)(2,1)} %pad_maximum_fusion.9), channel_id=1, source_target_pairs={{0,2},{1,3},{2,0},{3,1},{4,6},{5,7},{6,4},{7,5},{8,10},{9,11},{10,... | collective-permute-start | bytes 3538952 | tf_op jit(solution)/shard_map/ppermute | solution.py:434
  720.9 89.4 %collective-permute-start.61 = (bf16[4,96,1536]{2,1,0:T(8,128)(2,1)}, bf16[4,96,1536]{2,1,0:T(8,128)(2,1)}, u32[]{:S(2)}, u32[]{:S(2)}) collective-permute-start(bf16[4,96,1536]{2,1,0:T(8,128)(2,1)} %fusion.17), channel_id=1, source_target_pairs={{0,2},{1,3},{2,0},{3,1},{4,6},{5,7},{6,4},{7,5},{8,10},{9,11},{10,... | collective-permute-start | bytes 3538952 | tf_op jit(solution)/shard_map/ppermute | solution.py:434
  771.0 30.0 %collective-permute-start.36 = (bf16[256,768]{1,0:T(8,128)(2,1)}, bf16[256,768]{1,0:T(8,128)(2,1)}, u32[]{:S(2)}, u32[]{:S(2)}) collective-permute-start(bf16[256,768]{1,0:T(8,128)(2,1)} %constant_dynamic-slice_fusion), channel_id=1, source_target_pairs={{0,2},{1,3},{2,0},{3,1},{4,6},{5,7},{6,4},{7,5},{8,10},{9,11},{10,... | collective-permute-start | bytes 1179656 | tf_op jit(solution)/shard_map/ppermute | solution.py:434
  778.9 104.6 %collective-permute-start.55 = (bf16[4,96,1728]{2,1,0:T(8,128)(2,1)}, bf16[4,96,1728]{2,1,0:T(8,128)(2,1)}, u32[]{:S(2)}, u32[]{:S(2)}) collective-permute-start(bf16[4,96,1728]{2,1,0:T(8,128)(2,1)} %fusion.71), channel_id=1, source_target_pairs={{0,4},{4,0},{8,12},{12,8},{16,20},{20,16},{24,28},{28,24},{1,5},{5... | collective-permute-start | bytes 3981320 | tf_op jit(solution)/shard_map/ppermute | solution.py:438
  801.1 49.8 %collective-permute-start.39 = (bf16[4,96,768]{2,1,0:T(8,128)(2,1)S(1)}, bf16[4,96,768]{2,1,0:T(8,128)(2,1)S(1)}, u32[]{:S(2)}, u32[]{:S(2)}) collective-permute-start(bf16[4,96,768]{2,1,0:T(8,128)(2,1)S(1)} %fusion.123), channel_id=1, source_target_pairs={{0,4},{4,0},{8,12},{12,8},{16,20},{20,16},{24,28},{28,24},{1,5},{5... | collective-permute-start | bytes 1769480 | tf_op jit(solution)/shard_map/ppermute | solution.py:438
  802.6 10.8 %collective-permute-start.37 = (bf16[256,768]{1,0:T(8,128)(2,1)}, bf16[256,768]{1,0:T(8,128)(2,1)S(1)}, u32[]{:S(2)}, u32[]{:S(2)}) collective-permute-start(bf16[256,768]{1,0:T(8,128)(2,1)} %collective-permute-done.36), channel_id=1, source_target_pairs={{0,1},{1,0},{2,3},{3,2},{4,5},{5,4},{6,7},{7,6},{8,9},{9,8},{10,11... | collective-permute-start | bytes 1179656 | tf_op jit(solution)/shard_map/ppermute | solution.py:430
  805.3 15.4 %collective-permute-start.46 = (bf16[96,1920]{1,0:T(8,128)(2,1)S(1)}, bf16[96,1920]{1,0:T(8,128)(2,1)S(1)}, u32[]{:S(2)}, u32[]{:S(2)}) collective-permute-start(bf16[96,1920]{1,0:T(8,128)(2,1)S(1)} %get-tuple-element.220), channel_id=1, source_target_pairs={{0,8},{4,12},{8,16},{12,20},{16,24},{20,28},{24,0},{28,4},{1,9},{5... | collective-permute-start | bytes 1105928 | tf_op jit(solution)/shard_map/ppermute | solution.py:442
  810.3 27.7 %collective-permute-start.48 = (bf16[96,1920]{1,0:T(8,128)(2,1)S(1)}, bf16[96,1920]{1,0:T(8,128)(2,1)S(1)}, u32[]{:S(2)}, u32[]{:S(2)}) collective-permute-start(bf16[96,1920]{1,0:T(8,128)(2,1)S(1)} %get-tuple-element.221), channel_id=1, source_target_pairs={{0,24},{4,28},{8,0},{12,4},{16,8},{20,12},{24,16},{28,20},{1,25},{... | collective-permute-start | bytes 1105928 | tf_op jit(solution)/shard_map/ppermute | solution.py:442
  813.4 37.1 %collective-permute-start.47 = (bf16[96,1920]{1,0:T(8,128)(2,1)S(1)}, bf16[96,1920]{1,0:T(8,128)(2,1)S(1)}, u32[]{:S(2)}, u32[]{:S(2)}) collective-permute-start(bf16[96,1920]{1,0:T(8,128)(2,1)S(1)} %get-tuple-element.222), channel_id=1, source_target_pairs={{0,16},{4,20},{8,24},{12,28},{16,0},{20,4},{24,8},{28,12},{1,17},{... | collective-permute-start | bytes 1105928 | tf_op jit(solution)/shard_map/ppermute | solution.py:442
  820.7 36.2 %collective-permute-start.62 = (bf16[96,1536]{1,0:T(8,128)(2,1)S(1)}, bf16[96,1536]{1,0:T(8,128)(2,1)S(1)}, u32[]{:S(2)}, u32[]{:S(2)}) collective-permute-start(bf16[96,1536]{1,0:T(8,128)(2,1)S(1)} %get-tuple-element.232), channel_id=1, source_target_pairs={{0,8},{4,12},{8,16},{12,20},{16,24},{20,28},{24,0},{28,4},{1,9},{5... | collective-permute-start | bytes 884744 | tf_op jit(solution)/shard_map/ppermute | solution.py:442
  838.1 23.1 %collective-permute-start.64 = (bf16[96,1536]{1,0:T(8,128)(2,1)S(1)}, bf16[96,1536]{1,0:T(8,128)(2,1)S(1)}, u32[]{:S(2)}, u32[]{:S(2)}) collective-permute-start(bf16[96,1536]{1,0:T(8,128)(2,1)S(1)} %get-tuple-element.233), channel_id=1, source_target_pairs={{0,24},{4,28},{8,0},{12,4},{16,8},{20,12},{24,16},{28,20},{1,25},{... | collective-permute-start | bytes 884744 | tf_op jit(solution)/shard_map/ppermute | solution.py:442
  850.6 22.2 %collective-permute-start.63 = (bf16[96,1536]{1,0:T(8,128)(2,1)S(1)}, bf16[96,1536]{1,0:T(8,128)(2,1)S(1)}, u32[]{:S(2)}, u32[]{:S(2)}) collective-permute-start(bf16[96,1536]{1,0:T(8,128)(2,1)S(1)} %get-tuple-element.234), channel_id=1, source_target_pairs={{0,16},{4,20},{8,24},{12,28},{16,0},{20,4},{24,8},{28,12},{1,17},{... | collective-permute-start | bytes 884744 | tf_op jit(solution)/shard_map/ppermute | solution.py:442
  852.7 23.5 %collective-permute-start.40 = (bf16[96,768]{1,0:T(8,128)(2,1)S(1)}, bf16[96,768]{1,0:T(8,128)(2,1)S(1)}, u32[]{:S(2)}, u32[]{:S(2)}) collective-permute-start(bf16[96,768]{1,0:T(8,128)(2,1)S(1)} %get-tuple-element.249), channel_id=1, source_target_pairs={{0,8},{4,12},{8,16},{12,20},{16,24},{20,28},{24,0},{28,4},{1,9},{5... | collective-permute-start | bytes 442376 | tf_op jit(solution)/shard_map/ppermute | solution.py:442
  856.8 19.4 %collective-permute-start.42 = (bf16[96,768]{1,0:T(8,128)(2,1)S(1)}, bf16[96,768]{1,0:T(8,128)(2,1)S(1)}, u32[]{:S(2)}, u32[]{:S(2)}) collective-permute-start(bf16[96,768]{1,0:T(8,128)(2,1)S(1)} %get-tuple-element.250), channel_id=1, source_target_pairs={{0,24},{4,28},{8,0},{12,4},{16,8},{20,12},{24,16},{28,20},{1,25},{... | collective-permute-start | bytes 442376 | tf_op jit(solution)/shard_map/ppermute | solution.py:442
  861.1 21.0 %collective-permute-start.41 = (bf16[96,768]{1,0:T(8,128)(2,1)S(1)}, bf16[96,768]{1,0:T(8,128)(2,1)S(1)}, u32[]{:S(2)}, u32[]{:S(2)}) collective-permute-start(bf16[96,768]{1,0:T(8,128)(2,1)S(1)} %get-tuple-element.251), channel_id=1, source_target_pairs={{0,16},{4,20},{8,24},{12,28},{16,0},{20,4},{24,8},{28,12},{1,17},{... | collective-permute-start | bytes 442376 | tf_op jit(solution)/shard_map/ppermute | solution.py:442
  886.3 13.2 %collective-permute-start.56 = (bf16[96,1728]{1,0:T(8,128)(2,1)S(1)}, bf16[96,1728]{1,0:T(8,128)(2,1)S(1)}, u32[]{:S(2)}, u32[]{:S(2)}) collective-permute-start(bf16[96,1728]{1,0:T(8,128)(2,1)S(1)} %get-tuple-element.227), channel_id=1, source_target_pairs={{0,8},{4,12},{8,16},{12,20},{16,24},{20,28},{24,0},{28,4},{1,9},{5... | collective-permute-start | bytes 995336 | tf_op jit(solution)/shard_map/ppermute | solution.py:442
  887.7 17.0 %collective-permute-start.58 = (bf16[96,1728]{1,0:T(8,128)(2,1)S(1)}, bf16[96,1728]{1,0:T(8,128)(2,1)S(1)}, u32[]{:S(2)}, u32[]{:S(2)}) collective-permute-start(bf16[96,1728]{1,0:T(8,128)(2,1)S(1)} %get-tuple-element.228), channel_id=1, source_target_pairs={{0,24},{4,28},{8,0},{12,4},{16,8},{20,12},{24,16},{28,20},{1,25},{... | collective-permute-start | bytes 995336 | tf_op jit(solution)/shard_map/ppermute | solution.py:442
  890.8 29.7 %collective-permute-start.57 = (bf16[96,1728]{1,0:T(8,128)(2,1)S(1)}, bf16[96,1728]{1,0:T(8,128)(2,1)S(1)}, u32[]{:S(2)}, u32[]{:S(2)}) collective-permute-start(bf16[96,1728]{1,0:T(8,128)(2,1)S(1)} %get-tuple-element.229), channel_id=1, source_target_pairs={{0,16},{4,20},{8,24},{12,28},{16,0},{20,4},{24,8},{28,12},{1,17},{... | collective-permute-start | bytes 995336 | tf_op jit(solution)/shard_map/ppermute | solution.py:442
  (258 other events, 2886.3 us)

commit v2 on v0

--- a/solution.py
+++ b/solution.py
@@ -4,6 +4,8 @@
 import jax
 import jax.numpy as jnp
 from jax import lax
+from jax.experimental import pallas as pl
+from jax.experimental.pallas import tpu as pltpu
 from jax.sharding import PartitionSpec as P
 
 HD = 64
@@ -207,7 +209,7 @@
     return (first_new, second_new, update)
 
 
-def per_device(
+def generic_device(
     tokens,
     noise_field,
     codec_tokens,
@@ -418,7 +420,1051 @@
     )
 
 
+CORE_SWAP = [(i, i ^ 1) for i in range(4)]
+X_SWAP = [(i, i ^ 2) for i in range(4)]
+LOW = jnp.bfloat16
+F32 = jnp.float32
+
+
+def swap_core(v):
+    return lax.ppermute(v, "mp", CORE_SWAP)
+
+
+def swap_x(v):
+    return lax.ppermute(v, "mp", X_SWAP)
+
+
+def by_parity(flag, own, other, axis):
+    first = jnp.where(flag == 0, own, other)
+    second = jnp.where(flag == 0, other, own)
+    return jnp.stack([first, second], axis=axis)
+
+
+def pick(v, index, axis):
+    return lax.dynamic_index_in_dim(v, index, axis, keepdims=False)
+
+
+def ln_stats(v):
+    centre = v - jnp.mean(v, axis=-1, keepdims=True)
+    scale = lax.rsqrt(jnp.mean(centre * centre, axis=-1, keepdims=True) + NORM_EPS)
+    return centre * scale, scale
+
+
+def ln_back(v, gain, grad):
+    hat, scale = ln_stats(v)
+    pulled = grad * gain
+    back = scale * (
+        pulled
+        - jnp.mean(pulled, axis=-1, keepdims=True)
+        - hat * jnp.mean(pulled * hat, axis=-1, keepdims=True)
+    )
+    return back, jnp.sum(grad * hat, axis=0, keepdims=True), jnp.sum(grad, axis=0, keepdims=True)
+
+
+def mm(a, b):
+    return lax.dot_general(a, b, (((1,), (0,)), ((), ())), preferred_element_type=F32)
+
+
+def mm_nt(a, b):
+    return lax.dot_general(a, b, (((1,), (1,)), ((), ())), preferred_element_type=F32)
+
+
+def mm_tn(a, b):
+    return lax.dot_general(a, b, (((0,), (0,)), ((), ())), preferred_element_type=F32)
+
+
+ANY = pl.ANY
+VM = pltpu.VMEM
+ROWS = 512
+STEP_ROWS = 128
+
+
+def spec_any():
+    return pl.BlockSpec(memory_space=pl.ANY)
+
+
+def spec_vm():
+    return pl.BlockSpec(memory_space=pltpu.VMEM)
+
+
+def run_kernel(body, name, ins, outs, scratch, hbm=(), flops=0):
+    in_specs = [spec_any() if k in hbm else spec_vm() for k in range(len(ins))]
+    moved = sum(v.size * v.dtype.itemsize for v in ins) + sum(
+        math.prod(s) * jnp.dtype(t).itemsize for s, t in outs
+    )
+    return pl.pallas_call(
+        body,
+        name=name,
+        in_specs=in_specs,
+        out_specs=[spec_vm() for _ in outs],
+        out_shape=[jax.ShapeDtypeStruct(s, t) for s, t in outs],
+        scratch_shapes=scratch,
+        compiler_params=pltpu.CompilerParams(vmem_limit_bytes=56 << 20),
+        cost_estimate=pl.CostEstimate(flops=flops, bytes_accessed=moved, transcendentals=0),
+    )(*ins)
+
+
+def each_rows(fn, total=ROWS, step=STEP_ROWS):
+    def body(k, carry):
+        fn(pl.ds(pl.multiple_of(k * step, step), step))
+        return carry
+
+    lax.fori_loop(0, total // step, body, 0)
+
+
+def start_copies(pairs, sems):
+    copies = [pltpu.make_async_copy(a, b, sems.at[k]) for k, (a, b) in enumerate(pairs)]
+    for c in copies:
+        c.start()
+    return copies
+
+
+def group_mats(channels, width):
+    count = channels // width
+    r = lax.broadcasted_iota(jnp.int32, (channels, count), 0)
+    c = lax.broadcasted_iota(jnp.int32, (channels, count), 1) * width
+    down = ((r >= c) & (r < c + width)).astype(F32)
+    r = lax.broadcasted_iota(jnp.int32, (count, channels), 1)
+    c = lax.broadcasted_iota(jnp.int32, (count, channels), 0) * width
+    up = ((r >= c) & (r < c + width)).astype(F32)
+    return down, up
+
+
+def exact_dot(a, b):
+    return jnp.dot(a, b, precision=HIGHEST_PRECISION, preferred_element_type=F32)
+
+
+def group_average(row, mats, width):
+    wide = jnp.broadcast_to(row, (8, row.shape[1]))
+    return exact_dot(exact_dot(wide, mats[0]) * (1.0 / (width * ROWS)), mats[1])[0:1]
+
+
+def gelu_parts(v):
+    k = math.sqrt(2.0 / math.pi)
+    t = jnp.tanh(k * (v + 0.044715 * (v * v * v)))
+    return t, 0.5 * v * (1.0 + t)
+
+
+def gelu_slope(v, t):
+    k = math.sqrt(2.0 / math.pi)
+    return 0.5 * (1.0 + t) + 0.5 * v * (1.0 - t * t) * (k * (1.0 + 3 * 0.044715 * (v * v)))
+
+
+def column_of(shape):
+    return lax.broadcasted_iota(jnp.int32, shape, 0) % TIME
+
+
+def from_left(v):
+    return jnp.where(column_of(v.shape) == 0, 0.0, pltpu.roll(v, 1, 0))
+
+
+def from_right(v):
+    return jnp.where(column_of(v.shape) == TIME - 1, 0.0, pltpu.roll(v, v.shape[0] - 1, 0))
+
+
+def softmax_heads(q, k, v, heads, score_scale, mask):
+    mixed, logs = [], []
+    for h in range(heads):
+        s = mm_nt(q[:, HD * h : HD * (h + 1)], k[:, HD * h : HD * (h + 1)]) * score_scale
+        if mask is not None:
+            s = jnp.where(mask, s, MASK_VALUE)
+        top = jnp.max(s, axis=1, keepdims=True)
+        e = jnp.exp(s - top)
+        total = jnp.sum(e, axis=1, keepdims=True)
+        soft = (e * (1.0 / total)).astype(LOW)
+        mixed.append(mm(soft, v[:, HD * h : HD * (h + 1)]))
+        logs.append(top + jnp.log(total))
+    return jnp.concatenate(mixed, axis=1).astype(LOW), logs
+
+
+def softmax_heads_back(q, k, v, g, logs, heads, score_scale, mask):
+    dq, dk, dv = [], [], []
+    for h in range(heads):
+        cols = slice(HD * h, HD * (h + 1))
+        s = mm_nt(q[:, cols], k[:, cols]) * score_scale
+        if mask is not None:
+            s = jnp.where(mask, s, MASK_VALUE)
+        soft = jnp.exp(s - logs[h])
+        gs = mm_nt(g[:, cols], v[:, cols])
+        dv.append(mm_tn(soft.astype(LOW), g[:, cols]))
+        dot = jnp.sum(soft * gs, axis=1, keepdims=True)
+        ds = (soft * (gs - dot)).astype(LOW)
+        dq.append(mm(ds, k[:, cols]) * score_scale)
+        dk.append(mm_tn(ds, q[:, cols]))
+    return [jnp.concatenate(d, axis=1) for d in (dq, dk, dv)]
+
+
+def attn_forward(seg_col, seg_row, tok, norms, w, n1, qkv, mixed, logs, part, wv, sems):
+    n = mixed.shape[2]
+    copies = start_copies([(w.at[0], wv.at[0]), (w.at[1], wv.at[1])], sems)
+
+    def norm(r):
+        hat, _ = ln_stats(tok[r, :].astype(F32))
+        n1[r, :] = (hat * norms[0:1, :] + norms[1:2, :]).astype(LOW)
+
+    each_rows(norm)
+    for i in range(2):
+        copies[i].wait()
+        qkv[i] = mm(n1[...], wv[i, :, : 3 * n]).astype(LOW)
+
+    def heads(r):
+        mask = seg_col[r, :] == seg_row[...]
+        found = []
+        for i in range(2):
+            got, logs_i = softmax_heads(
+                qkv[i, r, 0:n], qkv[i, :, n : 2 * n], qkv[i, :, 2 * n : 3 * n],
+                n // HD, HD ** (-0.5), mask,
+            )
+            mixed[i, r, :] = got
+            found += logs_i
+        logs[r, :] = jnp.concatenate(found, axis=1)
+
+    each_rows(heads)
+    total = mm_nt(mixed[0], wv[0, :, 3 * n :]) + mm_nt(mixed[1], wv[1, :, 3 * n :])
+    part[...] = total.astype(LOW)
+
+
+def mlp_forward(tok, own, other, norms, w, resid, n2, part, wv, acc, sems):
+    hid = wv.shape[2] // 2
+    copies = start_copies([(w.at[0], wv.at[0]), (w.at[1], wv.at[1])], sems)
+
+    def norm(r):
+        v = tok[r, :].astype(F32) + (own[r, :].astype(F32) + other[r, :].astype(F32))
+        resid[r, :] = v
+        hat, _ = ln_stats(v)
+        n2[r, :] = (hat * norms[2:3, :] + norms[3:4, :]).astype(LOW)
+
+    each_rows(norm)
+    block = 256
+    for i in range(2):
+        copies[i].wait()
+        for b in range(hid // block):
+            pre = mm(n2[...], wv[i, :, block * b : block * (b + 1)])
+            hidden = gelu_parts(pre)[1].astype(LOW)
+            term = mm_nt(hidden, wv[i, :, hid + block * b : hid + block * (b + 1)])
+            if i == 0 and b == 0:
+                acc[...] = term
+            else:
+                acc[...] += term
+    part[...] = acc[...].astype(LOW)
+
+
+def conv_forward(
+    level, resid, own, other, noise, norms, side, embed, w, u,
+    noisy, first, conv, taps, part, pad, wv, uv, sems,
+):
+    n = conv.shape[2]
+    width = noisy.shape[1] // GROUPS
+    copies = start_copies(
+        [(w.at[0], wv.at[0]), (w.at[1], wv.at[1]), (u.at[0], uv.at[0]), (u.at[1], uv.at[1])], sems
+    )
+    mats = group_mats(noisy.shape[1], width)
+    mats_n = group_mats(n, width)
+    pad[0:TIME, :] = jnp.zeros((TIME, pad.shape[1]), LOW)
+    pad[TIME + ROWS :, :] = jnp.zeros((TIME, pad.shape[1]), LOW)
+
+    def join(r):
+        v = resid[r, :] + (own[r, :].astype(F32) + other[r, :].astype(F32))
+        noisy[r, :] = v + level[...] * noise[r, :].astype(F32)
+
+    each_rows(join)
+    mean = group_average(jnp.sum(noisy[...], axis=0, keepdims=True), mats, width)
+    centre = noisy[...] - mean
+    var = group_average(jnp.sum(centre * centre, axis=0, keepdims=True), mats, width)
+    scale = lax.rsqrt(var + NORM_EPS) * norms[4:5, :]
+
+    def act(r):
+        v = (noisy[r, :] - mean) * scale + norms[5:6, :]
+        low = (v * jax.nn.sigmoid(v)).astype(LOW)
+        first[r, :] = low
+
+    each_rows(act)
+    pad[TIME : TIME + ROWS, :] = first[...]
+    for i in range(2):
+        copies[i].wait()
+        q = None
+        for a in range(3):
+            term = mm(pad[TIME * a : TIME * a + ROWS, :], wv[i, :, 3 * n * a : 3 * n * (a + 1)])
+            q = term if q is None else q + term
+        shift = mm(embed[...], wv[i, :, 9 * n : 10 * n])[0:1]
+        c1 = from_left(q[:, :n]) + q[:, n : 2 * n] + from_right(q[:, 2 * n :]) + shift
+        conv[i] = c1
+        mean_n = group_average(jnp.sum(c1, axis=0, keepdims=True), mats_n, width)
+        c1 = c1 - mean_n
+        var_n = group_average(jnp.sum(c1 * c1, axis=0, keepdims=True), mats_n, width)
+        v = c1 * lax.rsqrt(var_n + NORM_EPS) * side[i, 0:1, :] + side[i, 1:2, :]
+        v = v * jax.nn.sigmoid(v)
+        taps[i, 0:TIME, :] = jnp.zeros((TIME, 3 * n), LOW)
+        taps[i, TIME + ROWS :, :] = jnp.zeros((TIME, 3 * n), LOW)
+        taps[i, TIME : TIME + ROWS, :] = jnp.concatenate(
+            [from_left(v), v, from_right(v)], axis=1
+        ).astype(LOW)
+    total = None
+    for i in range(2):
+        copies[2 + i].wait()
+        for a in range(3):
+            term = mm_nt(
+                taps[i, TIME * a : TIME * a + ROWS, :], uv[i, :, 3 * n * a : 3 * n * (a + 1)]
+            )
+            total = term if total is None else total + term
+    part[...] = total.astype(LOW)
+
+
+def cross_forward(
+    noisy, own, other, codec, norms, w, resid, n3, cq, ckv, mixed, logs, part, wv, sems
+):
+    n = mixed.shape[2]
+    copies = start_copies([(w.at[0], wv.at[0]), (w.at[1], wv.at[1])], sems)
+
+    def norm(r):
+        v = noisy[r, :] + (own[r, :].astype(F32) + other[r, :].astype(F32))
+        resid[r, :] = v
+        hat, _ = ln_stats(v)
+        n3[r, :] = (hat * norms[8:9, :] + norms[9:10, :]).astype(LOW)
+
+    each_rows(norm)
+    for i in range(2):
+        copies[i].wait()
+        cq[i] = mm(n3[...], wv[i, :, :n]).astype(LOW)
+        ckv[i] = mm(codec[...], wv[i, :, n : 3 * n]).astype(LOW)
+
+    def heads(r):
+        found = []
+        for i in range(2):
+            got, logs_i = softmax_heads(
+                cq[i, r, :], ckv[i, :, :n], ckv[i, :, n:], n // HD, HD ** (-0.5), None
+            )
+            mixed[i, r, :] = got
+            found += logs_i
+        logs[r, :] = jnp.concatenate(found, axis=1)
+
+    each_rows(heads)
+    total = mm_nt(mixed[0], wv[0, :, 3 * n :]) + mm_nt(mixed[1], wv[1, :, 3 * n :])
+    part[...] = total.astype(LOW)
+
+
+def cross_backward(
+    cot, n3, codec, cq, ckv, mixed, logs, w, d, part, wv, gm, dq, dkv, sems
+):
+    n = mixed.shape[2]
+    copies = start_copies([(w.at[0], wv.at[0]), (w.at[1], wv.at[1])], sems)
+    for i in (1, 0):
+        d[i, :, 3 * n :] = mm_tn(cot[...], mixed[i]).astype(LOW)
+    for i in range(2):
+        copies[i].wait()
+        gm[i] = mm(cot[...], wv[i, :, 3 * n :]).astype(LOW)
+    dkv[...] = jnp.zeros(dkv.shape, F32)
+
+    def heads(r):
+        for i in range(2):
+            per = n // HD
+            rows_logs = [logs[r, per * i + h : per * i + h + 1] for h in range(per)]
+            gq, gk, gv = softmax_heads_back(
+                cq[i, r, :], ckv[i, :, :n], ckv[i, :, n:], gm[i, r, :], rows_logs,
+                per, HD ** (-0.5), None,
+            )
+            dq[i, r, :] = gq.astype(LOW)
+            dkv[i] += jnp.concatenate([gk, gv], axis=1)
+
+    each_rows(heads)
+    total = None
+    for i in (1, 0):
+        low_kv = jnp.concatenate(
+            [dkv[i, :, :n] * (HD ** (-0.5)), dkv[i, :, n:]], axis=1
+        ).astype(LOW)
+        d[i, :, :n] = mm_tn(n3[...], dq[i]).astype(LOW)
+        d[i, :, n : 3 * n] = mm_tn(codec[...], low_kv).astype(LOW)
+        term = mm_nt(dq[i], wv[i, :, :n])
+        total = term if total is None else total + term
+    part[...] = total.astype(LOW)
+
+
+def conv_two_backward(
+    resid, own, other, cot, norms, side, conv, taps, u,
+    grad3, d, tapsg, ln_rows, gn_rows, gsum, pad, gl, uv, sems,
+):
+    n = conv.shape[2]
+    width = resid.shape[1] // GROUPS
+    mats_n = group_mats(n, width)
+    copies = start_copies([(u.at[0], uv.at[0]), (u.at[1], uv.at[1])], sems)
+    pad[0:TIME, :] = jnp.zeros((TIME, pad.shape[1]), LOW)
+    pad[TIME + ROWS :, :] = jnp.zeros((TIME, pad.shape[1]), LOW)
+    ln_rows[...] = jnp.zeros(ln_rows.shape, F32)
+
+    def pull(r):
+        g = own[r, :].astype(F32) + other[r, :].astype(F32)
+        back, gain, shift = ln_back(resid[r, :], norms[8:9, :], g)
+        v = cot[r, :].astype(F32) + back
+        grad3[r, :] = v
+        gl[r, :] = v.astype(LOW)
+        ln_rows[0:1, :] += gain
+        ln_rows[1:2, :] += shift
+
+    each_rows(pull)
+    pad[TIME : TIME + ROWS, :] = gl[...]
+    for i in (1, 0):
+        for a in range(3):
+            d[i, :, 3 * n * a : 3 * n * (a + 1)] = mm_tn(
+                gl[...], taps[i, TIME * a : TIME * a + ROWS, :]
+            ).astype(LOW)
+    for i in range(2):
+        copies[i].wait()
+        q = None
+        for a in range(3):
+            term = mm(
+                pad[TIME * (2 - a) : TIME * (2 - a) + ROWS, :],
+                uv[i, :, 3 * n * a : 3 * n * (a + 1)],
+            )
+            q = term if q is None else q + term
+        grad = from_right(q[:, :n]) + q[:, n : 2 * n] + from_left(q[:, 2 * n :])
+        c1 = conv[i]
+        c1 = c1 - group_average(jnp.sum(c1, axis=0, keepdims=True), mats_n, width)
+        var_n = group_average(jnp.sum(c1 * c1, axis=0, keepdims=True), mats_n, width)
+        scale = lax.rsqrt(var_n + NORM_EPS)
+        hat = c1 * scale
+        gain = side[i, 0:1, :]
+        pre = hat * gain + side[i, 1:2, :]
+        gate = jax.nn.sigmoid(pre)
+        grad = grad * gate * (1.0 + pre * (1.0 - gate))
+        d_gain = jnp.sum(grad * hat, axis=0, keepdims=True)
+        d_shift = jnp.sum(grad, axis=0, keepdims=True)
+        gn_rows[i] = jnp.concatenate([d_gain, d_shift], axis=0)
+        back = scale * (
+            grad * gain
+            - group_average(d_shift * gain, mats_n, width)
+            - hat * group_average(d_gain * gain, mats_n, width)
+        )
+        back = back.astype(LOW).astype(F32)
+        gsum[i : i + 1, :] = jnp.sum(back, axis=0, keepdims=True)
+        tapsg[i, 0:TIME, :] = jnp.zeros((TIME, 3 * n), LOW)
+        tapsg[i, TIME + ROWS :, :] = jnp.zeros((TIME, 3 * n), LOW)
+        tapsg[i, TIME : TIME + ROWS, :] = jnp.concatenate(
+            [from_right(back), back, from_left(back)], axis=1
+        ).astype(LOW)
+
+
+def conv_one_backward(first, tapsg, gsum, embed_col, w, d, part, wv, sems):
+    n = gsum.shape[1]
+    copies = start_copies([(w.at[0], wv.at[0]), (w.at[1], wv.at[1])], sems)
+    for i in (1, 0):
+        for a in range(3):
+            d[i, :, 3 * n * a : 3 * n * (a + 1)] = mm_tn(
+                first[...], tapsg[i, TIME * (2 - a) : TIME * (2 - a) + ROWS, :]
+            ).astype(LOW)
+        d[i, :, 9 * n :] = (embed_col[...] * gsum[i : i + 1, :]).astype(LOW)
+    total = None
+    for i in range(2):
+        copies[i].wait()
+        for a in range(3):
+            term = mm_nt(
+                tapsg[i, TIME * (2 - a) : TIME * (2 - a) + ROWS, :],
+                wv[i, :, 3 * n * a : 3 * n * (a + 1)],
+            )
+            total = term if total is None else total + term
+    part[...] = total.astype(LOW)
+
+
+def mlp_backward(
+    noisy, own, other, grad3, norms, n2, w, grad2, d, part, gn_rows, wv, gl, hb, acc, sems
+):
+    hid = wv.shape[2] // 2
+    width = noisy.shape[1] // GROUPS
+    mats = group_mats(noisy.shape[1], width)
+    copies = start_copies([(w.at[0], wv.at[0]), (w.at[1], wv.at[1])], sems)
+    mean = group_average(jnp.sum(noisy[...], axis=0, keepdims=True), mats, width)
+    centre = noisy[...] - mean
+    var = group_average(jnp.sum(centre * centre, axis=0, keepdims=True), mats, width)
+    scale = lax.rsqrt(var + NORM_EPS)
+    gain, shift = norms[4:5, :], norms[5:6, :]
+    gn_rows[...] = jnp.zeros(gn_rows.shape, F32)
+
+    def through_silu(r):
+        hat = (noisy[r, :] - mean) * scale
+        pre = hat * gain + shift
+        gate = jax.nn.sigmoid(pre)
+        g = own[r, :].astype(F32) + other[r, :].astype(F32)
+        g = g * gate * (1.0 + pre * (1.0 - gate))
+        acc[r, :] = g
+        gn_rows[0:1, :] += jnp.sum(g * hat, axis=0, keepdims=True)
+        gn_rows[1:2, :] += jnp.sum(g, axis=0, keepdims=True)
+
+    each_rows(through_silu)
+    mean_shift = group_average(gn_rows[1:2, :] * gain, mats, width)
+    mean_gain = group_average(gn_rows[0:1, :] * gain, mats, width)
+
+    def pull(r):
+        hat = (noisy[r, :] - mean) * scale
+        v = grad3[r, :] + scale * (acc[r, :] * gain - mean_shift - hat * mean_gain)
+        grad2[r, :] = v
+        gl[r, :] = v.astype(LOW)
+
+    each_rows(pull)
+    block = 256
+    started = False
+    copies[0].wait()
+    copies[1].wait()
+    for i in (1, 0):
+        for b in range(hid // block):
+            up = slice(block * b, block * (b + 1))
+            down = slice(hid + block * b, hid + block * (b + 1))
+            pre = mm(n2[...], wv[i, :, up])
+            t, hidden = gelu_parts(pre)
+            slope = gelu_slope(pre, t)
+            d[i, :, down] = mm_tn(gl[...], hidden.astype(LOW)).astype(LOW)
+            hb[...] = (mm(gl[...], wv[i, :, down]) * slope).astype(LOW)
+            d[i, :, up] = mm_tn(n2[...], hb[...]).astype(LOW)
+            term = mm_nt(hb[...], wv[i, :, up])
+            if started:
+                acc[...] += term
+            else:
+                acc[...] = term
+                started = True
+    part[...] = acc[...].astype(LOW)
+
+
+def attn_backward(
+    seg_col, seg_row, resid, own, other, grad2, norms, n1, qkv, mixed, logs, w,
+    grad1, d, part, ln_rows, wv, gl, gm, dqkv, dkv, sems,
+):
+    n = mixed.shape[2]
+    copies = start_copies([(w.at[0], wv.at[0]), (w.at[1], wv.at[1])], sems)
+    ln_rows[...] = jnp.zeros(ln_rows.shape, F32)
+
+    def pull(r):
+        g = own[r, :].astype(F32) + other[r, :].astype(F32)
+        back, gain, shift = ln_back(resid[r, :], norms[2:3, :], g)
+        v = grad2[r, :] + back
+        grad1[r, :] = v
+        gl[r, :] = v.astype(LOW)
+        ln_rows[0:1, :] += gain
+        ln_rows[1:2, :] += shift
+
+    each_rows(pull)
+    for i in range(2):
+        d[i, :, 3 * n :] = mm_tn(gl[...], mixed[i]).astype(LOW)
+        copies[i].wait()
+        gm[i] = mm(gl[...], wv[i, :, 3 * n :]).astype(LOW)
+    dkv[...] = jnp.zeros(dkv.shape, F32)
+
+    def heads(r):
+        mask = seg_col[r, :] == seg_row[...]
+        for i in range(2):
+            per = n // HD
+            rows_logs = [logs[r, per * i + h : per * i + h + 1] for h in range(per)]
+            gq, gk, gv = softmax_heads_back(
+                qkv[i, r, :n], qkv[i, :, n : 2 * n], qkv[i, :, 2 * n :], gm[i, r, :], rows_logs,
+                per, HD ** (-0.5), mask,
+            )
+            dqkv[i, r, :n] = gq.astype(LOW)
+            dkv[i] += jnp.concatenate([gk, gv], axis=1)
+
+    each_rows(heads)
+    total = None
+    for i in (1, 0):
+        dqkv[i, :, n:] = jnp.concatenate(
+            [dkv[i, :, :n] * (HD ** (-0.5)), dkv[i, :, n:]], axis=1
+        ).astype(LOW)
+        d[i, :, : 3 * n] = mm_tn(n1[...], dqkv[i]).astype(LOW)
+        term = mm_nt(dqkv[i], wv[i, :, : 3 * n])
+        total = term if total is None else total + term
+    part[...] = total.astype(LOW)
+
+
+def input_backward(tok, own, other, grad1, norms, grad_x, ln_rows):
+    ln_rows[...] = jnp.zeros(ln_rows.shape, F32)
+
+    def pull(r):
+        g = own[r, :].astype(F32) + other[r, :].astype(F32)
+        back, gain, shift = ln_back(tok[r, :].astype(F32), norms[0:1, :], g)
+        grad_x[r, :] = (grad1[r, :] + back).astype(LOW)
+        ln_rows[0:1, :] += gain
+        ln_rows[1:2, :] += shift
+
+    each_rows(pull)
+
+
+MESH_IDS = pl.DeviceIdType.MESH
+
+
+def place():
+    mp = lax.axis_index("mp")
+    dp = lax.axis_index("dp")
+    return mp // 2, mp % 2, dp // 2, dp % 2
+
+
+def device(x, core, z, y):
+    return (2 * z + y, 2 * x + core)
+
+
+def meet(peers):
+    barrier = pltpu.get_barrier_semaphore()
+    for peer in peers:
+        pl.semaphore_signal(barrier, inc=1, device_id=peer, device_id_type=MESH_IDS)
+    pl.semaphore_wait(barrier, len(peers))
+
+
+def chip_peers():
+    x, core, z, y = place()
+    along_z = [device(x, core, (z + k) % 4, y) for k in range(1, 4)]
+    return device(1 - x, core, z, y), device(x, core, z, 1 - y), along_z
+
+
+class Sender:
+    def __init__(self, send, recv):
+        self.send, self.recv, self.used = send, recv, 0
+
+    def start(self, src, dst, peer):
+        k = self.used
+        self.used += 1
+        copy = pltpu.make_async_remote_copy(
+            src_ref=src, dst_ref=dst, send_sem=self.send.at[k], recv_sem=self.recv.at[k],
+            device_id=peer, device_id_type=MESH_IDS,
+        )
+        copy.start()
+        return copy
+
+
+def gather_body(count, *refs):
+    pieces, outs, (own_sem, send, recv) = refs[:count], refs[count : 2 * count], refs[2 * count :]
+    x, core, z, y = place()
+    to_x, to_y, to_z = chip_peers()
+    net = Sender(send, recv)
+    local = [
+        pltpu.make_async_copy(pieces[g], outs[g].at[0, z, y], own_sem.at[g]) for g in range(count)
+    ]
+    for c in local:
+        c.start()
+    meet([to_x, to_y, *to_z])
+
+    def send_line(g):
+        return [net.start(pieces[g], outs[g].at[0, z, y], peer) for peer in to_z]
+
+    def send_planes(g):
+        line = outs[g].at[0, :, y]
+        return (
+            net.start(line, outs[g].at[1, :, y], to_x),
+            net.start(line, outs[g].at[0, :, y], to_y),
+        )
+
+    def send_corners(g):
+        return (
+            net.start(outs[g].at[0, 0:2, 1 - y], outs[g].at[1, 0:2, 1 - y], to_x),
+            net.start(outs[g].at[1, 2:4, y], outs[g].at[1, 2:4, y], to_y),
+        )
+
+    last = count - 1
+    src = pieces[last]
+    lines = {0: send_line(0)}
+    early_x = net.start(src, outs[last].at[1, z, y], to_x)
+    early_y = net.start(src, outs[last].at[0, z, y], to_y)
+    planes, corners, done = {}, {}, [early_x, early_y]
+    for g in range(last):
+        for c in lines[g]:
+            c.wait_recv()
+        local[g].wait()
+        planes[g] = send_planes(g)
+        if g + 1 < last:
+            lines[g + 1] = send_line(g + 1)
+        if g == 0:
+            early_x.wait_recv()
+            late = net.start(outs[last].at[1, z, y], outs[last].at[1, z, y], to_y)
+        if g == 1:
+            early_y.wait_recv()
+            late.wait_recv()
+            local[last].wait()
+            block = outs[last].at[:, z]
+            far = [net.start(block, outs[last].at[:, z], peer) for peer in to_z]
+        if g >= 1:
+            for c in planes[g - 1]:
+                c.wait_recv()
+            corners[g - 1] = send_corners(g - 1)
+    for c in planes[last - 1]:
+        c.wait_recv()
+    corners[last - 1] = send_corners(last - 1)
+    for g in range(last):
+        for c in corners[g]:
+            c.wait_recv()
+    for c in far:
+        c.wait_recv()
+    for c in [*done, late, *far]:
+        c.wait_send()
+    for g in range(last):
+        for c in [*lines[g], *planes[g], *corners[g]]:
+            c.wait_send()
+
+
+def gather_all(pieces):
+    count = len(pieces)
+    copies = (count - 1) * 7 + 6
+    return pl.pallas_call(
+        partial(gather_body, count),
+        name="gather_weights",
+        in_specs=[spec_any() for _ in pieces],
+        out_specs=[spec_any() for _ in pieces],
+        out_shape=[jax.ShapeDtypeStruct((2, 4, 2, *p.shape), LOW) for p in pieces],
+        scratch_shapes=[
+            pltpu.SemaphoreType.DMA((count,)), pltpu.SemaphoreType.DMA((copies,)),
+            pltpu.SemaphoreType.DMA((copies,)),
+        ],
+        compiler_params=pltpu.CompilerParams(collective_id=0, has_side_effects=True),
+    )(*pieces)
+
+
+def add_rows(target, terms, step=16):
+    def body(k, carry):
+        r = pl.ds(pl.multiple_of(k * step, step), step)
+        total = terms[0][r, :].astype(F32)
+        for t in terms[1:]:
+            total = total + t[r, :].astype(F32)
+        target[r, :] = total.astype(target.dtype)
+        return carry
+
+    lax.fori_loop(0, target.shape[0] // step, body, 0)
+
+
+def scatter_body(count, *refs):
+    last = count - 1
+    grads, outs, refs = refs[:count], refs[count : 2 * count], refs[2 * count :]
+    bufs, refs = refs[: 5 * last], refs[5 * last :]
+    far_buf, mid_buf, side_buf, send, recv = refs
+    x, core, z, y = place()
+    to_x, to_y, to_z = chip_peers()
+    net = Sender(send, recv)
+    meet([to_x, to_y, *to_z])
+    far = [
+        net.start(grads[last].at[:, (z + k) % 4], far_buf.at[k - 1], to_z[k - 1])
+        for k in range(1, 4)
+    ]
+    first, second, ends = {}, {}, {}
+    order = list(range(last))[::-1]
+
+    def send_raw(g):
+        cx, cy, lx, ly = bufs[5 * g : 5 * g + 4]
+        first[g] = (
+            net.start(grads[g].at[1, 0:2, 1 - y], cx, to_x),
+            net.start(grads[g].at[1, 2:4, 1 - y], cy, to_y),
+            net.start(grads[g].at[1, 0:2, y], lx.at[0:2], to_x),
+            net.start(grads[g].at[0, 2:4, 1 - y], ly.at[2:4], to_y),
+        )
+
+    def fold_corners(g):
+        cx, cy, lx, ly = bufs[5 * g : 5 * g + 4]
+        first[g][0].wait_recv()
+        for k in range(2):
+            add_rows(cx.at[k], [cx.at[k], grads[g].at[0, k, 1 - y]])
+        to_line = net.start(cx, ly.at[0:2], to_y)
+        first[g][1].wait_recv()
+        for k in range(2):
+            add_rows(cy.at[k], [cy.at[k], grads[g].at[1, 2 + k, y]])
+        second[g] = (to_line, net.start(cy, lx.at[2:4], to_x))
+
+    def fold_lines(g):
+        lx, ly, zb = bufs[5 * g + 2 : 5 * g + 5]
+        for c in (first[g][2], first[g][3], *second[g]):
+            c.wait_recv()
+        for k in range(4):
+            add_rows(lx.at[k], [lx.at[k], ly.at[k], grads[g].at[0, k, y]])
+        ends[g] = [
+            net.start(lx.at[(z + k) % 4], zb.at[k - 1], to_z[k - 1]) for k in range(1, 4)
+        ]
+
+    def finish_group(g):
+        lx, zb = bufs[5 * g + 2], bufs[5 * g + 4]
+        for c in ends[g]:
+            c.wait_recv()
+        add_rows(outs[g], [lx.at[z], zb.at[0], zb.at[1], zb.at[2]])
+
+    send_raw(order[0])
+    for c in far:
+        c.wait_recv()
+    for i in range(2):
+        for j in range(2):
+            add_rows(
+                mid_buf.at[i, j], [grads[last].at[i, z, j], *(far_buf.at[k, i, j] for k in range(3))]
+            )
+    half = net.start(mid_buf.at[:, 1 - y], side_buf.at[0:2], to_y)
+    for pos, g in enumerate(order):
+        fold_corners(g)
+        if pos + 1 < last:
+            send_raw(order[pos + 1])
+        if pos == 0:
+            half.wait_recv()
+            for i in (1, 0):
+                add_rows(mid_buf.at[i, y], [mid_buf.at[i, y], side_buf.at[i]])
+            tail = net.start(mid_buf.at[1, y], side_buf.at[2], to_x)
+        fold_lines(g)
+        if pos >= 1:
+            finish_group(order[pos - 1])
+    tail.wait_recv()
+    add_rows(outs[last], [mid_buf.at[0, y], side_buf.at[2]])
+    finish_group(order[-1])
+    for c in [*far, half, tail]:
+        c.wait_send()
+    for g in range(last):
+        for c in [*first[g], *second[g], *ends[g]]:
+            c.wait_send()
+
+
+def scatter_all(grads):
+    count = len(grads)
+    rows = grads[0].shape[3]
+    widths = [g.shape[4] for g in grads]
+    copies = (count - 1) * 9 + 5
+    scratch = []
+    for w in widths[:-1]:
+        scratch += [VM((k, rows, w), LOW) for k in (2, 2, 4, 4, 3)]
+    w = widths[-1]
+    scratch += [VM((3, 2, 2, rows, w), LOW), VM((2, 2, rows, w), LOW), VM((3, rows, w), LOW)]
+    return pl.pallas_call(
+        partial(scatter_body, count),
+        name="scatter_grads",
+        in_specs=[spec_vm() for _ in grads],
+        out_specs=[spec_vm() for _ in grads],
+        out_shape=[jax.ShapeDtypeStruct((rows, w), F32) for w in widths],
+        scratch_shapes=[
+            *scratch, pltpu.SemaphoreType.DMA((copies,)), pltpu.SemaphoreType.DMA((copies,)),
+        ],
+        compiler_params=pltpu.CompilerParams(
+            collective_id=1, has_side_effects=True, vmem_limit_bytes=60 << 20
+        ),
+    )(*grads)
+
+
+def fast_device(
+    tokens,
+    noise_field,
+    codec_tokens,
+    timesteps,
+    segments,
+    cotangent,
+    w_in,
+    w_back,
+    w_up,
+    w_down,
+    m_in,
+    m_back,
+    m_up,
+    m_down,
+    v_in,
+    v_back,
+    v_up,
+    v_down,
+    norm_params,
+    norm_m,
+    norm_v,
+):
+    length = segments.shape[1]
+    features = tokens.shape[1]
+    n = w_in.shape[2]
+    hid = w_up.shape[1]
+    heads = 2 * n // HD
+    mp = lax.axis_index("mp")
+    dp = lax.axis_index("dp")
+    x, core, z, y = mp // 2, mp % 2, dp // 2, dp % 2
+    lead = (core == 0).astype(F32)
+    slices = [2 * x + core, 2 * (1 - x) + core]
+
+    low_in = w_in.astype(LOW).transpose(1, 0, 2).reshape(w_in.shape[1], -1)
+    low_back = w_back.astype(LOW).transpose(2, 0, 1).reshape(w_back.shape[2], -1)
+    low_up = w_up.astype(LOW)
+    low_down = w_down.astype(LOW).T
+    piece_attn = jnp.concatenate([low_in[:, : 3 * n], low_back[:, :n]], axis=1)
+    piece_mlp = jnp.concatenate([low_up, low_down], axis=1)
+    piece_one = jnp.concatenate([low_in[:, 7 * n :], low_in[:, 3 * n : 4 * n]], axis=1)
+    piece_two = low_back[:, 2 * n :]
+    piece_cross = jnp.concatenate([low_in[:, 4 * n : 7 * n], low_back[:, n : 2 * n]], axis=1)
+    gathered = gather_all([piece_attn, piece_mlp, piece_one, piece_two, piece_cross])
+    w_attn, w_mlp, w_one, w_two, w_cross = [
+        w.reshape(2, features, -1) for w in gathered
+    ]
+    weight_sq = matrix_squares(w_in, w_back, w_up, w_down)
+
+    def own_rows(v):
+        return lax.dynamic_slice_in_dim(v, x * length, length, 0)
+
+    tok = own_rows(tokens)
+    noise = own_rows(noise_field)
+    cot = own_rows(cotangent)
+    codec = pick(codec_tokens, x, 0)
+    step = pick(timesteps, x, 0)
+    seg = pick(segments, x, 0)
+    seg_col, seg_row = seg[:, None], seg[None, :]
+    noise_level = jnp.sqrt((step.astype(F32) + 1.0) / TSTEPS).reshape(1, 1)
+    embed = jax.nn.silu(time_embedding(step[None], features)).astype(LOW)
+    embed_rows = jnp.broadcast_to(embed, (8, features))
+    embed_col = embed.astype(F32).reshape(features, 1)
+    side = jnp.stack(
+        [lax.dynamic_slice(norm_params, (6, s * n), (2, n)) for s in slices]
+    )
+    full = (length, features)
+    square = (features, 4 * n)
+    sem = pltpu.SemaphoreType.DMA
+    norms = norm_params
+
+    n1, qkv, mixed, logs, part = run_kernel(
+        attn_forward, "attn_forward",
+        [seg_col, seg_row, tok, norms, w_attn],
+        [(full, LOW), ((2, length, 3 * n), LOW), ((2, length, n), LOW), ((length, heads), F32), (full, LOW)],
+        [VM((2, *square), LOW), sem((2,))], hbm=(4,), flops=4 * 10**9,
+    )
+    resid_one, n2, part_two = run_kernel(
+        mlp_forward, "mlp_forward",
+        [tok, part, swap_core(part), norms, w_mlp],
+        [(full, F32), (full, LOW), (full, LOW)],
+        [VM((2, features, 2 * hid), LOW), VM(full, F32), sem((2,))], hbm=(4,), flops=3 * 10**9,
+    )
+    tall = length + 2 * TIME
+    noisy, first, conv, taps, part = run_kernel(
+        conv_forward, "conv_forward",
+        [noise_level, resid_one, part_two, swap_core(part_two), noise, norms, side, embed_rows, w_one, w_two],
+        [(full, F32), (full, LOW), ((2, length, n), F32), ((2, tall, 3 * n), LOW), (full, LOW)],
+        [
+            VM((tall, features), LOW), VM((2, features, 10 * n), LOW), VM((2, features, 9 * n), LOW),
+            sem((4,)),
+        ],
+        hbm=(8, 9), flops=7 * 10**9,
+    )
+    resid_three, n3, cq, ckv, cross, logs_c, part = run_kernel(
+        cross_forward, "cross_forward",
+        [noisy, part, swap_core(part), codec, norms, w_cross],
+        [
+            (full, F32), (full, LOW), ((2, length, n), LOW), ((2, codec.shape[0], 2 * n), LOW),
+            ((2, length, n), LOW), ((length, heads), F32), (full, LOW),
+        ],
+        [VM((2, *square), LOW), sem((2,))], hbm=(5,), flops=2 * 10**9,
+    )
+    result = resid_three + (part.astype(F32) + swap_core(part).astype(F32))
+    out_low = result.astype(LOW)
+    out_rows = by_parity(x, out_low, swap_x(out_low), 0).reshape(-1, features)
+
+    d, part = run_kernel(
+        cross_backward, "cross_backward",
+        [cot, n3, codec, cq, ckv, cross, logs_c, w_cross],
+        [((2, *square), LOW), (full, LOW)],
+        [
+            VM((2, *square), LOW), VM((2, length, n), LOW), VM((2, length, n), LOW),
+            VM((2, codec.shape[0], 2 * n), F32), sem((2,)),
+        ],
+        hbm=(7,), flops=4 * 10**9,
+    )
+    d_cross = d
+    wide = (features, 9 * n)
+    grad_three, d, tapsg, ln_eight, gn_six, gsum = run_kernel(
+        conv_two_backward, "conv_two_backward",
+        [resid_three, part, swap_core(part), cot, norms, side, conv, taps, w_two],
+        [
+            (full, F32), ((2, *wide), LOW), ((2, tall, 3 * n), LOW), ((2, features), F32),
+            ((2, 2, n), F32), ((2, n), F32),
+        ],
+        [VM((tall, features), LOW), VM(full, LOW), VM((2, *wide), LOW), sem((2,))],
+        hbm=(8,), flops=6 * 10**9,
+    )
+    d_two = d
+    wider = (features, 10 * n)
+    d, part = run_kernel(
+        conv_one_backward, "conv_one_backward",
+        [first, tapsg, gsum, embed_col, w_one],
+        [((2, *wider), LOW), (full, LOW)],
+        [VM((2, *wider), LOW), sem((2,))], hbm=(4,), flops=6 * 10**9,
+    )
+    d_one = d
+    double = (features, 2 * hid)
+    grad_two, d, part, gn_four = run_kernel(
+        mlp_backward, "mlp_backward",
+        [noisy, part, swap_core(part), grad_three, norms, n2, w_mlp],
+        [(full, F32), ((2, *double), LOW), (full, LOW), ((2, features), F32)],
+        [VM((2, *double), LOW), VM(full, LOW), VM((length, 256), LOW), VM(full, F32), sem((2,))],
+        hbm=(6,), flops=7 * 10**9,
+    )
+    d_mlp = d
+    grad_one, d, part, ln_two = run_kernel(
+        attn_backward, "attn_backward",
+        [seg_col, seg_row, resid_one, part, swap_core(part), grad_two, norms, n1, qkv, mixed, logs, w_attn],
+        [(full, F32), ((2, *square), LOW), (full, LOW), ((2, features), F32)],
+        [
+            VM((2, *square), LOW), VM(full, LOW), VM((2, length, n), LOW), VM((2, length, 3 * n), LOW),
+            VM((2, length, 2 * n), F32), sem((2,)),
+        ],
+        hbm=(11,), flops=8 * 10**9,
+    )
+    d_attn = d
+    grad_x, ln_zero = run_kernel(
+        input_backward, "input_backward",
+        [tok, part, swap_core(part), grad_one, norms],
+        [(full, LOW), ((2, features), F32)], [],
+    )
+    sums = scatter_all(
+        [v.reshape(2, 4, 2, -1, v.shape[2]) for v in (d_attn, d_mlp, d_one, d_two, d_cross)]
+    )
+    sum_attn, sum_mlp, sum_one, sum_two, sum_cross = sums
+    half = length // 2
+    mine = lax.dynamic_slice_in_dim(grad_x, core * half, half, 0)
+    got = swap_x(mine)
+    other_x = by_parity(core, got, swap_core(got), 0).reshape(length, features)
+    grad_rows = by_parity(x, grad_x, other_x, 0).reshape(-1, features).astype(F32)
+
+    def unpack_in(v):
+        return v.reshape(v.shape[0], -1, n).transpose(1, 0, 2)
+
+    def unpack_back(v):
+        return v.reshape(v.shape[0], -1, n).transpose(1, 2, 0)
+
+    summed_in = unpack_in(
+        jnp.concatenate(
+            [sum_attn[:, : 3 * n], sum_one[:, 9 * n :], sum_cross[:, : 3 * n], sum_one[:, : 9 * n]],
+            axis=1,
+        )
+    )
+    summed_back = unpack_back(
+        jnp.concatenate([sum_attn[:, 3 * n :], sum_cross[:, 3 * n :], sum_two], axis=1)
+    )
+    summed_up = sum_mlp[:, :hid]
+    summed_down = sum_mlp[:, hid:].T
+
+    group_rows = jnp.zeros((2, features), F32)
+    for i, s in enumerate(slices):
+        group_rows = lax.dynamic_update_slice(group_rows, gn_six[i], (0, s * n))
+    norm_grad = lax.psum(
+        jnp.concatenate(
+            [ln_zero * lead, ln_two * lead, gn_four * lead, group_rows, ln_eight * lead]
+        ),
+        ("dp", "mp"),
+    )
+    return finish(
+        out_rows, grad_rows, weight_sq, (summed_in, summed_back, summed_up, summed_down),
+        (w_in, w_back, w_up, w_down), (m_in, m_back, m_up, m_down), (v_in, v_back, v_up, v_down),
+        norm_grad, norm_params, norm_m, norm_v,
+    )
+
+
+def finish(out_rows, grad_rows, weight_sq, grads, masters, moments, squares, norm_grad, norm_params, norm_m, norm_v):
+    stepped = [
+        adam_update(w, g, m, v, WEIGHT_DECAY)
+        for w, g, m, v in zip(masters, grads, moments, squares)
+    ]
+    new_m = [s[0] for s in stepped]
+    new_v = [s[1] for s in stepped]
+    updates = [s[2] for s in stepped]
+    update_sq = matrix_squares(*updates)
+    weight_total, update_total = lax.psum((weight_sq, update_sq), ("dp", "mp"))
+    weight_len = jnp.sqrt(weight_total)
+    update_len = jnp.sqrt(update_total)
+    trust = LEARN_RATE * (weight_len / update_len)
+    scales = (trust[0:16, None, None], trust[16:27, None, None], trust[27], trust[28])
+    new_w = [w - s * u for w, s, u in zip(masters, scales, updates)]
+    norm_m_new, norm_v_new, upd_norm = adam_update(norm_params, norm_grad, norm_m, norm_v, 0.0)
+    row_trust = jnp.sqrt(jnp.sum(norm_params * norm_params, axis=1)) / jnp.sqrt(
+        jnp.sum(upd_norm * upd_norm, axis=1)
+    )
+    new_norm = norm_params - LEARN_RATE * row_trust[:, None] * upd_norm
+    return (
+        out_rows, grad_rows, *new_w, *new_m, *new_v, new_norm, norm_m_new, norm_v_new,
+        jnp.stack([weight_len, update_len]),
+    )
+
+
 def solution(mesh):
+    per_device = fast_device if dict(mesh.shape) == {"dp": 8, "mp": 4} else generic_device
     placed = (
         P("dp", None),
         P("dp", None),

time: 1580 us -> 718 us (0.45)
  waiting for transfers between devices: 974 us -> 4.92 us
  Pallas kernels: 0 us -> 570 us
  local copies, waits for them, and re-layouts: 262 us -> 39.4 us
  matrix products: 148 us -> 0 us
  other arithmetic: 130 us -> 39 us
  between operations: 18.4 us -> 2.26 us
    pallas_call x0 -> x12, Pallas kernels: none -> 570 us  [the longest x1 211 us: gather_all(): pl.pallas_call(partial(gather_body, count), name='gather_weights', in_spe...]
    psum x7 -> x0, waiting for transfers between devices: 328 us -> none  [tensor_parallel_sum(): return lax.psum(term_rows, 'mp')]
    unnamed x17 -> x0, waiting for transfers between devices: 275 us -> none
    all_gather x4 -> x0, waiting for transfers between devices: 244 us -> none  [the longest x1 92.9 us: per_device(): lax.all_gather(w_back.astype(jnp.bfloat16), 'dp', axis=2, tiled=True)]
    unnamed x513 -> x98, local copies, waits for them, and re-layouts: 176 us -> 8.05 us
    dot_general x96 -> x0, matrix products: 148 us -> none  [the longest x10 26.2 us: weight_grad(): jnp.einsum('nc,ne->ce', flatten_rows(left_low), flatten_rows(right_low),...]
    reduce_scatter x2 -> x0, waiting for transfers between devices: 127 us -> none  [the longest x1 69.6 us: per_device(): lax.psum_scatter(grad_w_down, 'dp', scatter_dimension=1, tiled=True)]
    reduce_sum x28 -> x1, other arithmetic: 58.5 us -> 1.03 us  [finish(): jnp.sum(norm_params * norm_params, axis=1)]
  transfers between devices with their start and end apart: 15 -> 11, of which waited for: 14 -> 4; matrix products, arithmetic and copies ran while one was open for 17% -> 6% of each run, Pallas kernels for 0% -> 8%
where the time goes in v2:
time: 718 us; the launch traced here: 708 us
  Pallas kernels  570 us (79%)
  blocking collectives  46.3 us (6%)
  local copies, waits for them, and re-layouts  39.4 us (5%)
  other arithmetic  39 us (5%)
    pallas_call x1, Pallas kernels, gather_all(): pl.pallas_call(partial(gather_body, count), name='gather_weights', in_spe...  211 us
    pallas_call x1, Pallas kernels, scatter_all(): pl.pallas_call(partial(scatter_body, count), name='scatter_grads', in_spe...  207 us
    pallas_call x10, Pallas kernels, run_kernel(): pl.pallas_call(body, name=name, in_specs=in_specs, out_specs=[spec_vm() f...  153 us
    psum x1, blocking collectives, finish(): weight_total, update_total = lax.psum((weight_sq, update_sq), ('dp', 'mp'))  46.3 us
  transfers between devices with their start and end apart: 11, of which 4 were waited for; matrix products, arithmetic and copies ran while one was open for 6% of the time, Pallas kernels for 8%

profile of v2, /device:TPU:0, one launch (start us, length us, event | category | flops | bytes accessed | tf_op | source)
XLA Modules:
  0.0 707.9 jit_solution(6551386082491747610)
XLA Ops:
  0.7 0.8 fusion.15
  1.5 1.3 constant_dynamic-slice_fusion.3.seg_row
  2.8 1.5 convert_bitcast_fusion
  4.7 1.6 reshape.221
  6.4 1.7 fusion.12
  8.0 1.9 slice.86
  9.9 1.6 slice.87
  11.6 0.8 slice.88
  12.4 0.9 copy.68.seg_col
  14.7 1.9 copy.74.refs_3_
  16.8 1.0 constant_dynamic-slice_fusion.4.tok
  17.9 0.8 pad_maximum_fusion.3.refs_2_
  19.4 0.8 pad_maximum_fusion.5
  20.2 211.0 %gather_weights.1 = (bf16[2,4,2,96,768]{4,3,2,1,0:T(8,128)(2,1)}, bf16[2,4,2,96,1536]{4,3,2,1,0:T(8,128)(2,1)}, bf16[2,4,2,96,1920]{4,3,2,1,0:T(8,128)(2,1)}, bf...) custom-call(bf16[96,768]{1,0:T(8,128)(2,1)} %get-tuple-element.160.refs_0_, ...), custom_call_target="tpu_custom_call" | custom-call | tf_op jit(solution)/shard_map/gather_weights/pallas_call | solution.py:1099
  231.3 15.6 %attn_forward.1 = (bf16[512,768]{1,0:T(8,128)(2,1)}, bf16[2,512,576]{2,1,0:T(8,128)(2,1)}, bf16[2,512,192]{2,1,0:T(8,128)(2,1)}, f32[512,6]{1,0:T(8,128)}, bf16[512,768]{1,0:T(8,128)(2,1)}) custom-call(s32[512,1]{1,0:T(8,128)} %copy.68.seg_col, s32[1,512]{1,0:T(1,128)} %constant_dynamic-slice_fusion.3.seg_row, ...), custom_call_target="tpu_custom_call" | custom-call | flops 4000000000 | bytes 6338560 | tf_op jit(solution)/shard_map/attn_forward/pallas_call | solution.py:495
  247.0 2.5 collective-permute-done.other
  249.5 0.9 copy-done.45
  250.4 7.9 %mlp_forward.1 = (f32[512,768]{1,0:T(8,128)}, bf16[512,768]{1,0:T(8,128)(2,1)}, bf16[512,768]{1,0:T(8,128)(2,1)}) custom-call(bf16[512,768]{1,0:T(8,128)(2,1)} %constant_dynamic-slice_fusion.4.tok, bf16[512,768]{1,0:T(8,128)(2,1)} %get-tuple-element.69.own, bf16[512,768]{1,0:T(8,128)(2,1)} %copy-done.45, f32[10,768]{1,0:T(8,128)} %norms.15, ...), custom_call_target="tpu_custom_call" | custom-call | flops 3000000000 | bytes 10254336 | tf_op jit(solution)/shard_map/mlp_forward/pallas_call | solution.py:495
  259.8 0.8 dynamic-slice_bitcast_fusion.2
  261.2 0.9 constant_dynamic-slice_fusion.2.noise
  263.0 19.7 %conv_forward.1 = (f32[512,768]{1,0:T(8,128)}, bf16[512,768]{1,0:T(8,128)(2,1)}, f32[2,512,192]{2,1,0:T(8,128)}, bf16[2,640,576]{2,1,0:T(8,128)(2,1)}, bf16[512,768]{1,0:T(8,128)(2,1)}) custom-call(f32[1,1]{1,0:T(1,128)} %bitcast.level, f32[512,768]{1,0:T(8,128)} %get-tuple-element.71.resid, bf16[512,768]{1,0:T(8,128)(2,1)} %get-tuple-element.72.own, ...), custom_call_target="tpu_custom_call" | custom-call | flops 7000000000 | bytes 20591620 | tf_op jit(solution)/shard_map/conv_forward/pallas_call | solution.py:495
  283.2 0.8 dynamic-slice_bitcast_fusion.codec
  284.0 1.0 constant_dynamic-slice_fusion.1.cot
  285.3 0.9 copy-done.44
  286.2 10.6 %cross_forward.1 = (f32[512,768]{1,0:T(8,128)}, bf16[512,768]{1,0:T(8,128)(2,1)}, bf16[2,512,192]{2,1,0:T(8,128)(2,1)}, bf16[2,256,384]{2,1,0:T(8,128)(2,1)}, bf...) custom-call(f32[512,768]{1,0:T(8,128)} %get-tuple-element.75.noisy, ...), custom_call_target="tpu_custom_call" | custom-call | flops 2000000000 | bytes 10266624 | tf_op jit(solution)/shard_map/cross_forward/pallas_call | solution.py:495
  296.8 16.4 %cross_backward.1 = (bf16[2,768,768]{2,1,0:T(8,128)(2,1)}, bf16[512,768]{1,0:T(8,128)(2,1)}) custom-call(bf16[512,768]{1,0:T(8,128)(2,1)} %constant_dynamic-slice_fusion.1.cot, bf16[512,768]{1,0:T(8,128)(2,1)} %get-tuple-element.81.n3, bf16[256,768]{1,0:T(8,128)(2,1)} %dynamic-slice_bitcast_fusion.codec, bf16[2,512,192]{2,1,0:T(8,128)(2,1)} %get-tuple-element.82.cq, ...), custom_call_target="tpu_custom_call" | custom-call | flops 4000000000 | bytes 8663040 | tf_op jit(solution)/shard_map/cross_backward/pallas_call | solution.py:495
  313.6 1.0 copy.69.embed_col
  314.7 1.1 collective-permute-done.5.other
  315.8 26.0 %conv_two_backward.1 = (f32[512,768]{1,0:T(8,128)}, bf16[2,768,1728]{2,1,0:T(8,128)(2,1)}, bf16[2,640,576]{2,1,0:T(8,128)(2,1)}, f32[2,768]{1,0:T(2,128)}, f32[2,2,192]{2,1,0:T(2,128)}, /*index=5*/f32[2,192]{1,0:T(2,128)}) custom-call(f32[512,768]{1,0:T(8,128)} %get-tuple-element.78.resid, bf16[512,768]{1,0:T(8,128)(2,1)} %get-tuple-element.86.own, ...), custom_call_target="tpu_custom_call" | custom-call | flops 6000000000 | bytes 19901952 | tf_op jit(solution)/shard_map/conv_two_backward/pallas_call | solution.py:495
  341.9 13.3 %conv_one_backward.1 = (bf16[2,768,1920]{2,1,0:T(8,128)(2,1)}, bf16[512,768]{1,0:T(8,128)(2,1)}) custom-call(bf16[512,768]{1,0:T(8,128)(2,1)} %get-tuple-element.80.first, bf16[2,640,576]{2,1,0:T(8,128)(2,1)} %get-tuple-element.89.tapsg, f32[2,192]{1,0:T(2,128)} %get-tuple-element.90.gsum, f32[768,1]{1,0:T(8,128)} %copy.69.embed_col, ...), custom_call_target="tpu_custom_call" | custom-call | flops 6000000000 | bytes 14848512 | tf_op jit(solution)/shard_map/conv_one_backward/pallas_call | solution.py:495
  355.6 1.6 add_convert_fusion
  357.2 1.4 collective-permute-start.4
  358.6 16.1 %mlp_backward.1 = (f32[512,768]{1,0:T(8,128)}, bf16[2,768,1536]{2,1,0:T(8,128)(2,1)}, bf16[512,768]{1,0:T(8,128)(2,1)}, f32[2,768]{1,0:T(2,128)}) custom-call(f32[512,768]{1,0:T(8,128)} %get-tuple-element.75.noisy, bf16[512,768]{1,0:T(8,128)(2,1)} %get-tuple-element.91.own, bf16[512,768]{1,0:T(8,128)(2,1)} %collective-permute-done.6.other, ...), custom_call_target="tpu_custom_call" | custom-call | flops 7000000000 | bytes 17338368 | tf_op jit(solution)/shard_map/mlp_backward/pallas_call | solution.py:495
  376.0 0.9 collective-permute-done.4
  376.9 1.2 select_bitcast_fusion.1
  378.2 0.9 copy-done.43
  379.0 22.6 %attn_backward.1 = (f32[512,768]{1,0:T(8,128)}, bf16[2,768,768]{2,1,0:T(8,128)(2,1)}, bf16[512,768]{1,0:T(8,128)(2,1)}, f32[2,768]{1,0:T(2,128)}) custom-call(s32[512,1]{1,0:T(8,128)} %copy.68.seg_col, s32[1,512]{1,0:T(1,128)} %constant_dynamic-slice_fusion.3.seg_row, f32[512,768]{1,0:T(8,128)} %get-tuple-element.71.resid, ...), custom_call_target="tpu_custom_call" | custom-call | flops 8000000000 | bytes 14209024 | tf_op jit(solution)/shard_map/attn_backward/pallas_call | solution.py:495
  401.6 206.7 %scatter_grads.1 = (f32[96,768]{1,0:T(8,128)}, f32[96,1536]{1,0:T(8,128)}, f32[96,1920]{1,0:T(8,128)}, f32[96,1728]{1,0:T(8,128)}, f32[96,768]{1,0:T(8,128)}) custom-call(bf16[2,4,2,96,768]{4,3,2,1,0:T(8,128)(2,1)} %bitcast.79, bf16[2,4,2,96,1536]{4,3,2,1,0:T(8,128)(2,1)} %bitcast.74, bf16[2,4,2,96,1920]{4,3,2,1,0:T(8,128)(2,1)} %bitcast.72, ...), custom_call_target="tpu_custom_call" | custom-call | tf_op jit(solution)/shard_map/scatter_grads/pallas_call | solution.py:1218
  608.3 1.2 slice.73
  609.6 1.0 slice.71
  612.8 1.4 concatenate.71
  614.2 1.9 reshape.235
  616.0 1.4 concatenate.72
  617.5 1.3 copy.72
  618.8 6.1 multiply_reduce_fusion.1
  625.0 2.3 multiply_reduce_fusion.3
  627.3 1.6 multiply_reduce_fusion.7
  628.9 1.6 multiply_reduce_fusion.6
  630.6 1.4 pad_maximum_fusion.10
  631.9 1.4 pad_maximum_fusion.11
  633.3 4.5 input_backward.1
  638.6 1.3 concatenate.74
  639.8 2.4 pad_maximum_fusion
  642.3 46.3 %all-reduce = (f32[29]{0:T(128)S(1)}, f32[29]{0:T(128)S(1)}, f32[10,768]{1,0:T(8,128)}) all-reduce(f32[29]{0:T(128)S(1)} %pad_maximum_fusion.11, f32[29]{0:T(128)S(1)} %pad_maximum_fusion.10, f32[10,768]{1,0:T(8,128)} %concatenate.74), channel_id=1, replica_groups=mesh['dp'=8,'mp'=4] {'dp','mp'}, use_global_device_ids=true, to_apply=%region_9.10 | all-reduce | flops 7738 | bytes 61904 | tf_op jit(solution)/shard_map/psum | solution.py:1449
  689.3 1.0 constant_dynamic-slice_fusion
  690.3 2.3 collective-permute-start.9
  692.6 1.0 multiply_reduce_fusion.9
  693.7 1.5 multiply_subtract_fusion.4
  695.2 2.7 multiply_subtract_fusion.2
  697.9 1.5 multiply_subtract_fusion.3
  700.0 1.6 multiply_subtract_fusion.1
  702.2 2.0 multiply_subtract_fusion
  704.4 1.0 copy-done.15
  705.7 2.0 bitcast_convert_fusion
  (144 shorter events, 13.6 us)
Async XLA Ops:
  0.7 16.1 %copy-start = (bf16[1024,768]{1,0:T(8,128)(2,1)S(1)}, bf16[1024,768]{1,0:T(8,128)(2,1)}, u32[]{:S(2)}) copy-start(bf16[1024,768]{1,0:T(8,128)(2,1)} %param.21) | copy-start | bytes 4718596
  4.7 6.8 copy-start.3
  11.6 5.1 copy-start.10
  11.6 5.1 copy-start.12
  16.7 1.1 copy-start.16
  16.7 2.7 copy-start.23
  16.8 2.6 copy-start.24
  16.8 1.1 copy-start.33
  16.8 2.6 copy-start.34
  16.8 2.6 copy-start.35
  246.9 2.6 collective-permute-start
  249.5 0.9 copy-start.45
  250.4 8.1 %copy-start.46 = (s32[2]{0:T(128)S(1)}, s32[2]{0:T(128)}, u32[]{:S(2)}) copy-start(s32[2]{0:T(128)} %param.24) | copy-start | bytes 28
  250.4 10.8 %copy-start.27 = (bf16[1024,768]{1,0:T(8,128)(2,1)S(1)}, bf16[1024,768]{1,0:T(8,128)(2,1)}, u32[]{:S(2)}) copy-start(bf16[1024,768]{1,0:T(8,128)(2,1)} %param.22) | copy-start | bytes 4718596
  258.2 3.9 collective-permute-start.1
  262.1 0.9 copy-start.42
  263.0 20.1 %copy-start.38 = (bf16[2,256,768]{2,1,0:T(8,128)(2,1)S(1)}, bf16[2,256,768]{2,1,0:T(8,128)(2,1)}, u32[]{:S(2)}) copy-start(bf16[2,256,768]{2,1,0:T(8,128)(2,1)} %param.23) | copy-start | bytes 2359300
  263.0 20.9 %copy-start.28 = (bf16[1024,768]{1,0:T(8,128)(2,1)S(1)}, bf16[1024,768]{1,0:T(8,128)(2,1)}, u32[]{:S(2)}) copy-start(bf16[1024,768]{1,0:T(8,128)(2,1)} %param.26) | copy-start | bytes 4718596
  282.7 2.6 collective-permute-start.2
  285.3 0.9 copy-start.44
  296.8 17.8 %copy-start.21 = (bf16[512,768]{1,0:T(8,128)(2,1)S(1)}, bf16[512,768]{1,0:T(8,128)(2,1)}, u32[]{:S(2)}) copy-start(bf16[512,768]{1,0:T(8,128)(2,1)} %get-tuple-element.79) | copy-start | bytes 2359300
  313.1 2.7 collective-permute-start.5
  314.6 41.0 %collective-permute-start.3 = (bf16[512,768]{1,0:T(8,128)(2,1)S(1)}, bf16[512,768]{1,0:T(8,128)(2,1)S(1)}, u32[]{:S(2)}, u32[]{:S(2)}) collective-permute-start(bf16[512,768]{1,0:T(8,128)(2,1)S(1)} %copy-done.21), channel_id=1, source_target_pairs={{0,1},{1,0},{2,3},{3,2},{4,5},{5,4},{6,7},{7,6},{8,9},{9,8},{10,11... | collective-permute-start | bytes 2359304 | tf_op jit(solution)/shard_map/ppermute | solution.py:430
  355.2 3.5 collective-permute-start.6
  357.2 19.7 %collective-permute-start.4 = (bf16[512,768]{1,0:T(8,128)(2,1)S(1)}, bf16[512,768]{1,0:T(8,128)(2,1)S(1)}, u32[]{:S(2)}, u32[]{:S(2)}) collective-permute-start(bf16[512,768]{1,0:T(8,128)(2,1)S(1)} %add_convert_fusion), channel_id=1, source_target_pairs={{0,2},{1,3},{2,0},{3,1},{4,6},{5,7},{6,4},{7,5},{8,10},{9,11},{10,... | collective-permute-start | bytes 2359304 | tf_op jit(solution)/shard_map/ppermute | solution.py:434
  358.6 16.2 %copy-start.41 = (f32[2,2,192]{2,1,0:T(2,128)S(1)}, f32[2,2,192]{2,1,0:T(2,128)}, u32[]{:S(2)}) copy-start(f32[2,2,192]{2,1,0:T(2,128)} %get-tuple-element.116) | copy-start | bytes 9220
  358.6 16.6 %copy-start.40 = (f32[2,768]{1,0:T(2,128)S(1)}, f32[2,768]{1,0:T(2,128)}, u32[]{:S(2)}) copy-start(f32[2,768]{1,0:T(2,128)} %get-tuple-element.117) | copy-start | bytes 18436
  374.8 3.4 collective-permute-start.7
  378.2 0.9 copy-start.43
  608.3 2.2 copy-start.26
  608.3 3.0 copy-start.25
  612.8 20.6 %collective-permute-start.8 = (bf16[512,768]{1,0:T(8,128)(2,1)}, bf16[512,768]{1,0:T(8,128)(2,1)}, u32[]{:S(2)}, u32[]{:S(2)}) collective-permute-start(bf16[512,768]{1,0:T(8,128)(2,1)} %get-tuple-element.100.own), channel_id=1, source_target_pairs={{0,1},{1,0},{2,3},{3,2},{4,5},{5,4},{6,7},{7,6},{8,9},{9,8},{10,11... | collective-permute-start | bytes 2359304 | tf_op jit(solution)/shard_map/ppermute | solution.py:430
  616.0 2.8 copy-start.2
  618.8 6.1 copy-start.8
  618.8 6.1 copy-start.19
  618.8 6.1 copy-start.20
  624.9 2.3 copy-start.13
  624.9 2.3 copy-start.22
  625.0 2.3 copy-start.29
  625.0 2.3 copy-start.30
  627.2 1.7 copy-start.11
  627.2 1.7 copy-start.31
  627.2 1.7 copy-start.32
  627.3 6.0 copy-start.39
  633.3 6.5 copy-start.9
  642.3 55.6 %copy-start.14 = (f32[96,768]{1,0:T(8,128)S(1)}, f32[96,768]{1,0:T(8,128)}, u32[]{:S(2)}) copy-start(f32[96,768]{1,0:T(8,128)} %param.29) | copy-start | bytes 884740
  642.3 55.6 %copy-start.17 = (f32[96,768]{1,0:T(8,128)S(1)}, f32[96,768]{1,0:T(8,128)}, u32[]{:S(2)}) copy-start(f32[96,768]{1,0:T(8,128)} %get-tuple-element.137) | copy-start | bytes 884740
  642.3 55.6 %copy-start.18 = (f32[96,768]{1,0:T(8,128)S(1)}, f32[96,768]{1,0:T(8,128)}, u32[]{:S(2)}) copy-start(f32[96,768]{1,0:T(8,128)} %get-tuple-element.138) | copy-start | bytes 884740
  690.3 9.7 %copy-start.6 = (f32[11,192,96]{2,1,0:T(8,128)S(1)}, f32[11,192,96]{2,1,0:T(8,128)}, u32[]{:S(2)}) copy-start(f32[11,192,96]{2,1,0:T(8,128)} %get-tuple-element.135) | copy-start | bytes 2433028
  690.3 9.7 %copy-start.7 = (f32[11,192,96]{2,1,0:T(8,128)S(1)}, f32[11,192,96]{2,1,0:T(8,128)}, u32[]{:S(2)}) copy-start(f32[11,192,96]{2,1,0:T(8,128)} %get-tuple-element.136) | copy-start | bytes 2433028
  690.3 11.2 %collective-permute-start.9 = (bf16[256,768]{1,0:T(8,128)(2,1)S(1)}, bf16[256,768]{1,0:T(8,128)(2,1)S(1)}, u32[]{:S(2)}, u32[]{:S(2)}) collective-permute-start(bf16[256,768]{1,0:T(8,128)(2,1)S(1)} %constant_dynamic-slice_fusion), channel_id=1, source_target_pairs={{0,2},{1,3},{2,0},{3,1},{4,6},{5,7},{6,4},{7,5},{8,10},{9,11},{10,... | collective-permute-start | bytes 1179656 | tf_op jit(solution)/shard_map/ppermute | solution.py:434
  693.6 7.9 %copy-start.36 = (f32[10,768]{1,0:T(8,128)}, f32[10,768]{1,0:T(8,128)S(1)}, u32[]{:S(2)}) copy-start(f32[10,768]{1,0:T(8,128)S(1)} %get-tuple-element.131) | copy-start | bytes 92164
  693.7 7.9 %copy-start.37 = (f32[10,768]{1,0:T(8,128)}, f32[10,768]{1,0:T(8,128)S(1)}, u32[]{:S(2)}) copy-start(f32[10,768]{1,0:T(8,128)S(1)} %get-tuple-element.132) | copy-start | bytes 92164
  700.0 1.7 copy-start.4
  700.0 2.3 copy-start.5
  701.6 2.7 collective-permute-start.10
  704.2 1.1 copy-start.15
  705.5 2.2 copy-start.1

commit v3 on v2

--- a/solution.py
+++ b/solution.py
@@ -592,155 +592,6 @@
         dq.append(mm(ds, k[:, cols]) * score_scale)
         dk.append(mm_tn(ds, q[:, cols]))
     return [jnp.concatenate(d, axis=1) for d in (dq, dk, dv)]
-
-
-def attn_forward(seg_col, seg_row, tok, norms, w, n1, qkv, mixed, logs, part, wv, sems):
-    n = mixed.shape[2]
-    copies = start_copies([(w.at[0], wv.at[0]), (w.at[1], wv.at[1])], sems)
-
-    def norm(r):
-        hat, _ = ln_stats(tok[r, :].astype(F32))
-        n1[r, :] = (hat * norms[0:1, :] + norms[1:2, :]).astype(LOW)
-
-    each_rows(norm)
-    for i in range(2):
-        copies[i].wait()
-        qkv[i] = mm(n1[...], wv[i, :, : 3 * n]).astype(LOW)
-
-    def heads(r):
-        mask = seg_col[r, :] == seg_row[...]
-        found = []
-        for i in range(2):
-            got, logs_i = softmax_heads(
-                qkv[i, r, 0:n], qkv[i, :, n : 2 * n], qkv[i, :, 2 * n : 3 * n],
-                n // HD, HD ** (-0.5), mask,
-            )
-            mixed[i, r, :] = got
-            found += logs_i
-        logs[r, :] = jnp.concatenate(found, axis=1)
-
-    each_rows(heads)
-    total = mm_nt(mixed[0], wv[0, :, 3 * n :]) + mm_nt(mixed[1], wv[1, :, 3 * n :])
-    part[...] = total.astype(LOW)
-
-
-def mlp_forward(tok, own, other, norms, w, resid, n2, part, wv, acc, sems):
-    hid = wv.shape[2] // 2
-    copies = start_copies([(w.at[0], wv.at[0]), (w.at[1], wv.at[1])], sems)
-
-    def norm(r):
-        v = tok[r, :].astype(F32) + (own[r, :].astype(F32) + other[r, :].astype(F32))
-        resid[r, :] = v
-        hat, _ = ln_stats(v)
-        n2[r, :] = (hat * norms[2:3, :] + norms[3:4, :]).astype(LOW)
-
-    each_rows(norm)
-    block = 256
-    for i in range(2):
-        copies[i].wait()
-        for b in range(hid // block):
-            pre = mm(n2[...], wv[i, :, block * b : block * (b + 1)])
-            hidden = gelu_parts(pre)[1].astype(LOW)
-            term = mm_nt(hidden, wv[i, :, hid + block * b : hid + block * (b + 1)])
-            if i == 0 and b == 0:
-                acc[...] = term
-            else:
-                acc[...] += term
-    part[...] = acc[...].astype(LOW)
-
-
-def conv_forward(
-    level, resid, own, other, noise, norms, side, embed, w, u,
-    noisy, first, conv, taps, part, pad, wv, uv, sems,
-):
-    n = conv.shape[2]
-    width = noisy.shape[1] // GROUPS
-    copies = start_copies(
-        [(w.at[0], wv.at[0]), (w.at[1], wv.at[1]), (u.at[0], uv.at[0]), (u.at[1], uv.at[1])], sems
-    )
-    mats = group_mats(noisy.shape[1], width)
-    mats_n = group_mats(n, width)
-    pad[0:TIME, :] = jnp.zeros((TIME, pad.shape[1]), LOW)
-    pad[TIME + ROWS :, :] = jnp.zeros((TIME, pad.shape[1]), LOW)
-
-    def join(r):
-        v = resid[r, :] + (own[r, :].astype(F32) + other[r, :].astype(F32))
-        noisy[r, :] = v + level[...] * noise[r, :].astype(F32)
-
-    each_rows(join)
-    mean = group_average(jnp.sum(noisy[...], axis=0, keepdims=True), mats, width)
-    centre = noisy[...] - mean
-    var = group_average(jnp.sum(centre * centre, axis=0, keepdims=True), mats, width)
-    scale = lax.rsqrt(var + NORM_EPS) * norms[4:5, :]
-
-    def act(r):
-        v = (noisy[r, :] - mean) * scale + norms[5:6, :]
-        low = (v * jax.nn.sigmoid(v)).astype(LOW)
-        first[r, :] = low
-
-    each_rows(act)
-    pad[TIME : TIME + ROWS, :] = first[...]
-    for i in range(2):
-        copies[i].wait()
-        q = None
-        for a in range(3):
-            term = mm(pad[TIME * a : TIME * a + ROWS, :], wv[i, :, 3 * n * a : 3 * n * (a + 1)])
-            q = term if q is None else q + term
-        shift = mm(embed[...], wv[i, :, 9 * n : 10 * n])[0:1]
-        c1 = from_left(q[:, :n]) + q[:, n : 2 * n] + from_right(q[:, 2 * n :]) + shift
-        conv[i] = c1
-        mean_n = group_average(jnp.sum(c1, axis=0, keepdims=True), mats_n, width)
-        c1 = c1 - mean_n
-        var_n = group_average(jnp.sum(c1 * c1, axis=0, keepdims=True), mats_n, width)
-        v = c1 * lax.rsqrt(var_n + NORM_EPS) * side[i, 0:1, :] + side[i, 1:2, :]
-        v = v * jax.nn.sigmoid(v)
-        taps[i, 0:TIME, :] = jnp.zeros((TIME, 3 * n), LOW)
-        taps[i, TIME + ROWS :, :] = jnp.zeros((TIME, 3 * n), LOW)
-        taps[i, TIME : TIME + ROWS, :] = jnp.concatenate(
-            [from_left(v), v, from_right(v)], axis=1
-        ).astype(LOW)
-    total = None
-    for i in range(2):
-        copies[2 + i].wait()
-        for a in range(3):
-            term = mm_nt(
-                taps[i, TIME * a : TIME * a + ROWS, :], uv[i, :, 3 * n * a : 3 * n * (a + 1)]
-            )
-            total = term if total is None else total + term
-    part[...] = total.astype(LOW)
-
-
-def cross_forward(
-    noisy, own, other, codec, norms, w, resid, n3, cq, ckv, mixed, logs, part, wv, sems
-):
-    n = mixed.shape[2]
-    copies = start_copies([(w.at[0], wv.at[0]), (w.at[1], wv.at[1])], sems)
-
-    def norm(r):
-        v = noisy[r, :] + (own[r, :].astype(F32) + other[r, :].astype(F32))
-        resid[r, :] = v
-        hat, _ = ln_stats(v)
-        n3[r, :] = (hat * norms[8:9, :] + norms[9:10, :]).astype(LOW)
-
-    each_rows(norm)
-    for i in range(2):
-        copies[i].wait()
-        cq[i] = mm(n3[...], wv[i, :, :n]).astype(LOW)
-        ckv[i] = mm(codec[...], wv[i, :, n : 3 * n]).astype(LOW)
-
-    def heads(r):
-        found = []
-        for i in range(2):
-            got, logs_i = softmax_heads(
-                cq[i, r, :], ckv[i, :, :n], ckv[i, :, n:], n // HD, HD ** (-0.5), None
-            )
-            mixed[i, r, :] = got
-            found += logs_i
-        logs[r, :] = jnp.concatenate(found, axis=1)
-
-    each_rows(heads)
-    total = mm_nt(mixed[0], wv[0, :, 3 * n :]) + mm_nt(mixed[1], wv[1, :, 3 * n :])
-    part[...] = total.astype(LOW)
 
 
 def cross_backward(
@@ -1011,103 +862,406 @@
 
 class Sender:
     def __init__(self, send, recv):
-        self.send, self.recv, self.used = send, recv, 0
+        self.send, self.recv, self.made = send, recv, []
 
     def start(self, src, dst, peer):
-        k = self.used
-        self.used += 1
+        k = len(self.made)
         copy = pltpu.make_async_remote_copy(
             src_ref=src, dst_ref=dst, send_sem=self.send.at[k], recv_sem=self.recv.at[k],
             device_id=peer, device_id_type=MESH_IDS,
         )
         copy.start()
+        self.made.append(copy)
         return copy
 
-
-def gather_body(count, *refs):
-    pieces, outs, (own_sem, send, recv) = refs[:count], refs[count : 2 * count], refs[2 * count :]
+    def close(self):
+        for copy in self.made:
+            copy.wait_send()
+
+
+def pack_piece(g, w_in, w_back, w_up, w_down, piece):
+    n = w_in.shape[2]
+    if g == 1:
+        hid = w_up.shape[1]
+        piece[:, :hid] = w_up[...].astype(LOW)
+        piece[:, hid:] = w_down[...].astype(LOW)
+        return
+    ins, backs = GROUPS_OF[g]
+    cols = [w_in[j] for j in ins] + [w_back[j].T for j in backs]
+    for k in range(0, len(cols), 2):
+        pair = cols[k : k + 2]
+        both = pair[0] if len(pair) == 1 else jnp.concatenate(pair, axis=1)
+        piece[:, n * k : n * (k + len(pair))] = both.astype(LOW)
+
+
+GROUPS_OF = {
+    0: ([0, 1, 2], [0]),
+    2: ([*range(7, 16), 3], []),
+    3: ([], [*range(2, 11)]),
+    4: ([4, 5, 6], [1]),
+}
+
+
+def row_of(values):
+    lane = lax.broadcasted_iota(jnp.int32, (1, 128), 1)
+    row = jnp.zeros((1, 128), F32)
+    for j, v in enumerate(values):
+        row = row + jnp.where(lane == j, v, 0.0)
+    return row
+
+
+def square_sum(v):
+    return jnp.sum(jnp.sum(v * v, axis=1, keepdims=True), axis=0, keepdims=True)
+
+
+class Gather:
+    def __init__(self, pieces, outs, net):
+        self.pieces, self.outs, self.net = pieces, outs, net
+        self.x, self.core, self.z, self.y = place()
+        self.to_x, self.to_y, self.to_z = chip_peers()
+        self.lines, self.planes, self.corners = {}, {}, {}
+
+    def line(self, g):
+        self.lines[g] = [
+            self.net.start(self.pieces[g], self.outs[g].at[0, self.z, self.y], peer)
+            for peer in self.to_z
+        ]
+
+    def own(self, g):
+        z, y, out = self.z, self.y, self.outs[g]
+        self.planes[g] = [
+            self.net.start(self.pieces[g], out.at[1, z, y], self.to_x),
+            self.net.start(self.pieces[g], out.at[0, z, y], self.to_y),
+        ]
+
+    def spread(self, g, k):
+        self.lines[g][k - 1].wait_recv()
+        src = self.outs[g].at[0, (self.z - k) % 4, self.y]
+        dst = self.outs[g].at[1, (self.z - k) % 4, self.y]
+        self.planes[g] += [self.net.start(src, dst, self.to_x), self.net.start(src, src, self.to_y)]
+
+    def turn(self, g):
+        for c in self.planes[g]:
+            c.wait_recv()
+        out, y = self.outs[g], self.y
+        self.corners[g] = [
+            self.net.start(out.at[0, 0:2, 1 - y], out.at[1, 0:2, 1 - y], self.to_x),
+            self.net.start(out.at[1, 2:4, y], out.at[1, 2:4, y], self.to_y),
+        ]
+
+    def ready(self, g):
+        for c in self.corners[g]:
+            c.wait_recv()
+
+    def early(self, g):
+        z, y, out = self.z, self.y, self.outs[g]
+        self.first = [
+            self.net.start(self.pieces[g], out.at[1, z, y], self.to_x),
+            self.net.start(self.pieces[g], out.at[0, z, y], self.to_y),
+        ]
+
+    def late(self, g):
+        self.first[0].wait_recv()
+        src = self.outs[g].at[1, self.z, self.y]
+        self.first.append(self.net.start(src, src, self.to_y))
+
+    def far(self, g):
+        self.first[1].wait_recv()
+        self.first[2].wait_recv()
+        block = self.outs[g].at[:, self.z]
+        self.corners[g] = [self.net.start(block, block, peer) for peer in self.to_z]
+
+
+def matrix_of(ref, i, first, last):
+    block = ref[i, :, :, :, first:last]
+    return block.reshape(-1, last - first)
+
+
+def forward_body(
+    w_in, w_back, w_up, w_down, seg_col, seg_row, norms, side, embed, level, tokens, noises, codecs,
+    g0, g1, g2, g3, g4, sq, n1_o, qkv_o, mixed_o, logs_o, resid_o, n2_o, noisy_o, first_o, conv_o,
+    taps_o, resid3_o, n3_o, cq_o, ckv_o, cross_o, logs_c_o, out_o,
+    p0, p1, p2, p3, p4, v0, v1, v2, v3, v4, tok, noise, codec, n1, qkv, mixed, logs, resid, n2,
+    noisy, first, conv, taps, resid3, n3, cq, ckv, cross, logs_c, out, pad, acc, sent, got,
+    in_sem, out_sem, own_sem, send, recv,
+):
+    pieces, held, kept = (p0, p1, p2, p3, p4), (v0, v1, v2, v3, v4), (g0, g1, g2, g3, g4)
+    n = mixed.shape[2]
+    hid = w_up.shape[1]
+    features = norms.shape[1]
+    width = features // GROUPS
+    heads = n // HD
+    score_scale = HD ** (-0.5)
+    net = Sender(send, recv)
+    run = Gather(pieces, held, net)
     x, core, z, y = place()
-    to_x, to_y, to_z = chip_peers()
-    net = Sender(send, recv)
-    local = [
-        pltpu.make_async_copy(pieces[g], outs[g].at[0, z, y], own_sem.at[g]) for g in range(count)
+    sibling = device(x, 1 - core, z, y)
+    loads = [
+        pltpu.make_async_copy(tokens.at[pl.ds(pl.multiple_of(x * ROWS, ROWS), ROWS), :], tok, in_sem.at[0]),
+        pltpu.make_async_copy(noises.at[pl.ds(pl.multiple_of(x * ROWS, ROWS), ROWS), :], noise, in_sem.at[1]),
+        pltpu.make_async_copy(codecs.at[x], codec, in_sem.at[2]),
     ]
-    for c in local:
+    for c in loads:
         c.start()
-    meet([to_x, to_y, *to_z])
-
-    def send_line(g):
-        return [net.start(pieces[g], outs[g].at[0, z, y], peer) for peer in to_z]
-
-    def send_planes(g):
-        line = outs[g].at[0, :, y]
-        return (
-            net.start(line, outs[g].at[1, :, y], to_x),
-            net.start(line, outs[g].at[0, :, y], to_y),
-        )
-
-    def send_corners(g):
-        return (
-            net.start(outs[g].at[0, 0:2, 1 - y], outs[g].at[1, 0:2, 1 - y], to_x),
-            net.start(outs[g].at[1, 2:4, y], outs[g].at[1, 2:4, y], to_y),
-        )
-
-    last = count - 1
-    src = pieces[last]
-    lines = {0: send_line(0)}
-    early_x = net.start(src, outs[last].at[1, z, y], to_x)
-    early_y = net.start(src, outs[last].at[0, z, y], to_y)
-    planes, corners, done = {}, {}, [early_x, early_y]
-    for g in range(last):
-        for c in lines[g]:
-            c.wait_recv()
-        local[g].wait()
-        planes[g] = send_planes(g)
-        if g + 1 < last:
-            lines[g + 1] = send_line(g + 1)
-        if g == 0:
-            early_x.wait_recv()
-            late = net.start(outs[last].at[1, z, y], outs[last].at[1, z, y], to_y)
-        if g == 1:
-            early_y.wait_recv()
-            late.wait_recv()
-            local[last].wait()
-            block = outs[last].at[:, z]
-            far = [net.start(block, outs[last].at[:, z], peer) for peer in to_z]
-        if g >= 1:
-            for c in planes[g - 1]:
-                c.wait_recv()
-            corners[g - 1] = send_corners(g - 1)
-    for c in planes[last - 1]:
-        c.wait_recv()
-    corners[last - 1] = send_corners(last - 1)
-    for g in range(last):
-        for c in corners[g]:
-            c.wait_recv()
-    for c in far:
-        c.wait_recv()
-    for c in [*done, late, *far]:
-        c.wait_send()
-    for g in range(last):
-        for c in [*lines[g], *planes[g], *corners[g]]:
-            c.wait_send()
-
-
-def gather_all(pieces):
-    count = len(pieces)
-    copies = (count - 1) * 7 + 6
-    return pl.pallas_call(
-        partial(gather_body, count),
-        name="gather_weights",
-        in_specs=[spec_any() for _ in pieces],
-        out_specs=[spec_any() for _ in pieces],
-        out_shape=[jax.ShapeDtypeStruct((2, 4, 2, *p.shape), LOW) for p in pieces],
+    stores = []
+
+    def store(src, dst):
+        copy = pltpu.make_async_copy(src, dst, out_sem.at[len(stores)])
+        copy.start()
+        stores.append(copy)
+
+    def pack(g):
+        pack_piece(g, w_in, w_back, w_up, w_down, pieces[g])
+        copy = pltpu.make_async_copy(pieces[g], held[g].at[0, z, y], own_sem.at[g])
+        copy.start()
+        return copy
+
+    def exchange(k, total):
+        sent[k] = total.astype(LOW)
+        return net.start(sent.at[k], got.at[k], sibling)
+
+    def joined(k, r):
+        return sent[k, r, :].astype(F32) + got[k, r, :].astype(F32)
+
+    local = [pack(0)]
+    meet([run.to_x, run.to_y, *run.to_z, sibling])
+    run.line(0)
+    run.own(0)
+    local.append(pack(1))
+    run.own(1)
+    local += [pack(2), pack(3), pack(4)]
+    run.early(4)
+    loads[0].wait()
+
+    def norm_one(r):
+        hat, _ = ln_stats(tok[r, :].astype(F32))
+        n1[r, :] = (hat * norms[0:1, :] + norms[1:2, :]).astype(LOW)
+
+    each_rows(norm_one)
+    store(n1, n1_o)
+    run.spread(0, 1)
+    run.line(1)
+    run.spread(0, 2)
+    run.spread(0, 3)
+    run.own(2)
+    sq[...] = row_of(
+        [square_sum(w_in[j]) for j in range(16)] + [square_sum(w_back[j]) for j in range(11)]
+        + [square_sum(w_up[...]), square_sum(w_down[...])]
+    )
+    run.turn(0)
+    run.late(4)
+    local[0].wait()
+    run.ready(0)
+    store(v0, g0)
+    for i in range(2):
+        qkv[i] = mm(n1[...], matrix_of(v0, i, 0, 3 * n)).astype(LOW)
+    store(qkv, qkv_o)
+    run.spread(1, 1)
+    run.line(2)
+    run.spread(1, 2)
+    run.spread(1, 3)
+    run.own(3)
+
+    def self_heads(r):
+        mask = seg_col[r, :] == seg_row[...]
+        found = []
+        for i in range(2):
+            part, logs_i = softmax_heads(
+                qkv[i, r, 0:n], qkv[i, :, n : 2 * n], qkv[i, :, 2 * n : 3 * n], heads, score_scale, mask
+            )
+            mixed[i, r, :] = part
+            found += logs_i
+        logs[r, :] = jnp.concatenate(found, axis=1)
+
+    each_rows(self_heads)
+    swap = exchange(
+        0,
+        mm_nt(mixed[0], matrix_of(v0, 0, 3 * n, 4 * n)) + mm_nt(mixed[1], matrix_of(v0, 1, 3 * n, 4 * n)),
+    )
+    store(mixed, mixed_o)
+    store(logs, logs_o)
+    run.turn(1)
+    swap.wait_recv()
+
+    def norm_two(r):
+        v = tok[r, :].astype(F32) + joined(0, r)
+        resid[r, :] = v
+        hat, _ = ln_stats(v)
+        n2[r, :] = (hat * norms[2:3, :] + norms[3:4, :]).astype(LOW)
+
+    each_rows(norm_two)
+    store(resid, resid_o)
+    store(n2, n2_o)
+    run.spread(2, 1)
+    run.line(3)
+    run.spread(2, 2)
+    run.spread(2, 3)
+    local[1].wait()
+    run.ready(1)
+    store(v1, g1)
+    block = 256
+    for i in range(2):
+        for b in range(hid // block):
+            pre = mm(n2[...], matrix_of(v1, i, block * b, block * (b + 1)))
+            low = gelu_parts(pre)[1].astype(LOW)
+            term = mm_nt(low, matrix_of(v1, i, hid + block * b, hid + block * (b + 1)))
+            if i == 0 and b == 0:
+                acc[...] = term
+            else:
+                acc[...] += term
+    swap = exchange(1, acc[...])
+    run.turn(2)
+    loads[1].wait()
+    swap.wait_recv()
+
+    def add_noise(r):
+        noisy[r, :] = resid[r, :] + joined(1, r) + level[...] * noise[r, :].astype(F32)
+
+    each_rows(add_noise)
+    store(noisy, noisy_o)
+    mats = group_mats(features, width)
+    mats_n = group_mats(n, width)
+    mean = group_average(jnp.sum(noisy[...], axis=0, keepdims=True), mats, width)
+    centre = noisy[...] - mean
+    var = group_average(jnp.sum(centre * centre, axis=0, keepdims=True), mats, width)
+    scale = lax.rsqrt(var + NORM_EPS) * norms[4:5, :]
+    pad[0:TIME, :] = jnp.zeros((TIME, features), LOW)
+    pad[TIME + ROWS :, :] = jnp.zeros((TIME, features), LOW)
+
+    def act(r):
+        v = (noisy[r, :] - mean) * scale + norms[5:6, :]
+        first[r, :] = (v * jax.nn.sigmoid(v)).astype(LOW)
+
+    each_rows(act)
+    pad[TIME : TIME + ROWS, :] = first[...]
+    store(first, first_o)
+    run.spread(3, 1)
+    run.spread(3, 2)
+    run.spread(3, 3)
+    local[4].wait()
+    run.far(4)
+    local[2].wait()
+    run.ready(2)
+    store(v2, g2)
+    for i in range(2):
+        q = None
+        for a in range(3):
+            term = mm(
+                pad[TIME * a : TIME * a + ROWS, :], matrix_of(v2, i, 3 * n * a, 3 * n * (a + 1))
+            )
+            q = term if q is None else q + term
+        shift = mm(embed[...], matrix_of(v2, i, 9 * n, 10 * n))[0:1]
+        c1 = from_left(q[:, :n]) + q[:, n : 2 * n] + from_right(q[:, 2 * n :]) + shift
+        conv[i] = c1
+        c1 = c1 - group_average(jnp.sum(c1, axis=0, keepdims=True), mats_n, width)
+        var_n = group_average(jnp.sum(c1 * c1, axis=0, keepdims=True), mats_n, width)
+        v = c1 * lax.rsqrt(var_n + NORM_EPS) * side[i, 0:1, :] + side[i, 1:2, :]
+        v = v * jax.nn.sigmoid(v)
+        taps[i, 0:TIME, :] = jnp.zeros((TIME, 3 * n), LOW)
+        taps[i, TIME + ROWS :, :] = jnp.zeros((TIME, 3 * n), LOW)
+        taps[i, TIME : TIME + ROWS, :] = jnp.concatenate(
+            [from_left(v), v, from_right(v)], axis=1
+        ).astype(LOW)
+    store(conv, conv_o)
+    store(taps, taps_o)
+    run.turn(3)
+    local[3].wait()
+    run.ready(3)
+    store(v3, g3)
+    total = None
+    for i in range(2):
+        for a in range(3):
+            term = mm_nt(
+                taps[i, TIME * a : TIME * a + ROWS, :], matrix_of(v3, i, 3 * n * a, 3 * n * (a + 1))
+            )
+            total = term if total is None else total + term
+    swap = exchange(2, total)
+    loads[2].wait()
+    run.ready(4)
+    store(v4, g4)
+    for i in range(2):
+        ckv[i] = mm(codec[...], matrix_of(v4, i, n, 3 * n)).astype(LOW)
+    store(ckv, ckv_o)
+    swap.wait_recv()
+
+    def norm_three(r):
+        v = noisy[r, :] + joined(2, r)
+        resid3[r, :] = v
+        hat, _ = ln_stats(v)
+        n3[r, :] = (hat * norms[8:9, :] + norms[9:10, :]).astype(LOW)
+
+    each_rows(norm_three)
+    store(resid3, resid3_o)
+    store(n3, n3_o)
+    for i in range(2):
+        cq[i] = mm(n3[...], matrix_of(v4, i, 0, n)).astype(LOW)
+    store(cq, cq_o)
+
+    def cross_heads(r):
+        found = []
+        for i in range(2):
+            part, logs_i = softmax_heads(
+                cq[i, r, :], ckv[i, :, :n], ckv[i, :, n:], heads, score_scale, None
+            )
+            cross[i, r, :] = part
+            found += logs_i
+        logs_c[r, :] = jnp.concatenate(found, axis=1)
+
+    each_rows(cross_heads)
+    swap = exchange(
+        3,
+        mm_nt(cross[0], matrix_of(v4, 0, 3 * n, 4 * n)) + mm_nt(cross[1], matrix_of(v4, 1, 3 * n, 4 * n)),
+    )
+    store(cross, cross_o)
+    store(logs_c, logs_c_o)
+    swap.wait_recv()
+
+    def finish_rows(r):
+        out[r, :] = (resid3[r, :] + joined(3, r)).astype(LOW)
+
+    each_rows(finish_rows)
+    store(out, out_o)
+    for c in stores:
+        c.wait()
+    net.close()
+
+
+def forward_all(w_in, w_back, w_up, w_down, seg_col, seg_row, norms, side, embed, level, tokens, noises, codecs):
+    n, hid = w_in.shape[2], w_up.shape[1]
+    rows, features = w_in.shape[1], norms.shape[1]
+    heads = 2 * n // HD
+    ctok = codecs.shape[1]
+    widths = [4 * n, 2 * hid, 10 * n, 9 * n, 4 * n]
+    full = (ROWS, features)
+    tall = ROWS + 2 * TIME
+    kept = [
+        (full, LOW), ((2, ROWS, 3 * n), LOW), ((2, ROWS, n), LOW), ((ROWS, heads), F32), (full, F32),
+        (full, LOW), (full, F32), (full, LOW), ((2, ROWS, n), F32), ((2, tall, 3 * n), LOW),
+        (full, F32), (full, LOW), ((2, ROWS, n), LOW), ((2, ctok, 2 * n), LOW), ((2, ROWS, n), LOW),
+        ((ROWS, heads), F32), (full, LOW),
+    ]
+    groups = [(2, 4, 2, rows, w) for w in widths]
+    dma = pltpu.SemaphoreType.DMA
+    copies = 4 * 13 + 6 + 4
+    res = pl.pallas_call(
+        forward_body,
+        name="forward",
+        in_specs=[spec_vm() for _ in range(10)] + [spec_any() for _ in range(3)],
+        out_specs=[spec_any() for _ in groups] + [spec_vm()] + [spec_any() for _ in kept],
+        out_shape=[jax.ShapeDtypeStruct(s, LOW) for s in groups]
+        + [jax.ShapeDtypeStruct((1, 128), F32)]
+        + [jax.ShapeDtypeStruct(s, t) for s, t in kept],
         scratch_shapes=[
-            pltpu.SemaphoreType.DMA((count,)), pltpu.SemaphoreType.DMA((copies,)),
-            pltpu.SemaphoreType.DMA((copies,)),
+            *[VM((rows, w), LOW) for w in widths], *[VM(s, LOW) for s in groups],
+            VM(full, LOW), VM(full, LOW), VM((ctok, features), LOW), *[VM(s, t) for s, t in kept],
+            VM((tall, features), LOW), VM(full, F32), VM((4, *full), LOW), VM((4, *full), LOW),
+            dma((3,)), dma((22,)), dma((5,)), dma((copies,)), dma((copies,)),
         ],
-        compiler_params=pltpu.CompilerParams(collective_id=0, has_side_effects=True),
-    )(*pieces)
+        compiler_params=pltpu.CompilerParams(
+            collective_id=0, has_side_effects=True, vmem_limit_bytes=62 << 20
+        ),
+    )(w_in, w_back, w_up, w_down, seg_col, seg_row, norms, side, embed, level, tokens, noises, codecs)
+    return res[:5], res[5], res[6:]
 
 
 def add_rows(target, terms, step=16):
@@ -1230,6 +1384,121 @@
     )(*grads)
 
 
+def adam_rows(w, g, m, v, decay_rate):
+    m_new = MOMENT_DECAY * m + (1.0 - MOMENT_DECAY) * g
+    v_new = MOMENT_DECAY * v + (1.0 - MOMENT_DECAY) * g * g
+    correct = 1.0 - MOMENT_DECAY**STEP
+    update = m_new / correct / (jnp.sqrt(v_new / correct) + ADAM_EPS) + decay_rate * w
+    return m_new, v_new, update
+
+
+def moments_body(*refs):
+    sums, refs = refs[:5], refs[5:]
+    w_in, w_back, w_up, w_down, m_in, m_back, m_up, m_down, v_in, v_back, v_up, v_down = refs[:12]
+    nm_in, nm_back, nm_up, nm_down, nv_in, nv_back, nv_up, nv_down = refs[12:20]
+    u_in, u_back, u_up, u_down, usq = refs[20:]
+    n = w_in.shape[2]
+    squares = [None] * 29
+
+    def place_in(j, g):
+        m, v, u = adam_rows(w_in[j], g, m_in[j], v_in[j], WEIGHT_DECAY)
+        nm_in[j], nv_in[j], u_in[j] = m, v, u
+        squares[j] = square_sum(u)
+
+    def place_back(j, g):
+        m, v, u = adam_rows(w_back[j], g.T, m_back[j], v_back[j], WEIGHT_DECAY)
+        nm_back[j], nv_back[j], u_back[j] = m, v, u
+        squares[16 + j] = square_sum(u)
+
+    for g, (ins, backs) in GROUPS_OF.items():
+        for k, j in enumerate(ins):
+            place_in(j, sums[g][:, n * k : n * (k + 1)])
+        for k, j in enumerate(backs, len(ins)):
+            place_back(j, sums[g][:, n * k : n * (k + 1)])
+    hid = w_up.shape[1]
+    m, v, u = adam_rows(w_up[...], sums[1][:, :hid], m_up[...], v_up[...], WEIGHT_DECAY)
+    nm_up[...], nv_up[...], u_up[...] = m, v, u
+    squares[27] = square_sum(u)
+    m, v, u = adam_rows(w_down[...], sums[1][:, hid:], m_down[...], v_down[...], WEIGHT_DECAY)
+    nm_down[...], nv_down[...], u_down[...] = m, v, u
+    squares[28] = square_sum(u)
+    usq[...] = row_of(squares)
+
+
+def totals_body(rows, sq, usq, out, ring, ring_b, send, recv):
+    mp, dp = lax.axis_index("mp"), lax.axis_index("dp")
+    dp_peers = [((dp + k) % 8, mp) for k in range(1, 8)]
+    mp_peers = [(dp, (mp + k) % 4) for k in range(1, 4)]
+    ring[dp] = jnp.zeros(ring.shape[1:], F32)
+    ring[dp, 0:10, :] = rows[...]
+    ring[dp, 10:11, 0:128] = sq[...]
+    ring[dp, 11:12, 0:128] = usq[...]
+    meet(dp_peers + mp_peers)
+    net = Sender(send, recv)
+    copies = [net.start(ring.at[dp], ring.at[dp], p) for p in dp_peers]
+    for c in copies:
+        c.wait_recv()
+    total = ring[0]
+    for k in range(1, 8):
+        total = total + ring[k]
+    ring_b[mp] = total
+    copies = [net.start(ring_b.at[mp], ring_b.at[mp], p) for p in mp_peers]
+    for c in copies:
+        c.wait_recv()
+    out[...] = ring_b[0] + ring_b[1] + ring_b[2] + ring_b[3]
+    net.close()
+
+
+def apply_body(total, w_in, w_back, w_up, w_down, u_in, u_back, u_up, u_down, norms, norm_m, norm_v, *outs):
+    nw_in, nw_back, nw_up, nw_down, new_norm, new_nm, new_nv, lens = outs
+    both = jnp.sqrt(total[10:12, 0:128])
+    lens[...] = both[:, 0:29]
+    trust = LEARN_RATE * (both[0:1, :] / jnp.where(both[1:2, :] == 0.0, 1.0, both[1:2, :]))
+    lane = lax.broadcasted_iota(jnp.int32, (1, 128), 1)
+
+    def trust_of(j):
+        return jnp.sum(jnp.where(lane == j, trust, 0.0), axis=1, keepdims=True)
+
+    for j in range(16):
+        nw_in[j] = w_in[j] - trust_of(j) * u_in[j]
+    for j in range(11):
+        nw_back[j] = w_back[j] - trust_of(16 + j) * u_back[j]
+    nw_up[...] = w_up[...] - trust_of(27) * u_up[...]
+    nw_down[...] = w_down[...] - trust_of(28) * u_down[...]
+    m, v, u = adam_rows(norms[...], total[0:10, :], norm_m[...], norm_v[...], 0.0)
+    w = norms[...]
+    row_trust = jnp.sqrt(jnp.sum(w * w, axis=1, keepdims=True)) / jnp.sqrt(
+        jnp.sum(u * u, axis=1, keepdims=True)
+    )
+    new_norm[...] = w - LEARN_RATE * row_trust * u
+    new_nm[...] = m
+    new_nv[...] = v
+
+
+def lamb_all(sums, sq, rows, masters, moments, squares, norms, norm_m, norm_v):
+    shapes = [(v.shape, F32) for v in masters]
+    *mvu, usq = run_kernel(
+        moments_body, "lamb_moments", [*sums, *masters, *moments, *squares],
+        [*shapes, *shapes, *shapes, ((1, 128), F32)], [],
+    )
+    dma = pltpu.SemaphoreType.DMA
+    wide = norms.shape[1]
+    total = pl.pallas_call(
+        totals_body,
+        name="norm_totals",
+        in_specs=[spec_vm() for _ in range(3)],
+        out_specs=spec_vm(),
+        out_shape=jax.ShapeDtypeStruct((16, wide), F32),
+        scratch_shapes=[VM((8, 16, wide), F32), VM((4, 16, wide), F32), dma((10,)), dma((10,))],
+        compiler_params=pltpu.CompilerParams(collective_id=2, has_side_effects=True),
+    )(rows, sq, usq)
+    *weights, new_norm, new_nm, new_nv, lens = run_kernel(
+        apply_body, "lamb_apply", [total, *masters, *mvu[8:], norms, norm_m, norm_v],
+        [*shapes, *[(norms.shape, F32)] * 3, ((2, 29), F32)], [],
+    )
+    return (*weights, *mvu[:8], new_norm, new_nm, new_nv, lens)
+
+
 def fast_device(
     tokens,
     noise_field,
@@ -1257,33 +1526,16 @@
     features = tokens.shape[1]
     n = w_in.shape[2]
     hid = w_up.shape[1]
-    heads = 2 * n // HD
     mp = lax.axis_index("mp")
     dp = lax.axis_index("dp")
     x, core, z, y = mp // 2, mp % 2, dp // 2, dp % 2
     lead = (core == 0).astype(F32)
     slices = [2 * x + core, 2 * (1 - x) + core]
 
-    low_in = w_in.astype(LOW).transpose(1, 0, 2).reshape(w_in.shape[1], -1)
-    low_back = w_back.astype(LOW).transpose(2, 0, 1).reshape(w_back.shape[2], -1)
-    low_up = w_up.astype(LOW)
-    low_down = w_down.astype(LOW).T
-    piece_attn = jnp.concatenate([low_in[:, : 3 * n], low_back[:, :n]], axis=1)
-    piece_mlp = jnp.concatenate([low_up, low_down], axis=1)
-    piece_one = jnp.concatenate([low_in[:, 7 * n :], low_in[:, 3 * n : 4 * n]], axis=1)
-    piece_two = low_back[:, 2 * n :]
-    piece_cross = jnp.concatenate([low_in[:, 4 * n : 7 * n], low_back[:, n : 2 * n]], axis=1)
-    gathered = gather_all([piece_attn, piece_mlp, piece_one, piece_two, piece_cross])
-    w_attn, w_mlp, w_one, w_two, w_cross = [
-        w.reshape(2, features, -1) for w in gathered
-    ]
-    weight_sq = matrix_squares(w_in, w_back, w_up, w_down)
-
     def own_rows(v):
         return lax.dynamic_slice_in_dim(v, x * length, length, 0)
 
     tok = own_rows(tokens)
-    noise = own_rows(noise_field)
     cot = own_rows(cotangent)
     codec = pick(codec_tokens, x, 0)
     step = pick(timesteps, x, 0)
@@ -1301,40 +1553,14 @@
     sem = pltpu.SemaphoreType.DMA
     norms = norm_params
 
-    n1, qkv, mixed, logs, part = run_kernel(
-        attn_forward, "attn_forward",
-        [seg_col, seg_row, tok, norms, w_attn],
-        [(full, LOW), ((2, length, 3 * n), LOW), ((2, length, n), LOW), ((length, heads), F32), (full, LOW)],
-        [VM((2, *square), LOW), sem((2,))], hbm=(4,), flops=4 * 10**9,
-    )
-    resid_one, n2, part_two = run_kernel(
-        mlp_forward, "mlp_forward",
-        [tok, part, swap_core(part), norms, w_mlp],
-        [(full, F32), (full, LOW), (full, LOW)],
-        [VM((2, features, 2 * hid), LOW), VM(full, F32), sem((2,))], hbm=(4,), flops=3 * 10**9,
-    )
+    gathered, weight_sq, kept = forward_all(
+        w_in, w_back, w_up, w_down.T, seg_col, seg_row, norms, side, embed_rows, noise_level,
+        tokens, noise_field, codec_tokens,
+    )
+    w_attn, w_mlp, w_one, w_two, w_cross = [w.reshape(2, features, -1) for w in gathered]
+    n1, qkv, mixed, logs, resid_one, n2, noisy, first, conv, taps = kept[:10]
+    resid_three, n3, cq, ckv, cross, logs_c, out_low = kept[10:]
     tall = length + 2 * TIME
-    noisy, first, conv, taps, part = run_kernel(
-        conv_forward, "conv_forward",
-        [noise_level, resid_one, part_two, swap_core(part_two), noise, norms, side, embed_rows, w_one, w_two],
-        [(full, F32), (full, LOW), ((2, length, n), F32), ((2, tall, 3 * n), LOW), (full, LOW)],
-        [
-            VM((tall, features), LOW), VM((2, features, 10 * n), LOW), VM((2, features, 9 * n), LOW),
-            sem((4,)),
-        ],
-        hbm=(8, 9), flops=7 * 10**9,
-    )
-    resid_three, n3, cq, ckv, cross, logs_c, part = run_kernel(
-        cross_forward, "cross_forward",
-        [noisy, part, swap_core(part), codec, norms, w_cross],
-        [
-            (full, F32), (full, LOW), ((2, length, n), LOW), ((2, codec.shape[0], 2 * n), LOW),
-            ((2, length, n), LOW), ((length, heads), F32), (full, LOW),
-        ],
-        [VM((2, *square), LOW), sem((2,))], hbm=(5,), flops=2 * 10**9,
-    )
-    result = resid_three + (part.astype(F32) + swap_core(part).astype(F32))
-    out_low = result.astype(LOW)
     out_rows = by_parity(x, out_low, swap_x(out_low), 0).reshape(-1, features)
 
     d, part = run_kernel(
@@ -1396,71 +1622,24 @@
     sums = scatter_all(
         [v.reshape(2, 4, 2, -1, v.shape[2]) for v in (d_attn, d_mlp, d_one, d_two, d_cross)]
     )
-    sum_attn, sum_mlp, sum_one, sum_two, sum_cross = sums
     half = length // 2
     mine = lax.dynamic_slice_in_dim(grad_x, core * half, half, 0)
     got = swap_x(mine)
     other_x = by_parity(core, got, swap_core(got), 0).reshape(length, features)
     grad_rows = by_parity(x, grad_x, other_x, 0).reshape(-1, features).astype(F32)
 
-    def unpack_in(v):
-        return v.reshape(v.shape[0], -1, n).transpose(1, 0, 2)
-
-    def unpack_back(v):
-        return v.reshape(v.shape[0], -1, n).transpose(1, 2, 0)
-
-    summed_in = unpack_in(
-        jnp.concatenate(
-            [sum_attn[:, : 3 * n], sum_one[:, 9 * n :], sum_cross[:, : 3 * n], sum_one[:, : 9 * n]],
-            axis=1,
-        )
-    )
-    summed_back = unpack_back(
-        jnp.concatenate([sum_attn[:, 3 * n :], sum_cross[:, 3 * n :], sum_two], axis=1)
-    )
-    summed_up = sum_mlp[:, :hid]
-    summed_down = sum_mlp[:, hid:].T
-
     group_rows = jnp.zeros((2, features), F32)
     for i, s in enumerate(slices):
         group_rows = lax.dynamic_update_slice(group_rows, gn_six[i], (0, s * n))
-    norm_grad = lax.psum(
-        jnp.concatenate(
-            [ln_zero * lead, ln_two * lead, gn_four * lead, group_rows, ln_eight * lead]
-        ),
-        ("dp", "mp"),
-    )
-    return finish(
-        out_rows, grad_rows, weight_sq, (summed_in, summed_back, summed_up, summed_down),
-        (w_in, w_back, w_up, w_down), (m_in, m_back, m_up, m_down), (v_in, v_back, v_up, v_down),
-        norm_grad, norm_params, norm_m, norm_v,
-    )
-
-
-def finish(out_rows, grad_rows, weight_sq, grads, masters, moments, squares, norm_grad, norm_params, norm_m, norm_v):
-    stepped = [
-        adam_update(w, g, m, v, WEIGHT_DECAY)
-        for w, g, m, v in zip(masters, grads, moments, squares)
-    ]
-    new_m = [s[0] for s in stepped]
-    new_v = [s[1] for s in stepped]
-    updates = [s[2] for s in stepped]
-    update_sq = matrix_squares(*updates)
-    weight_total, update_total = lax.psum((weight_sq, update_sq), ("dp", "mp"))
-    weight_len = jnp.sqrt(weight_total)
-    update_len = jnp.sqrt(update_total)
-    trust = LEARN_RATE * (weight_len / update_len)
-    scales = (trust[0:16, None, None], trust[16:27, None, None], trust[27], trust[28])
-    new_w = [w - s * u for w, s, u in zip(masters, scales, updates)]
-    norm_m_new, norm_v_new, upd_norm = adam_update(norm_params, norm_grad, norm_m, norm_v, 0.0)
-    row_trust = jnp.sqrt(jnp.sum(norm_params * norm_params, axis=1)) / jnp.sqrt(
-        jnp.sum(upd_norm * upd_norm, axis=1)
-    )
-    new_norm = norm_params - LEARN_RATE * row_trust[:, None] * upd_norm
-    return (
-        out_rows, grad_rows, *new_w, *new_m, *new_v, new_norm, norm_m_new, norm_v_new,
-        jnp.stack([weight_len, update_len]),
-    )
+    rows = jnp.concatenate(
+        [ln_zero * lead, ln_two * lead, gn_four * lead, group_rows, ln_eight * lead]
+    )
+    stepped = lamb_all(
+        sums, weight_sq, rows, (w_in, w_back, w_up, w_down.T), (m_in, m_back, m_up, m_down.T),
+        (v_in, v_back, v_up, v_down.T), norm_params, norm_m, norm_v,
+    )
+    stepped = [v.T if k in (3, 7, 11) else v for k, v in enumerate(stepped)]
+    return (out_rows, grad_rows, *stepped)
 
 
 def solution(mesh):

time: 718 us -> 565 us (0.79)
  blocking collectives: 46.3 us -> 0 us
  Pallas kernels: 570 us -> 525 us
  other arithmetic: 39 us -> 4.52 us
  local copies, waits for them, and re-layouts: 39.4 us -> 16.4 us
    psum x1 -> x0, blocking collectives: 46.3 us -> none  [finish(): weight_total, update_total = lax.psum((weight_sq, update_sq), ('dp', 'mp'))]
    pallas_call x10 -> x8, Pallas kernels: 153 us -> 116 us  [run_kernel(): pl.pallas_call(body, name=name, in_specs=in_specs, out_specs=[spec_vm() f...]
    reduce_sum x5 -> x0, other arithmetic: 12.6 us -> none  [the longest x1 6.1 us: matrix_squares(): jnp.sum(first_stack * first_stack, axis=(1, 2))]
    slice x13 -> x0, local copies, waits for them, and re-layouts: 11 us -> none  [the longest x1 1.87 us: fast_device(): low_in[:, 7 * n:]]
    sub x5 -> x0, other arithmetic: 9.27 us -> none  [the longest x4 7.75 us: finish(): new_w = [w - s * u for w, s, u in zip(masters, scales, updates)]]
    pallas_call x1 -> x2, Pallas kernels: 211 us -> 206 us  [the longest x1 183 us: forward_all(): pl.pallas_call(forward_body, name='forward', in_specs=[spec_vm() for _ in...]
  transfers between devices with their start and end apart: 11 -> 7, of which waited for: 4 -> 4; matrix products, arithmetic and copies ran while one was open for 6% -> 1% of each run, Pallas kernels for 8% -> 48%
where the time goes in v3:
time: 565 us; the launch traced here: 558 us
  Pallas kernels  525 us (93%)
  local copies, waits for them, and re-layouts  16.4 us (3%)
  waiting for transfers between devices  6.22 us (1%)
    pallas_call x1, Pallas kernels, scatter_all(): pl.pallas_call(partial(scatter_body, count), name='scatter_grads', in_spe...  204 us
    pallas_call x1, Pallas kernels, forward_all(): pl.pallas_call(forward_body, name='forward', in_specs=[spec_vm() for _ in...  183 us
    pallas_call x8, Pallas kernels, run_kernel(): pl.pallas_call(body, name=name, in_specs=in_specs, out_specs=[spec_vm() f...  116 us
    pallas_call x1, Pallas kernels, lamb_all(): pl.pallas_call(totals_body, name='norm_totals', in_specs=[spec_vm() for _...  22.1 us
  transfers between devices with their start and end apart: 7, of which 4 were waited for; matrix products, arithmetic and copies ran while one was open for 1% of the time, Pallas kernels for 48%

profile of v3, /device:TPU:0, one launch (start us, length us, event | category | flops | bytes accessed | tf_op | source)
XLA Modules:
  0.0 557.8 jit_solution(1361662857319404106)
XLA Ops:
  0.7 0.0 copy-start
  0.7 0.8 fusion.2
  1.5 1.3 constant_dynamic-slice_fusion.3.seg_row
  2.8 0.9 copy.48.seg_col
  3.6 1.2 dynamic_slice.30
  5.6 1.8 dynamic-slice_bitcast_fusion.codec
  7.4 0.8 dynamic-slice_bitcast_fusion.2
  8.2 0.6 pad_maximum_fusion.3.side
  8.8 0.0 copy-done
  8.8 0.9 constant_dynamic-slice_fusion.1.cot
  9.8 0.6 broadcast_in_dim.7.embed
  10.4 183.4 %forward.1 = (bf16[2,4,2,96,768]{4,3,2,1,0:T(8,128)(2,1)}, bf16[2,4,2,96,1536]{4,3,2,1,0:T(8,128)(2,1)}, bf16[2,4,2,96,1920]{4,3,2,1,0:T(8,128)(2,1)}, bf16[2,4,...) custom-call(f32[16,96,192]{2,1,0:T(8,128)} %w_in.3, ...), custom_call_target="tpu_custom_call" | custom-call | tf_op jit(solution)/shard_map/forward/pallas_call | solution.py:1246
  193.8 16.3 %cross_backward.1 = (bf16[2,768,768]{2,1,0:T(8,128)(2,1)}, bf16[512,768]{1,0:T(8,128)(2,1)}) custom-call(bf16[512,768]{1,0:T(8,128)(2,1)} %constant_dynamic-slice_fusion.1.cot, bf16[512,768]{1,0:T(8,128)(2,1)} %get-tuple-element.92.n3, bf16[256,768]{1,0:T(8,128)(2,1)} %dynamic-slice_bitcast_fusion.codec, bf16[2,512,192]{2,1,0:T(8,128)(2,1)} %get-tuple-element.93.cq, ...), custom_call_target="tpu_custom_call" | custom-call | flops 4000000000 | bytes 8663040 | tf_op jit(solution)/shard_map/cross_backward/pallas_call | solution.py:495
  210.1 0.1 collective-permute-start.1
  210.2 0.9 copy.49.embed_col
  211.2 1.5 collective-permute-done.1.other
  212.7 0.9 copy-done.10
  213.6 26.0 %conv_two_backward.1 = (f32[512,768]{1,0:T(8,128)}, bf16[2,768,1728]{2,1,0:T(8,128)(2,1)}, bf16[2,640,576]{2,1,0:T(8,128)(2,1)}, f32[2,768]{1,0:T(2,128)}, f32[2,2,192]{2,1,0:T(2,128)}, /*index=5*/f32[2,192]{1,0:T(2,128)}) custom-call(f32[512,768]{1,0:T(8,128)} %get-tuple-element.91.resid, bf16[512,768]{1,0:T(8,128)(2,1)} %get-tuple-element.98.own, ...), custom_call_target="tpu_custom_call" | custom-call | flops 6000000000 | bytes 19901952 | tf_op jit(solution)/shard_map/conv_two_backward/pallas_call | solution.py:495
  239.6 13.3 %conv_one_backward.1 = (bf16[2,768,1920]{2,1,0:T(8,128)(2,1)}, bf16[512,768]{1,0:T(8,128)(2,1)}) custom-call(bf16[512,768]{1,0:T(8,128)(2,1)} %get-tuple-element.90.first, bf16[2,640,576]{2,1,0:T(8,128)(2,1)} %get-tuple-element.102.tapsg, f32[2,192]{1,0:T(2,128)} %get-tuple-element.103.gsum, f32[768,1]{1,0:T(8,128)} %copy.49.embed_col, ...), custom_call_target="tpu_custom_call" | custom-call | flops 6000000000 | bytes 14848512 | tf_op jit(solution)/shard_map/conv_one_backward/pallas_call | solution.py:495
  252.9 0.2 collective-permute-start.2
  253.1 2.4 collective-permute-done.2.other
  255.5 0.9 copy-done.12
  256.4 16.2 %mlp_backward.1 = (f32[512,768]{1,0:T(8,128)}, bf16[2,768,1536]{2,1,0:T(8,128)(2,1)}, bf16[512,768]{1,0:T(8,128)(2,1)}, f32[2,768]{1,0:T(2,128)}) custom-call(f32[512,768]{1,0:T(8,128)} %get-tuple-element.89.noisy, bf16[512,768]{1,0:T(8,128)(2,1)} %get-tuple-element.105.own, bf16[512,768]{1,0:T(8,128)(2,1)} %copy-done.12, ...), custom_call_target="tpu_custom_call" | custom-call | flops 7000000000 | bytes 17338368 | tf_op jit(solution)/shard_map/mlp_backward/pallas_call | solution.py:495
  272.6 0.2 collective-permute-start.3
  272.8 0.0 copy-done.4
  272.8 1.4 collective-permute-start
  274.2 0.9 collective-permute-done.3.other
  275.1 0.9 copy-done.11
  276.0 22.7 %attn_backward.1 = (f32[512,768]{1,0:T(8,128)}, bf16[2,768,768]{2,1,0:T(8,128)(2,1)}, bf16[512,768]{1,0:T(8,128)(2,1)}, f32[2,768]{1,0:T(2,128)}) custom-call(s32[512,1]{1,0:T(8,128)} %copy.48.seg_col, s32[1,512]{1,0:T(1,128)} %constant_dynamic-slice_fusion.3.seg_row, f32[512,768]{1,0:T(8,128)} %get-tuple-element.88.resid, ...), custom_call_target="tpu_custom_call" | custom-call | flops 8000000000 | bytes 14209024 | tf_op jit(solution)/shard_map/attn_backward/pallas_call | solution.py:495
  298.7 0.0 copy-start.7
  298.7 0.2 collective-permute-start.4
  298.9 0.0 copy-done.2
  298.9 0.9 constant_dynamic-slice_fusion.2.tok
  299.9 0.0 copy-done.7
  299.9 0.0 collective-permute-done
  299.9 0.1 select_bitcast_fusion.1
  300.0 1.4 collective-permute-done.4.other
  301.4 4.5 input_backward.1
  305.9 1.0 constant_dynamic-slice_fusion
  307.0 1.5 collective-permute-start.5
  308.4 0.2 dynamic_update_slice.6
  308.6 0.2 dynamic_update_slice.7
  308.8 0.0 copy-start.6
  308.8 1.3 pad_maximum_fusion
  310.1 0.0 copy-done.6
  310.1 204.0 %scatter_grads.1 = (f32[96,768]{1,0:T(8,128)}, f32[96,1536]{1,0:T(8,128)}, f32[96,1920]{1,0:T(8,128)}, f32[96,1728]{1,0:T(8,128)}, f32[96,768]{1,0:T(8,128)}) custom-call(bf16[2,4,2,96,768]{4,3,2,1,0:T(8,128)(2,1)} %bitcast.56, bf16[2,4,2,96,1536]{4,3,2,1,0:T(8,128)(2,1)} %bitcast.49, bf16[2,4,2,96,1920]{4,3,2,1,0:T(8,128)(2,1)} %bitcast.47, ...), custom_call_target="tpu_custom_call" | custom-call | tf_op jit(solution)/shard_map/scatter_grads/pallas_call | solution.py:1372
  514.0 0.0 copy-start.5
  514.1 0.0 copy-start.8
  514.1 11.8 %lamb_moments.1 = (f32[16,96,192]{2,1,0:T(8,128)}, f32[11,192,96]{2,1,0:T(8,128)}, f32[96,768]{1,0:T(8,128)}, f32[96,768]{1,0:T(8,128)}, f32[16,96,192]{2,1,0:T(...) custom-call(f32[96,768]{1,0:T(8,128)} %get-tuple-element.130.refs_0_, ...), custom_call_target="tpu_custom_call" | custom-call | bytes 18063872 | tf_op jit(solution)/shard_map/lamb_moments/pallas_call | solution.py:495
  525.8 0.0 collective-permute-done.5
  525.8 0.1 collective-permute-start.6
  526.0 1.3 concatenate.42.rows
  527.2 22.1 %norm_totals.1.total = f32[16,768]{1,0:T(8,128)} custom-call(f32[10,768]{1,0:T(8,128)} %concatenate.42.rows, f32[1,128]{1,0:T(1,128)} %get-tuple-element.124.sq, f32[1,128]{1,0:T(1,128)} %get-tuple-element.135.usq), custom_call_target="tpu_custom_call" | custom-call | tf_op jit(solution)/shard_map/norm_totals/pallas_call | solution.py:1486
  549.3 4.8 lamb_apply.1
  554.1 0.0 copy-start.3
  554.1 0.0 collective-permute-done.6
  554.1 0.1 select_bitcast_fusion.3
  554.2 0.1 pad_maximum_fusion.2
  554.3 1.0 copy-done.3
  555.3 0.2 bitcast_select_fusion.1
  555.4 0.0 copy-start.1
  555.4 0.1 pad_maximum_fusion.1
  555.6 2.0 bitcast_convert_fusion
  557.6 0.0 copy-done.1
  (20 shorter events, 0.1 us)
Async XLA Ops:
  0.7 8.2 %copy-start = (bf16[1024,768]{1,0:T(8,128)(2,1)S(1)}, bf16[1024,768]{1,0:T(8,128)(2,1)}, u32[]{:S(2)}) copy-start(bf16[1024,768]{1,0:T(8,128)(2,1)} %param.26) | copy-start | bytes 4718596
  210.1 2.6 collective-permute-start.1
  212.7 0.9 copy-start.10
  252.9 2.6 collective-permute-start.2
  255.5 0.9 copy-start.12
  256.3 16.4 %copy-start.4 = (bf16[512,768]{1,0:T(8,128)(2,1)S(1)}, bf16[512,768]{1,0:T(8,128)(2,1)}, u32[]{:S(2)}) copy-start(bf16[512,768]{1,0:T(8,128)(2,1)} %get-tuple-element.87) | copy-start | bytes 2359300
  272.6 2.6 collective-permute-start.3
  272.8 27.1 %collective-permute-start = (bf16[512,768]{1,0:T(8,128)(2,1)S(1)}, bf16[512,768]{1,0:T(8,128)(2,1)S(1)}, u32[]{:S(2)}, u32[]{:S(2)}) collective-permute-start(bf16[512,768]{1,0:T(8,128)(2,1)S(1)} %copy-done.4), channel_id=1, source_target_pairs={{0,2},{1,3},{2,0},{3,1},{4,6},{5,7},{6,4},{7,5},{8,10},{9,11},{10,... | collective-permute-start | bytes 2359304 | tf_op jit(solution)/shard_map/ppermute | solution.py:434
  275.1 0.9 copy-start.11
  276.0 22.9 %copy-start.2 = (bf16[1024,768]{1,0:T(8,128)(2,1)S(1)}, bf16[1024,768]{1,0:T(8,128)(2,1)}, u32[]{:S(2)}) copy-start(bf16[1024,768]{1,0:T(8,128)(2,1)} %tokens.1) | copy-start | bytes 4718596
  298.7 1.2 copy-start.7
  298.7 2.7 collective-permute-start.4
  301.4 7.0 %copy-start.9 = (f32[2,2,192]{2,1,0:T(2,128)S(1)}, f32[2,2,192]{2,1,0:T(2,128)}, u32[]{:S(2)}) copy-start(f32[2,2,192]{2,1,0:T(2,128)} %get-tuple-element.122) | copy-start | bytes 9220
  307.0 218.9 %collective-permute-start.5 = (bf16[256,768]{1,0:T(8,128)(2,1)S(1)}, bf16[256,768]{1,0:T(8,128)(2,1)S(1)}, u32[]{:S(2)}, u32[]{:S(2)}) collective-permute-start(bf16[256,768]{1,0:T(8,128)(2,1)S(1)} %constant_dynamic-slice_fusion), channel_id=1, source_target_pairs={{0,2},{1,3},{2,0},{3,1},{4,6},{5,7},{6,4},{7,5},{8,10},{9,11},{10,... | collective-permute-start | bytes 1179656 | tf_op jit(solution)/shard_map/ppermute | solution.py:434
  308.8 1.3 copy-start.6
  514.0 11.9 %copy-start.5 = (f32[2,768]{1,0:T(2,128)S(1)}, f32[2,768]{1,0:T(2,128)}, u32[]{:S(2)}) copy-start(f32[2,768]{1,0:T(2,128)} %get-tuple-element.120) | copy-start | bytes 18436
  514.1 11.9 %copy-start.8 = (f32[2,768]{1,0:T(2,128)S(1)}, f32[2,768]{1,0:T(2,128)}, u32[]{:S(2)}) copy-start(f32[2,768]{1,0:T(2,128)} %get-tuple-element.119) | copy-start | bytes 18436
  525.8 28.3 %collective-permute-start.6 = (bf16[256,768]{1,0:T(8,128)(2,1)S(1)}, bf16[256,768]{1,0:T(8,128)(2,1)S(1)}, u32[]{:S(2)}, u32[]{:S(2)}) collective-permute-start(bf16[256,768]{1,0:T(8,128)(2,1)S(1)} %collective-permute-done.5), channel_id=1, source_target_pairs={{0,1},{1,0},{2,3},{3,2},{4,5},{5,4},{6,7},{7,6},{8,9},{9,8},{10,11... | collective-permute-start | bytes 1179656 | tf_op jit(solution)/shard_map/ppermute | solution.py:430
  554.1 1.1 copy-start.3
  555.4 2.2 copy-start.1

commit v4 on v3

--- a/solution.py
+++ b/solution.py
@@ -594,246 +594,6 @@
     return [jnp.concatenate(d, axis=1) for d in (dq, dk, dv)]
 
 
-def cross_backward(
-    cot, n3, codec, cq, ckv, mixed, logs, w, d, part, wv, gm, dq, dkv, sems
-):
-    n = mixed.shape[2]
-    copies = start_copies([(w.at[0], wv.at[0]), (w.at[1], wv.at[1])], sems)
-    for i in (1, 0):
-        d[i, :, 3 * n :] = mm_tn(cot[...], mixed[i]).astype(LOW)
-    for i in range(2):
-        copies[i].wait()
-        gm[i] = mm(cot[...], wv[i, :, 3 * n :]).astype(LOW)
-    dkv[...] = jnp.zeros(dkv.shape, F32)
-
-    def heads(r):
-        for i in range(2):
-            per = n // HD
-            rows_logs = [logs[r, per * i + h : per * i + h + 1] for h in range(per)]
-            gq, gk, gv = softmax_heads_back(
-                cq[i, r, :], ckv[i, :, :n], ckv[i, :, n:], gm[i, r, :], rows_logs,
-                per, HD ** (-0.5), None,
-            )
-            dq[i, r, :] = gq.astype(LOW)
-            dkv[i] += jnp.concatenate([gk, gv], axis=1)
-
-    each_rows(heads)
-    total = None
-    for i in (1, 0):
-        low_kv = jnp.concatenate(
-            [dkv[i, :, :n] * (HD ** (-0.5)), dkv[i, :, n:]], axis=1
-        ).astype(LOW)
-        d[i, :, :n] = mm_tn(n3[...], dq[i]).astype(LOW)
-        d[i, :, n : 3 * n] = mm_tn(codec[...], low_kv).astype(LOW)
-        term = mm_nt(dq[i], wv[i, :, :n])
-        total = term if total is None else total + term
-    part[...] = total.astype(LOW)
-
-
-def conv_two_backward(
-    resid, own, other, cot, norms, side, conv, taps, u,
-    grad3, d, tapsg, ln_rows, gn_rows, gsum, pad, gl, uv, sems,
-):
-    n = conv.shape[2]
-    width = resid.shape[1] // GROUPS
-    mats_n = group_mats(n, width)
-    copies = start_copies([(u.at[0], uv.at[0]), (u.at[1], uv.at[1])], sems)
-    pad[0:TIME, :] = jnp.zeros((TIME, pad.shape[1]), LOW)
-    pad[TIME + ROWS :, :] = jnp.zeros((TIME, pad.shape[1]), LOW)
-    ln_rows[...] = jnp.zeros(ln_rows.shape, F32)
-
-    def pull(r):
-        g = own[r, :].astype(F32) + other[r, :].astype(F32)
-        back, gain, shift = ln_back(resid[r, :], norms[8:9, :], g)
-        v = cot[r, :].astype(F32) + back
-        grad3[r, :] = v
-        gl[r, :] = v.astype(LOW)
-        ln_rows[0:1, :] += gain
-        ln_rows[1:2, :] += shift
-
-    each_rows(pull)
-    pad[TIME : TIME + ROWS, :] = gl[...]
-    for i in (1, 0):
-        for a in range(3):
-            d[i, :, 3 * n * a : 3 * n * (a + 1)] = mm_tn(
-                gl[...], taps[i, TIME * a : TIME * a + ROWS, :]
-            ).astype(LOW)
-    for i in range(2):
-        copies[i].wait()
-        q = None
-        for a in range(3):
-            term = mm(
-                pad[TIME * (2 - a) : TIME * (2 - a) + ROWS, :],
-                uv[i, :, 3 * n * a : 3 * n * (a + 1)],
-            )
-            q = term if q is None else q + term
-        grad = from_right(q[:, :n]) + q[:, n : 2 * n] + from_left(q[:, 2 * n :])
-        c1 = conv[i]
-        c1 = c1 - group_average(jnp.sum(c1, axis=0, keepdims=True), mats_n, width)
-        var_n = group_average(jnp.sum(c1 * c1, axis=0, keepdims=True), mats_n, width)
-        scale = lax.rsqrt(var_n + NORM_EPS)
-        hat = c1 * scale
-        gain = side[i, 0:1, :]
-        pre = hat * gain + side[i, 1:2, :]
-        gate = jax.nn.sigmoid(pre)
-        grad = grad * gate * (1.0 + pre * (1.0 - gate))
-        d_gain = jnp.sum(grad * hat, axis=0, keepdims=True)
-        d_shift = jnp.sum(grad, axis=0, keepdims=True)
-        gn_rows[i] = jnp.concatenate([d_gain, d_shift], axis=0)
-        back = scale * (
-            grad * gain
-            - group_average(d_shift * gain, mats_n, width)
-            - hat * group_average(d_gain * gain, mats_n, width)
-        )
-        back = back.astype(LOW).astype(F32)
-        gsum[i : i + 1, :] = jnp.sum(back, axis=0, keepdims=True)
-        tapsg[i, 0:TIME, :] = jnp.zeros((TIME, 3 * n), LOW)
-        tapsg[i, TIME + ROWS :, :] = jnp.zeros((TIME, 3 * n), LOW)
-        tapsg[i, TIME : TIME + ROWS, :] = jnp.concatenate(
-            [from_right(back), back, from_left(back)], axis=1
-        ).astype(LOW)
-
-
-def conv_one_backward(first, tapsg, gsum, embed_col, w, d, part, wv, sems):
-    n = gsum.shape[1]
-    copies = start_copies([(w.at[0], wv.at[0]), (w.at[1], wv.at[1])], sems)
-    for i in (1, 0):
-        for a in range(3):
-            d[i, :, 3 * n * a : 3 * n * (a + 1)] = mm_tn(
-                first[...], tapsg[i, TIME * (2 - a) : TIME * (2 - a) + ROWS, :]
-            ).astype(LOW)
-        d[i, :, 9 * n :] = (embed_col[...] * gsum[i : i + 1, :]).astype(LOW)
-    total = None
-    for i in range(2):
-        copies[i].wait()
-        for a in range(3):
-            term = mm_nt(
-                tapsg[i, TIME * (2 - a) : TIME * (2 - a) + ROWS, :],
-                wv[i, :, 3 * n * a : 3 * n * (a + 1)],
-            )
-            total = term if total is None else total + term
-    part[...] = total.astype(LOW)
-
-
-def mlp_backward(
-    noisy, own, other, grad3, norms, n2, w, grad2, d, part, gn_rows, wv, gl, hb, acc, sems
-):
-    hid = wv.shape[2] // 2
-    width = noisy.shape[1] // GROUPS
-    mats = group_mats(noisy.shape[1], width)
-    copies = start_copies([(w.at[0], wv.at[0]), (w.at[1], wv.at[1])], sems)
-    mean = group_average(jnp.sum(noisy[...], axis=0, keepdims=True), mats, width)
-    centre = noisy[...] - mean
-    var = group_average(jnp.sum(centre * centre, axis=0, keepdims=True), mats, width)
-    scale = lax.rsqrt(var + NORM_EPS)
-    gain, shift = norms[4:5, :], norms[5:6, :]
-    gn_rows[...] = jnp.zeros(gn_rows.shape, F32)
-
-    def through_silu(r):
-        hat = (noisy[r, :] - mean) * scale
-        pre = hat * gain + shift
-        gate = jax.nn.sigmoid(pre)
-        g = own[r, :].astype(F32) + other[r, :].astype(F32)
-        g = g * gate * (1.0 + pre * (1.0 - gate))
-        acc[r, :] = g
-        gn_rows[0:1, :] += jnp.sum(g * hat, axis=0, keepdims=True)
-        gn_rows[1:2, :] += jnp.sum(g, axis=0, keepdims=True)
-
-    each_rows(through_silu)
-    mean_shift = group_average(gn_rows[1:2, :] * gain, mats, width)
-    mean_gain = group_average(gn_rows[0:1, :] * gain, mats, width)
-
-    def pull(r):
-        hat = (noisy[r, :] - mean) * scale
-        v = grad3[r, :] + scale * (acc[r, :] * gain - mean_shift - hat * mean_gain)
-        grad2[r, :] = v
-        gl[r, :] = v.astype(LOW)
-
-    each_rows(pull)
-    block = 256
-    started = False
-    copies[0].wait()
-    copies[1].wait()
-    for i in (1, 0):
-        for b in range(hid // block):
-            up = slice(block * b, block * (b + 1))
-            down = slice(hid + block * b, hid + block * (b + 1))
-            pre = mm(n2[...], wv[i, :, up])
-            t, hidden = gelu_parts(pre)
-            slope = gelu_slope(pre, t)
-            d[i, :, down] = mm_tn(gl[...], hidden.astype(LOW)).astype(LOW)
-            hb[...] = (mm(gl[...], wv[i, :, down]) * slope).astype(LOW)
-            d[i, :, up] = mm_tn(n2[...], hb[...]).astype(LOW)
-            term = mm_nt(hb[...], wv[i, :, up])
-            if started:
-                acc[...] += term
-            else:
-                acc[...] = term
-                started = True
-    part[...] = acc[...].astype(LOW)
-
-
-def attn_backward(
-    seg_col, seg_row, resid, own, other, grad2, norms, n1, qkv, mixed, logs, w,
-    grad1, d, part, ln_rows, wv, gl, gm, dqkv, dkv, sems,
-):
-    n = mixed.shape[2]
-    copies = start_copies([(w.at[0], wv.at[0]), (w.at[1], wv.at[1])], sems)
-    ln_rows[...] = jnp.zeros(ln_rows.shape, F32)
-
-    def pull(r):
-        g = own[r, :].astype(F32) + other[r, :].astype(F32)
-        back, gain, shift = ln_back(resid[r, :], norms[2:3, :], g)
-        v = grad2[r, :] + back
-        grad1[r, :] = v
-        gl[r, :] = v.astype(LOW)
-        ln_rows[0:1, :] += gain
-        ln_rows[1:2, :] += shift
-
-    each_rows(pull)
-    for i in range(2):
-        d[i, :, 3 * n :] = mm_tn(gl[...], mixed[i]).astype(LOW)
-        copies[i].wait()
-        gm[i] = mm(gl[...], wv[i, :, 3 * n :]).astype(LOW)
-    dkv[...] = jnp.zeros(dkv.shape, F32)
-
-    def heads(r):
-        mask = seg_col[r, :] == seg_row[...]
-        for i in range(2):
-            per = n // HD
-            rows_logs = [logs[r, per * i + h : per * i + h + 1] for h in range(per)]
-            gq, gk, gv = softmax_heads_back(
-                qkv[i, r, :n], qkv[i, :, n : 2 * n], qkv[i, :, 2 * n :], gm[i, r, :], rows_logs,
-                per, HD ** (-0.5), mask,
-            )
-            dqkv[i, r, :n] = gq.astype(LOW)
-            dkv[i] += jnp.concatenate([gk, gv], axis=1)
-
-    each_rows(heads)
-    total = None
-    for i in (1, 0):
-        dqkv[i, :, n:] = jnp.concatenate(
-            [dkv[i, :, :n] * (HD ** (-0.5)), dkv[i, :, n:]], axis=1
-        ).astype(LOW)
-        d[i, :, : 3 * n] = mm_tn(n1[...], dqkv[i]).astype(LOW)
-        term = mm_nt(dqkv[i], wv[i, :, : 3 * n])
-        total = term if total is None else total + term
-    part[...] = total.astype(LOW)
-
-
-def input_backward(tok, own, other, grad1, norms, grad_x, ln_rows):
-    ln_rows[...] = jnp.zeros(ln_rows.shape, F32)
-
-    def pull(r):
-        g = own[r, :].astype(F32) + other[r, :].astype(F32)
-        back, gain, shift = ln_back(tok[r, :].astype(F32), norms[0:1, :], g)
-        grad_x[r, :] = (grad1[r, :] + back).astype(LOW)
-        ln_rows[0:1, :] += gain
-        ln_rows[1:2, :] += shift
-
-    each_rows(pull)
-
-
 MESH_IDS = pl.DeviceIdType.MESH
 
 
@@ -879,6 +639,10 @@
             copy.wait_send()
 
 
+def padded_width(w):
+    return -(-w // 128) * 128
+
+
 def pack_piece(g, w_in, w_back, w_up, w_down, piece):
     n = w_in.shape[2]
     if g == 1:
@@ -888,10 +652,13 @@
         return
     ins, backs = GROUPS_OF[g]
     cols = [w_in[j] for j in ins] + [w_back[j].T for j in backs]
+    spare = piece.shape[1] - n * len(cols)
+    if spare:
+        cols.append(jnp.zeros((piece.shape[0], spare), F32))
     for k in range(0, len(cols), 2):
         pair = cols[k : k + 2]
         both = pair[0] if len(pair) == 1 else jnp.concatenate(pair, axis=1)
-        piece[:, n * k : n * (k + len(pair))] = both.astype(LOW)
+        piece[:, n * k : n * k + both.shape[1]] = both.astype(LOW)
 
 
 GROUPS_OF = {
@@ -1231,7 +998,7 @@
     rows, features = w_in.shape[1], norms.shape[1]
     heads = 2 * n // HD
     ctok = codecs.shape[1]
-    widths = [4 * n, 2 * hid, 10 * n, 9 * n, 4 * n]
+    widths = [4 * n, 2 * hid, 10 * n, padded_width(9 * n), 4 * n]
     full = (ROWS, features)
     tall = ROWS + 2 * TIME
     kept = [
@@ -1276,112 +1043,475 @@
     lax.fori_loop(0, target.shape[0] // step, body, 0)
 
 
-def scatter_body(count, *refs):
-    last = count - 1
-    grads, outs, refs = refs[:count], refs[count : 2 * count], refs[2 * count :]
-    bufs, refs = refs[: 5 * last], refs[5 * last :]
-    far_buf, mid_buf, side_buf, send, recv = refs
+class Scatter:
+    def __init__(self, net, d, bufs, free=None):
+        self.net, self.d, self.free = net, d, free
+        self.cx, self.cy, self.lx, self.ly, self.zb = bufs
+        self.x, self.core, self.z, self.y = place()
+        self.to_x, self.to_y, self.to_z = chip_peers()
+
+    def raw(self):
+        if self.free is not None:
+            for k in range(2):
+                pl.semaphore_wait(self.free.at[k], 1)
+        d, y, start = self.d, self.y, self.net.start
+        self.first = (
+            start(d.at[1, 0:2, 1 - y], self.cx, self.to_x),
+            start(d.at[1, 2:4, 1 - y], self.cy, self.to_y),
+            start(d.at[1, 0:2, y], self.lx.at[0:2], self.to_x),
+            start(d.at[0, 2:4, 1 - y], self.ly.at[2:4], self.to_y),
+        )
+
+    def corners(self):
+        d, y, start = self.d, self.y, self.net.start
+        self.first[0].wait_recv()
+        for k in range(2):
+            add_rows(self.cx.at[k], [self.cx.at[k], d.at[0, k, 1 - y]])
+        to_line = start(self.cx, self.ly.at[0:2], self.to_y)
+        self.first[1].wait_recv()
+        for k in range(2):
+            add_rows(self.cy.at[k], [self.cy.at[k], d.at[1, 2 + k, y]])
+        self.second = (to_line, start(self.cy, self.lx.at[2:4], self.to_x))
+
+    def lines(self, credit=None):
+        d, y, z = self.d, self.y, self.z
+        for c in (self.first[2], self.first[3], *self.second):
+            c.wait_recv()
+        for k in range(4):
+            add_rows(d.at[0, k, y], [d.at[0, k, y], self.lx.at[k], self.ly.at[k]])
+        if credit is not None:
+            for c in self.second:
+                c.wait_send()
+            for k, peer in enumerate((self.to_x, self.to_y)):
+                pl.semaphore_signal(credit.at[k], inc=1, device_id=peer, device_id_type=MESH_IDS)
+        if self.free is not None:
+            for k in range(3):
+                pl.semaphore_wait(self.free.at[2 + k], 1)
+        self.ends = [
+            self.net.start(d.at[0, (z + k) % 4, y], self.zb.at[k - 1], self.to_z[k - 1])
+            for k in range(1, 4)
+        ]
+
+    def finish(self, target, credit=None):
+        for c in self.ends:
+            c.wait_recv()
+        add_rows(target, [self.d.at[0, self.z, self.y], *(self.zb.at[k] for k in range(3))])
+        if credit is not None:
+            for k in range(1, 4):
+                pl.semaphore_signal(
+                    credit.at[2 + (4 - k) - 1], inc=1, device_id=self.to_z[k - 1], device_id_type=MESH_IDS
+                )
+
+
+def backward_body(
+    seg_col, seg_row, norms, side, embed_col, tokens, cots, codecs,
+    g0, g1, g2, g3, g4, n1_h, qkv_h, mixed_h, logs_h, resid_h, n2_h, noisy_h, first_h, conv_h, taps_h,
+    resid3_h, n3_h, cq_h, ckv_h, cross_h, logs_c_h, out_h,
+    s0, s1, s2, s3, s4, grad_x, other_x, other_out, rows,
+    d_a, d_t, d_o, d_m, wv, cot, codec, cq, ckv, cross, gm, dq, logs, resid, nrm, grad, pad, taps, tapsg,
+    conv, hb, acc, sent, got, cx_p, cy_p, lx_p, ly_p, zb_p, cx_q, cy_q, lx_q, ly_q, zb_q,
+    far_buf, mid_buf, side_buf, stage, gsum, load_sem, out_sem, send, recv, free_p, free_q,
+):
+    n = cq.shape[2]
+    features = norms.shape[1]
+    width = features // GROUPS
+    heads = n // HD
+    hid = d_m.shape[4] // 2
+    ctok = codec.shape[0]
+    score_scale = HD ** (-0.5)
     x, core, z, y = place()
     to_x, to_y, to_z = chip_peers()
+    sibling = device(x, 1 - core, z, y)
     net = Sender(send, recv)
-    meet([to_x, to_y, *to_z])
-    far = [
-        net.start(grads[last].at[:, (z + k) % 4], far_buf.at[k - 1], to_z[k - 1])
-        for k in range(1, 4)
+    loads = []
+
+    def load(src, dst):
+        copy = pltpu.make_async_copy(src, dst, load_sem.at[len(loads)])
+        copy.start()
+        loads.append(copy)
+        return copy
+
+    def weights(ref, i):
+        w = ref.shape[2]
+        return load(ref.at[i], wv.at[i, :, pl.ds(0, w)])
+
+    own = pl.ds(pl.multiple_of(x * ROWS, ROWS), ROWS)
+    half = pl.ds(pl.multiple_of(core * (ROWS // 2), ROWS // 2), ROWS // 2)
+    ready = [
+        load(cots.at[own, :], cot), load(cross_h, cross), load(g4.at[0], wv.at[0, :, pl.ds(0, 4 * n)]),
+        load(g4.at[1], wv.at[1, :, pl.ds(0, 4 * n)]), load(cq_h, cq), load(ckv_h, ckv),
+        load(logs_c_h, logs), load(n3_h, nrm), load(codecs.at[x], codec),
     ]
-    first, second, ends = {}, {}, {}
-    order = list(range(last))[::-1]
-
-    def send_raw(g):
-        cx, cy, lx, ly = bufs[5 * g : 5 * g + 4]
-        first[g] = (
-            net.start(grads[g].at[1, 0:2, 1 - y], cx, to_x),
-            net.start(grads[g].at[1, 2:4, 1 - y], cy, to_y),
-            net.start(grads[g].at[1, 0:2, y], lx.at[0:2], to_x),
-            net.start(grads[g].at[0, 2:4, 1 - y], ly.at[2:4], to_y),
+    later = [load(resid3_h, resid), load(taps_h, taps), load(conv_h, conv)]
+    meet([to_x, to_y, *to_z, sibling])
+    out_far = net.start(out_h.at[half, :], other_out.at[half, :], to_x)
+    sends = {}
+
+    def exchange(k, total):
+        if k >= 2:
+            sends[k - 2].wait_send()
+        sent[k % 2] = total.astype(LOW)
+        sends[k] = net.start(sent.at[k % 2], got.at[k % 2], sibling)
+
+    def joined(k, r):
+        return sent[k % 2, r, :].astype(F32) + got[k % 2, r, :].astype(F32)
+
+    def put(ref, i, first, value):
+        w = value.shape[1]
+        ref[i, :, :, :, first : first + w] = value.astype(LOW).reshape(4, 2, -1, w)
+
+    rows[...] = jnp.zeros(rows.shape, F32)
+    for c in ready:
+        c.wait()
+    for i in (1, 0):
+        put(d_a, i, 3 * n, mm_tn(cot[...], cross[i]))
+        gm[i] = mm(cot[...], wv[i, :, 3 * n : 4 * n]).astype(LOW)
+    acc_kv = acc.at[0:ctok, :]
+    acc_kv[...] = jnp.zeros((ctok, 4 * n), F32)
+
+    def cross_heads(r):
+        for i in range(2):
+            rows_logs = [logs[r, heads * i + h : heads * i + h + 1] for h in range(heads)]
+            gq, gk, gv = softmax_heads_back(
+                cq[i, r, :], ckv[i, :, :n], ckv[i, :, n:], gm[i, r, :], rows_logs, heads, score_scale, None
+            )
+            dq[i, r, :] = gq.astype(LOW)
+            acc_kv[:, 2 * n * i : 2 * n * (i + 1)] += jnp.concatenate([gk, gv], axis=1)
+
+    each_rows(cross_heads)
+    total = None
+    for i in (1, 0):
+        both = acc_kv[:, 2 * n * i : 2 * n * (i + 1)]
+        low = jnp.concatenate([both[:, :n] * score_scale, both[:, n:]], axis=1).astype(LOW)
+        put(d_a, i, 0, mm_tn(nrm[...], dq[i]))
+        put(d_a, i, n, mm_tn(codec[...], low))
+        term = mm_nt(dq[i], wv[i, :, :n])
+        total = term if total is None else total + term
+    exchange(0, total)
+    far = [net.start(d_a.at[:, (z + k) % 4], far_buf.at[k - 1], to_z[k - 1]) for k in range(1, 4)]
+    two_w = [weights(g3, i) for i in range(2)]
+    first_load = load(first_h, nrm)
+    pad[0:TIME, :] = jnp.zeros((TIME, features), LOW)
+    pad[TIME + ROWS :, :] = jnp.zeros((TIME, features), LOW)
+    low_grad = pad.at[TIME : TIME + ROWS, :]
+    for c in later:
+        c.wait()
+    out_far.wait_recv()
+    out_near = net.start(other_out.at[half, :], other_out.at[half, :], sibling)
+    sends[0].wait_recv()
+
+    def pull_three(r):
+        back, gain, shift = ln_back(resid[r, :], norms[8:9, :], joined(0, r))
+        v = cot[r, :].astype(F32) + back
+        grad[r, :] = v
+        low_grad[r, :] = v.astype(LOW)
+        rows[8:9, :] += gain
+        rows[9:10, :] += shift
+
+    each_rows(pull_three)
+    tok_load = load(tokens.at[own, :], cot)
+    noisy_load = load(noisy_h, resid)
+    two = Scatter(net, d_t, (cx_p, cy_p, lx_p, ly_p, zb_p))
+    for i in (1, 0):
+        for a in range(3):
+            put(d_t, i, 3 * n * a, mm_tn(low_grad[...], taps[i, TIME * a : TIME * a + ROWS, :]))
+    d_t[:, :, :, :, 9 * n :] = jnp.zeros((*d_t.shape[:4], d_t.shape[4] - 9 * n), LOW)
+    two.raw()
+    mats_n = group_mats(n, width)
+    gn_rows = []
+    one_w = []
+    for i in range(2):
+        two_w[i].wait()
+        q = None
+        for a in range(3):
+            term = mm(
+                pad[TIME * (2 - a) : TIME * (2 - a) + ROWS, :], wv[i, :, 3 * n * a : 3 * n * (a + 1)]
+            )
+            q = term if q is None else q + term
+        one_w.append(weights(g2, i))
+        g = from_right(q[:, :n]) + q[:, n : 2 * n] + from_left(q[:, 2 * n :])
+        c1 = conv[i]
+        c1 = c1 - group_average(jnp.sum(c1, axis=0, keepdims=True), mats_n, width)
+        var_n = group_average(jnp.sum(c1 * c1, axis=0, keepdims=True), mats_n, width)
+        scale = lax.rsqrt(var_n + NORM_EPS)
+        hat = c1 * scale
+        gain = side[i, 0:1, :]
+        pre = hat * gain + side[i, 1:2, :]
+        gate = jax.nn.sigmoid(pre)
+        g = g * gate * (1.0 + pre * (1.0 - gate))
+        d_gain = jnp.sum(g * hat, axis=0, keepdims=True)
+        d_shift = jnp.sum(g, axis=0, keepdims=True)
+        gn_rows.append(jnp.concatenate([d_gain, d_shift], axis=0))
+        back = scale * (
+            g * gain
+            - group_average(d_shift * gain, mats_n, width)
+            - hat * group_average(d_gain * gain, mats_n, width)
         )
-
-    def fold_corners(g):
-        cx, cy, lx, ly = bufs[5 * g : 5 * g + 4]
-        first[g][0].wait_recv()
-        for k in range(2):
-            add_rows(cx.at[k], [cx.at[k], grads[g].at[0, k, 1 - y]])
-        to_line = net.start(cx, ly.at[0:2], to_y)
-        first[g][1].wait_recv()
-        for k in range(2):
-            add_rows(cy.at[k], [cy.at[k], grads[g].at[1, 2 + k, y]])
-        second[g] = (to_line, net.start(cy, lx.at[2:4], to_x))
-
-    def fold_lines(g):
-        lx, ly, zb = bufs[5 * g + 2 : 5 * g + 5]
-        for c in (first[g][2], first[g][3], *second[g]):
-            c.wait_recv()
-        for k in range(4):
-            add_rows(lx.at[k], [lx.at[k], ly.at[k], grads[g].at[0, k, y]])
-        ends[g] = [
-            net.start(lx.at[(z + k) % 4], zb.at[k - 1], to_z[k - 1]) for k in range(1, 4)
-        ]
-
-    def finish_group(g):
-        lx, zb = bufs[5 * g + 2], bufs[5 * g + 4]
-        for c in ends[g]:
-            c.wait_recv()
-        add_rows(outs[g], [lx.at[z], zb.at[0], zb.at[1], zb.at[2]])
-
-    send_raw(order[0])
+        back = back.astype(LOW).astype(F32)
+        gsum[i : i + 1, :] = jnp.sum(back, axis=0, keepdims=True)
+        tapsg[i, 0:TIME, :] = jnp.zeros((TIME, 3 * n), LOW)
+        tapsg[i, TIME + ROWS :, :] = jnp.zeros((TIME, 3 * n), LOW)
+        tapsg[i, TIME : TIME + ROWS, :] = jnp.concatenate(
+            [from_right(back), back, from_left(back)], axis=1
+        ).astype(LOW)
+    blocks = []
+    for s in range(4):
+        block = jnp.zeros((2, n), F32)
+        for i in range(2):
+            here = (2 * jnp.bitwise_xor(x, i) + core) == s
+            block = block + jnp.where(here, gn_rows[i], 0.0)
+        blocks.append(block)
+    rows[6:8, :] = jnp.concatenate(blocks, axis=1)
+
+    one = Scatter(net, d_o, (cx_q, cy_q, lx_q, ly_q, zb_q))
+    first_load.wait()
+    for i in (1, 0):
+        for a in range(3):
+            put(
+                d_o, i, 3 * n * a,
+                mm_tn(nrm[...], tapsg[i, TIME * (2 - a) : TIME * (2 - a) + ROWS, :]),
+            )
+        put(d_o, i, 9 * n, embed_col[...] * gsum[i : i + 1, :])
+    one.raw()
+    n2_load = load(n2_h, nrm)
+    total = None
+    mlp_w = []
+    for i in range(2):
+        one_w[i].wait()
+        for a in range(3):
+            term = mm_nt(
+                tapsg[i, TIME * (2 - a) : TIME * (2 - a) + ROWS, :], wv[i, :, 3 * n * a : 3 * n * (a + 1)]
+            )
+            total = term if total is None else total + term
+    exchange(1, total)
+    mlp_w = [weights(g1, i) for i in range(2)]
+
+    noisy_load.wait()
+    mats = group_mats(features, width)
+    mean = group_average(jnp.sum(resid[...], axis=0, keepdims=True), mats, width)
+    centre = resid[...] - mean
+    var = group_average(jnp.sum(centre * centre, axis=0, keepdims=True), mats, width)
+    scale = lax.rsqrt(var + NORM_EPS)
+    gain, shift = norms[4:5, :], norms[5:6, :]
+    sends[1].wait_recv()
+
+    def through_silu(r):
+        hat = (resid[r, :] - mean) * scale
+        pre = hat * gain + shift
+        gate = jax.nn.sigmoid(pre)
+        g = joined(1, r)
+        g = g * gate * (1.0 + pre * (1.0 - gate))
+        acc[r, :] = g
+        rows[4:5, :] += jnp.sum(g * hat, axis=0, keepdims=True)
+        rows[5:6, :] += jnp.sum(g, axis=0, keepdims=True)
+
+    each_rows(through_silu)
+    mean_shift = group_average(rows[5:6, :] * gain, mats, width)
+    mean_gain = group_average(rows[4:5, :] * gain, mats, width)
+
+    def pull_two(r):
+        hat = (resid[r, :] - mean) * scale
+        v = grad[r, :] + scale * (acc[r, :] * gain - mean_shift - hat * mean_gain)
+        grad[r, :] = v
+        low_grad[r, :] = v.astype(LOW)
+
+    each_rows(pull_two)
+    resid_load = load(resid_h, resid)
+    two.corners()
+    n2_load.wait()
+    block = 256
+    started = False
+    for i in (1, 0):
+        mlp_w[i].wait()
+        for b in range(hid // block):
+            up, down = block * b, hid + block * b
+            pre = mm(nrm[...], wv[i, :, up : up + block])
+            t, hidden = gelu_parts(pre)
+            slope = gelu_slope(pre, t)
+            put(d_m, i, down, mm_tn(low_grad[...], hidden.astype(LOW)))
+            hb[...] = (mm(low_grad[...], wv[i, :, down : down + block]) * slope).astype(LOW)
+            put(d_m, i, up, mm_tn(nrm[...], hb[...]))
+            term = mm_nt(hb[...], wv[i, :, up : up + block])
+            if started:
+                acc[...] += term
+            else:
+                acc[...] = term
+                started = True
+    exchange(2, acc[...])
+    attn_w = [weights(g0, i) for i in range(2)]
+    tail_loads = [
+        load(n1_h, nrm), load(qkv_h, tapsg.at[:, pl.ds(0, ROWS), :]), load(mixed_h, cross), load(logs_h, logs),
+    ]
     for c in far:
         c.wait_recv()
     for i in range(2):
         for j in range(2):
-            add_rows(
-                mid_buf.at[i, j], [grads[last].at[i, z, j], *(far_buf.at[k, i, j] for k in range(3))]
+            add_rows(mid_buf.at[i, j], [d_a.at[i, z, j], *(far_buf.at[k, i, j] for k in range(3))])
+    halves = net.start(mid_buf.at[:, 1 - y], side_buf.at[0:2], to_y)
+    resid_load.wait()
+    sends[2].wait_recv()
+
+    def pull_one(r):
+        back, g_gain, g_shift = ln_back(resid[r, :], norms[2:3, :], joined(2, r))
+        v = grad[r, :] + back
+        grad[r, :] = v
+        low_grad[r, :] = v.astype(LOW)
+        rows[2:3, :] += g_gain
+        rows[3:4, :] += g_shift
+
+    each_rows(pull_one)
+    two.lines(free_p)
+    mlp = Scatter(
+        net, d_m, (cx_p.at[:, :, pl.ds(0, 2 * hid)], cy_p.at[:, :, pl.ds(0, 2 * hid)],
+                   lx_p.at[:, :, pl.ds(0, 2 * hid)], ly_p.at[:, :, pl.ds(0, 2 * hid)],
+                   zb_p.at[:, :, pl.ds(0, 2 * hid)]), free_p,
+    )
+    mlp.raw()
+    for c in (*attn_w, *tail_loads):
+        c.wait()
+    for i in range(2):
+        gm[i] = mm(low_grad[...], wv[i, :, 3 * n : 4 * n]).astype(LOW)
+    acc[...] = jnp.zeros(acc.shape, F32)
+
+    def self_heads(r):
+        mask = seg_col[r, :] == seg_row[...]
+        for i in range(2):
+            rows_logs = [logs[r, heads * i + h : heads * i + h + 1] for h in range(heads)]
+            gq, gk, gv = softmax_heads_back(
+                tapsg[i, r, :n], tapsg[i, 0:ROWS, n : 2 * n], tapsg[i, 0:ROWS, 2 * n :], gm[i, r, :],
+                rows_logs, heads, score_scale, mask,
             )
-    half = net.start(mid_buf.at[:, 1 - y], side_buf.at[0:2], to_y)
-    for pos, g in enumerate(order):
-        fold_corners(g)
-        if pos + 1 < last:
-            send_raw(order[pos + 1])
-        if pos == 0:
-            half.wait_recv()
-            for i in (1, 0):
-                add_rows(mid_buf.at[i, y], [mid_buf.at[i, y], side_buf.at[i]])
-            tail = net.start(mid_buf.at[1, y], side_buf.at[2], to_x)
-        fold_lines(g)
-        if pos >= 1:
-            finish_group(order[pos - 1])
-    tail.wait_recv()
-    add_rows(outs[last], [mid_buf.at[0, y], side_buf.at[2]])
-    finish_group(order[-1])
-    for c in [*far, half, tail]:
+            taps[i, r, :n] = gq.astype(LOW)
+            acc[:, 2 * n * i : 2 * n * (i + 1)] += jnp.concatenate([gk, gv], axis=1)
+
+    each_rows(self_heads)
+    one.corners()
+    for c in far:
         c.wait_send()
-    for g in range(last):
-        for c in [*first[g], *second[g], *ends[g]]:
-            c.wait_send()
-
-
-def scatter_all(grads):
-    count = len(grads)
-    rows = grads[0].shape[3]
-    widths = [g.shape[4] for g in grads]
-    copies = (count - 1) * 9 + 5
-    scratch = []
-    for w in widths[:-1]:
-        scratch += [VM((k, rows, w), LOW) for k in (2, 2, 4, 4, 3)]
-    w = widths[-1]
-    scratch += [VM((3, 2, 2, rows, w), LOW), VM((2, 2, rows, w), LOW), VM((3, rows, w), LOW)]
-    return pl.pallas_call(
-        partial(scatter_body, count),
-        name="scatter_grads",
-        in_specs=[spec_vm() for _ in grads],
-        out_specs=[spec_vm() for _ in grads],
-        out_shape=[jax.ShapeDtypeStruct((rows, w), F32) for w in widths],
+    attn = Scatter(
+        net, d_a, (cx_q.at[:, :, pl.ds(0, 4 * n)], cy_q.at[:, :, pl.ds(0, 4 * n)],
+                   lx_q.at[:, :, pl.ds(0, 4 * n)], ly_q.at[:, :, pl.ds(0, 4 * n)],
+                   zb_q.at[:, :, pl.ds(0, 4 * n)]), free_q,
+    )
+    total = None
+    for i in (1, 0):
+        both = acc[:, 2 * n * i : 2 * n * (i + 1)]
+        taps[i, 0:ROWS, n:] = jnp.concatenate([both[:, :n] * score_scale, both[:, n:]], axis=1).astype(LOW)
+        put(d_a, i, 3 * n, mm_tn(low_grad[...], cross[i]))
+        put(d_a, i, 0, mm_tn(nrm[...], taps[i, 0:ROWS, :]))
+        term = mm_nt(taps[i, 0:ROWS, :], wv[i, :, : 3 * n])
+        total = term if total is None else total + term
+    exchange(3, total)
+    halves.wait_recv()
+    for i in (1, 0):
+        add_rows(mid_buf.at[i, y], [mid_buf.at[i, y], side_buf.at[i]])
+    last = net.start(mid_buf.at[1, y], side_buf.at[2], to_x)
+    tok_load.wait()
+    sends[3].wait_recv()
+
+    def pull_zero(r):
+        back, g_gain, g_shift = ln_back(cot[r, :].astype(F32), norms[0:1, :], joined(3, r))
+        low_grad[r, :] = (grad[r, :] + back).astype(LOW)
+        rows[0:1, :] += g_gain
+        rows[1:2, :] += g_shift
+
+    each_rows(pull_zero)
+    store_x = pltpu.make_async_copy(low_grad, grad_x, out_sem.at[5])
+    store_x.start()
+    middle = pl.ds(pl.multiple_of(TIME + core * (ROWS // 2), TIME), ROWS // 2)
+    x_far = net.start(pad.at[middle, :], other_x.at[half, :], to_x)
+    rows[0:6, :] = jnp.where(core == 0, rows[0:6, :], 0.0)
+    rows[8:10, :] = jnp.where(core == 0, rows[8:10, :], 0.0)
+
+    def deliver(group, k, out, credit=None):
+        w = out.shape[1]
+        part = stage.at[:, pl.ds(0, w)]
+        group.finish(part, credit)
+        copy = pltpu.make_async_copy(part, out, out_sem.at[k])
+        copy.start()
+        return copy
+
+    out_two = deliver(two, 0, s3, free_p)
+    one.lines(free_q)
+    attn.raw()
+    x_far.wait_recv()
+    x_near = net.start(other_x.at[half, :], other_x.at[half, :], sibling)
+    mlp.corners()
+    last.wait_recv()
+    out_two.wait()
+    part = stage.at[:, pl.ds(0, 4 * n)]
+    add_rows(part, [mid_buf.at[0, y], side_buf.at[2]])
+    out_cross = pltpu.make_async_copy(part, s4, out_sem.at[1])
+    out_cross.start()
+    out_cross.wait()
+    out_one = deliver(one, 2, s2, free_q)
+    mlp.lines()
+    attn.corners()
+    attn.lines()
+    out_one.wait()
+    out_mlp = deliver(mlp, 3, s1)
+    out_mlp.wait()
+    out_attn = deliver(attn, 4, s0)
+    out_attn.wait()
+    out_near.wait_recv()
+    x_near.wait_recv()
+    store_x.wait()
+    wait_sends(net, [*far, sends[0], sends[1], *two.second, *one.second])
+
+
+def wait_sends(net, done):
+    for copy in net.made:
+        if all(copy is not d for d in done):
+            copy.wait_send()
+
+
+def backward_all(seg_col, seg_row, norms, side, embed_col, tokens, cots, codecs, gathered, kept):
+    features = norms.shape[1]
+    n = side.shape[2]
+    rows = gathered[0].shape[3]
+    widths = [g.shape[4] for g in gathered]
+    hid = widths[1] // 2
+    heads = 2 * n // HD
+    ctok = codecs.shape[1]
+    full = (ROWS, features)
+    tall = ROWS + 2 * TIME
+    ins = [
+        seg_col, seg_row, norms, side, embed_col, tokens, cots, codecs,
+        *[g.reshape(2, features, -1) for g in gathered], *kept,
+    ]
+    dma = pltpu.SemaphoreType.DMA
+    regular = pltpu.SemaphoreType.REGULAR
+
+    def receive(w):
+        return [VM((k, rows, w), LOW) for k in (2, 2, 4, 4, 3)]
+
+    copies = 2 + 4 + 2 + 3 + 1 + 1 + 4 * 9
+    res = pl.pallas_call(
+        backward_body,
+        name="backward",
+        in_specs=[spec_vm() for _ in range(5)] + [spec_any() for _ in ins[5:]],
+        out_specs=[spec_any() for _ in range(8)] + [spec_vm()],
+        out_shape=[jax.ShapeDtypeStruct((rows, w), F32) for w in widths]
+        + [jax.ShapeDtypeStruct(full, LOW)] * 3
+        + [jax.ShapeDtypeStruct((10, features), F32)],
         scratch_shapes=[
-            *scratch, pltpu.SemaphoreType.DMA((copies,)), pltpu.SemaphoreType.DMA((copies,)),
+            VM((2, 4, 2, rows, 4 * n), LOW), VM((2, 4, 2, rows, widths[3]), LOW),
+            VM((2, 4, 2, rows, 10 * n), LOW), VM((2, 4, 2, rows, 2 * hid), LOW),
+            VM((2, features, 10 * n), LOW), VM(full, LOW), VM((ctok, features), LOW),
+            VM((2, ROWS, n), LOW), VM((2, ctok, 2 * n), LOW), VM((2, ROWS, n), LOW), VM((2, ROWS, n), LOW),
+            VM((2, ROWS, n), LOW), VM((ROWS, heads), F32), VM(full, F32), VM(full, LOW), VM(full, F32),
+            VM((tall, features), LOW), VM((2, tall, 3 * n), LOW), VM((2, tall, 3 * n), LOW),
+            VM((2, ROWS, n), F32), VM((ROWS, 256), LOW), VM(full, F32), VM((2, *full), LOW), VM((2, *full), LOW),
+            *receive(widths[3]), *receive(10 * n),
+            VM((3, 2, 2, rows, 4 * n), LOW), VM((2, 2, rows, 4 * n), LOW), VM((3, rows, 4 * n), LOW),
+            VM((rows, 10 * n), F32), VM((2, n), F32),
+            dma((30,)), dma((6,)), dma((copies,)), dma((copies,)), regular((5,)), regular((5,)),
         ],
         compiler_params=pltpu.CompilerParams(
-            collective_id=1, has_side_effects=True, vmem_limit_bytes=60 << 20
+            collective_id=1, has_side_effects=True, vmem_limit_bytes=64 << 20
         ),
-    )(*grads)
+    )(*ins)
+    return res[:5], res[5], res[6], res[7], res[8]
 
 
 def adam_rows(w, g, m, v, decay_rate):
@@ -1522,22 +1652,13 @@
     norm_m,
     norm_v,
 ):
-    length = segments.shape[1]
     features = tokens.shape[1]
     n = w_in.shape[2]
-    hid = w_up.shape[1]
     mp = lax.axis_index("mp")
     dp = lax.axis_index("dp")
     x, core, z, y = mp // 2, mp % 2, dp // 2, dp % 2
-    lead = (core == 0).astype(F32)
     slices = [2 * x + core, 2 * (1 - x) + core]
 
-    def own_rows(v):
-        return lax.dynamic_slice_in_dim(v, x * length, length, 0)
-
-    tok = own_rows(tokens)
-    cot = own_rows(cotangent)
-    codec = pick(codec_tokens, x, 0)
     step = pick(timesteps, x, 0)
     seg = pick(segments, x, 0)
     seg_col, seg_row = seg[:, None], seg[None, :]
@@ -1548,92 +1669,17 @@
     side = jnp.stack(
         [lax.dynamic_slice(norm_params, (6, s * n), (2, n)) for s in slices]
     )
-    full = (length, features)
-    square = (features, 4 * n)
-    sem = pltpu.SemaphoreType.DMA
     norms = norm_params
 
     gathered, weight_sq, kept = forward_all(
         w_in, w_back, w_up, w_down.T, seg_col, seg_row, norms, side, embed_rows, noise_level,
         tokens, noise_field, codec_tokens,
     )
-    w_attn, w_mlp, w_one, w_two, w_cross = [w.reshape(2, features, -1) for w in gathered]
-    n1, qkv, mixed, logs, resid_one, n2, noisy, first, conv, taps = kept[:10]
-    resid_three, n3, cq, ckv, cross, logs_c, out_low = kept[10:]
-    tall = length + 2 * TIME
-    out_rows = by_parity(x, out_low, swap_x(out_low), 0).reshape(-1, features)
-
-    d, part = run_kernel(
-        cross_backward, "cross_backward",
-        [cot, n3, codec, cq, ckv, cross, logs_c, w_cross],
-        [((2, *square), LOW), (full, LOW)],
-        [
-            VM((2, *square), LOW), VM((2, length, n), LOW), VM((2, length, n), LOW),
-            VM((2, codec.shape[0], 2 * n), F32), sem((2,)),
-        ],
-        hbm=(7,), flops=4 * 10**9,
-    )
-    d_cross = d
-    wide = (features, 9 * n)
-    grad_three, d, tapsg, ln_eight, gn_six, gsum = run_kernel(
-        conv_two_backward, "conv_two_backward",
-        [resid_three, part, swap_core(part), cot, norms, side, conv, taps, w_two],
-        [
-            (full, F32), ((2, *wide), LOW), ((2, tall, 3 * n), LOW), ((2, features), F32),
-            ((2, 2, n), F32), ((2, n), F32),
-        ],
-        [VM((tall, features), LOW), VM(full, LOW), VM((2, *wide), LOW), sem((2,))],
-        hbm=(8,), flops=6 * 10**9,
-    )
-    d_two = d
-    wider = (features, 10 * n)
-    d, part = run_kernel(
-        conv_one_backward, "conv_one_backward",
-        [first, tapsg, gsum, embed_col, w_one],
-        [((2, *wider), LOW), (full, LOW)],
-        [VM((2, *wider), LOW), sem((2,))], hbm=(4,), flops=6 * 10**9,
-    )
-    d_one = d
-    double = (features, 2 * hid)
-    grad_two, d, part, gn_four = run_kernel(
-        mlp_backward, "mlp_backward",
-        [noisy, part, swap_core(part), grad_three, norms, n2, w_mlp],
-        [(full, F32), ((2, *double), LOW), (full, LOW), ((2, features), F32)],
-        [VM((2, *double), LOW), VM(full, LOW), VM((length, 256), LOW), VM(full, F32), sem((2,))],
-        hbm=(6,), flops=7 * 10**9,
-    )
-    d_mlp = d
-    grad_one, d, part, ln_two = run_kernel(
-        attn_backward, "attn_backward",
-        [seg_col, seg_row, resid_one, part, swap_core(part), grad_two, norms, n1, qkv, mixed, logs, w_attn],
-        [(full, F32), ((2, *square), LOW), (full, LOW), ((2, features), F32)],
-        [
-            VM((2, *square), LOW), VM(full, LOW), VM((2, length, n), LOW), VM((2, length, 3 * n), LOW),
-            VM((2, length, 2 * n), F32), sem((2,)),
-        ],
-        hbm=(11,), flops=8 * 10**9,
-    )
-    d_attn = d
-    grad_x, ln_zero = run_kernel(
-        input_backward, "input_backward",
-        [tok, part, swap_core(part), grad_one, norms],
-        [(full, LOW), ((2, features), F32)], [],
-    )
-    sums = scatter_all(
-        [v.reshape(2, 4, 2, -1, v.shape[2]) for v in (d_attn, d_mlp, d_one, d_two, d_cross)]
-    )
-    half = length // 2
-    mine = lax.dynamic_slice_in_dim(grad_x, core * half, half, 0)
-    got = swap_x(mine)
-    other_x = by_parity(core, got, swap_core(got), 0).reshape(length, features)
-    grad_rows = by_parity(x, grad_x, other_x, 0).reshape(-1, features).astype(F32)
-
-    group_rows = jnp.zeros((2, features), F32)
-    for i, s in enumerate(slices):
-        group_rows = lax.dynamic_update_slice(group_rows, gn_six[i], (0, s * n))
-    rows = jnp.concatenate(
-        [ln_zero * lead, ln_two * lead, gn_four * lead, group_rows, ln_eight * lead]
-    )
+    sums, own_x, other_x, other_out, rows = backward_all(
+        seg_col, seg_row, norms, side, embed_col, tokens, cotangent, codec_tokens, gathered, kept
+    )
+    out_rows = by_parity(x, kept[-1], other_out, 0).reshape(-1, features)
+    grad_rows = by_parity(x, own_x, other_x, 0).reshape(-1, features).astype(F32)
     stepped = lamb_all(
         sums, weight_sq, rows, (w_in, w_back, w_up, w_down.T), (m_in, m_back, m_up, m_down.T),
         (v_in, v_back, v_up, v_down.T), norm_params, norm_m, norm_v,

time: 565 us -> 470 us (0.83)
  Pallas kernels: 525 us -> 449 us
  local copies, waits for them, and re-layouts: 16.4 us -> 6.64 us
  waiting for transfers between devices: 6.22 us -> 0 us
    pallas_call x8 -> x2, Pallas kernels: 116 us -> 16.5 us  [run_kernel(): pl.pallas_call(body, name=name, in_specs=in_specs, out_specs=[spec_vm() f...]
    pallas_call x1, Pallas kernels: 204 us -> 228 us  [backward_all(): pl.pallas_call(backward_body, name='backward', in_specs=[spec_vm() for _...]
    ppermute x7 -> x0, waiting for transfers between devices: 6.22 us -> none  [the longest x5 6.22 us: swap_core(): return lax.ppermute(v, 'mp', CORE_SWAP)]
  transfers between devices with their start and end apart: 7 -> 0, of which waited for: 4 -> 0; matrix products, arithmetic and copies ran while one was open for 1% -> 0% of each run, Pallas kernels for 48% -> 0%
where the time goes in v4:
time: 470 us; the launch traced here: 463 us
  Pallas kernels  449 us (96%)
  local copies, waits for them, and re-layouts  6.64 us (1%)
  other arithmetic  5.8 us (1%)
    pallas_call x1, Pallas kernels, backward_all(): pl.pallas_call(backward_body, name='backward', in_specs=[spec_vm() for _...  228 us
    pallas_call x1, Pallas kernels, forward_all(): pl.pallas_call(forward_body, name='forward', in_specs=[spec_vm() for _ in...  184 us
    pallas_call x1, Pallas kernels, lamb_all(): pl.pallas_call(totals_body, name='norm_totals', in_specs=[spec_vm() for _...  20.3 us
    pallas_call x2, Pallas kernels, run_kernel(): pl.pallas_call(body, name=name, in_specs=in_specs, out_specs=[spec_vm() f...  16.5 us

profile of v4, /device:TPU:0, one launch (start us, length us, event | category | flops | bytes accessed | tf_op | source)
XLA Modules:
  0.0 462.7 jit_solution(15004799692376930989)
XLA Ops:
  0.7 1.2 dynamic_slice.17
  2.6 1.3 constant_dynamic-slice_fusion.seg_row
  3.9 0.7 fusion.2
  4.6 0.8 dynamic-slice_bitcast_fusion.1
  5.4 0.6 pad_maximum_fusion.2.side
  6.1 0.6 broadcast_in_dim.5.embed
  6.7 0.9 copy.48.seg_col
  7.6 0.9 copy.50.embed_col
  8.5 183.5 %forward.1 = (bf16[2,4,2,96,768]{4,3,2,1,0:T(8,128)(2,1)}, bf16[2,4,2,96,1536]{4,3,2,1,0:T(8,128)(2,1)}, bf16[2,4,2,96,1920]{4,3,2,1,0:T(8,128)(2,1)}, bf16[2,4,...) custom-call(f32[16,96,192]{2,1,0:T(8,128)} %w_in.3, ...), custom_call_target="tpu_custom_call" | custom-call | tf_op jit(solution)/shard_map/forward/pallas_call | solution.py:1013
  192.0 228.2 %backward.1 = (f32[96,768]{1,0:T(8,128)}, f32[96,1536]{1,0:T(8,128)}, f32[96,1920]{1,0:T(8,128)}, f32[96,1792]{1,0:T(8,128)}, f32[96,768]{1,0:T(8,128)}, /*index...) custom-call(s32[512,1]{1,0:T(8,128)} %copy.48.seg_col, ...), custom_call_target="tpu_custom_call" | custom-call | tf_op jit(solution)/shard_map/backward/pallas_call | solution.py:1489
  420.2 0.0 copy-start
  420.3 0.0 copy-start.1
  420.3 1.6 select_bitcast_fusion.3
  421.9 0.0 copy-done
  421.9 0.2 copy-done.1
  422.1 0.1 select_bitcast_fusion.1
  422.2 0.1 pad_maximum_fusion.1
  422.4 1.3 pad_maximum_fusion
  423.6 2.0 bitcast_convert_fusion
  425.6 11.7 %lamb_moments.1 = (f32[16,96,192]{2,1,0:T(8,128)}, f32[11,192,96]{2,1,0:T(8,128)}, f32[96,768]{1,0:T(8,128)}, f32[96,768]{1,0:T(8,128)}, f32[16,96,192]{2,1,0:T(...) custom-call(f32[96,768]{1,0:T(8,128)} %get-tuple-element.98.refs_0_,, ...), custom_call_target="tpu_custom_call" | custom-call | bytes 18088448 | tf_op jit(solution)/shard_map/lamb_moments/pallas_call | solution.py:495
  437.3 20.3 %norm_totals.1.total = f32[16,768]{1,0:T(8,128)} custom-call(f32[10,768]{1,0:T(8,128)} %get-tuple-element.96.rows, f32[1,128]{1,0:T(1,128)} %get-tuple-element.97.sq, f32[1,128]{1,0:T(1,128)} %get-tuple-element.103.usq), custom_call_target="tpu_custom_call" | custom-call | tf_op jit(solution)/shard_map/norm_totals/pallas_call | solution.py:1616
  457.6 4.8 %lamb_apply.1 = (f32[16,96,192]{2,1,0:T(8,128)}, f32[11,192,96]{2,1,0:T(8,128)}, f32[96,768]{1,0:T(8,128)}, f32[96,768]{1,0:T(8,128)}, f32[10,768]{1,0:T(8,128)}...) custom-call(f32[16,768]{1,0:T(8,128)} %norm_totals.1.total, f32[16,96,192]{2,1,0:T(8,128)} %w_in.3, ...), custom_call_target="tpu_custom_call" | custom-call | bytes 7975144 | tf_op jit(solution)/shard_map/lamb_apply/pallas_call | solution.py:495
  (5 shorter events, 0.1 us)
Async XLA Ops:
  420.2 1.6 copy-start
  420.3 1.8 copy-start.1
